TPU v7x, 32 devices: a whole 2x2x4 slice. The times are simulated.
32 devices in a mesh: plant: 8 (over z, core), col: 4 (over y, x).
Axes of the slice: x: 2, y: 2, z: 4, core: 2. Of those that a mesh axis runs over, the one named last changes fastest.
Arguments:
- tiles: bfloat16 [8, 4, 48, 256, 256], P('plant', 'col'), may hold values from -0.109375 to 0.109375
- tile_row: int32 [8, 4, 48], P('plant', 'col'), may hold values from 0 to 15
- tile_col: int32 [8, 4, 48], P('plant', 'col'), may hold values from 0 to 63
- row_count: int32 [8], P('plant'), may hold values from 2048 to 4096, as said below
- x_start: float32 [32, 65536], P(None, 'col'), may hold values from 0 to 1
- y_start: float32 [32, 32768], P(None, 'plant'), may hold values from 0 to 1
- cost: float32 [65536], P('col'), may hold values from -3 to 3
- upper: float32 [65536], P('col'), may hold values from 0.5 to 2
- demand: float32 [32, 32768], P(None, 'plant'), may hold values from -6 to 6
- tau: float32 [32], replicated, may hold values from 0.2 to 1
- sigma: float32 [32], replicated, may hold values from 0.2 to 1
Outputs:
- primal: float32 [32, 65536], P(None, 'col')
- dual: float32 [32, 32768], P(None, 'plant')
Inputs may be any that keep to these rules, and one draw needn't show every extreme that they name: Each plant block has row_count live rows, the first ones of its block; at least one plant block is full. `tile_row`: tiles at the same position add up.
All inputs are finite; a program needn't handle non-finite values.
Results may differ from a plain program's by a relative error of at most 0.003.
Values sent between devices are 32-bit elements; how exact they have to be, the bound alone decides.
No kernel may reach another device: no remote copies, remote signals or barrier semaphores. Data moves between devices by JAX's collectives and lax.ppermute only.
A program may use at most 64 MiB of HBM per device.

v0:
```python
import jax
import jax.numpy as jnp
from jax import lax
from jax.sharding import PartitionSpec as P

ITERS = 3


def body(tiles, tile_row, tile_col, row_count, x_start, y_start, cost, upper, demand, tau, sigma):
    blocks = tiles[0, 0]
    rows = tile_row[0, 0]
    cols = tile_col[0, 0]
    tile_width = blocks.shape[1]
    scenarios, rows_dev = y_start.shape
    col_width = x_start.shape[1]
    row_tiles = rows_dev // tile_width
    col_tiles = col_width // tile_width
    live = (jnp.arange(rows_dev, dtype=jnp.int32) < row_count[0]).astype(jnp.float32)[None, :]
    row_hot = (jnp.arange(row_tiles, dtype=jnp.int32)[:, None] == rows[None, :]).astype(jnp.float32)
    col_hot = (jnp.arange(col_tiles, dtype=jnp.int32)[:, None] == cols[None, :]).astype(jnp.float32)
    step_primal = tau[:, None]
    step_dual = sigma[:, None]
    cost_row = cost[None, :]
    upper_row = upper[None, :]
    primal = x_start
    dual = y_start * live
    for iteration in range(ITERS):
        dual_low = dual.astype(jnp.bfloat16).reshape(scenarios, row_tiles, tile_width)
        picked = jnp.take(dual_low, rows, axis=1)
        contrib = jnp.einsum("str,trc->stc", picked, blocks, preferred_element_type=jnp.float32)
        kty_part = jnp.einsum(
            "kt,stc->skc", col_hot, contrib, precision=lax.Precision.HIGHEST
        ).reshape(scenarios, col_width)
        kty = lax.psum(kty_part, "plant")
        primal_new = jnp.minimum(
            jnp.maximum(primal - step_primal * (cost_row - kty), 0.0), upper_row
        )
        extra = (
            (2.0 * primal_new - primal)
            .astype(jnp.bfloat16)
            .reshape(scenarios, col_tiles, tile_width)
        )
        chosen = jnp.take(extra, cols, axis=1)
        product = jnp.einsum("stc,trc->str", chosen, blocks, preferred_element_type=jnp.float32)
        kx_part = jnp.einsum(
            "kt,str->skr", row_hot, product, precision=lax.Precision.HIGHEST
        ).reshape(scenarios, rows_dev)
        kx = lax.psum(kx_part, "col")
        dual = jnp.maximum(dual + step_dual * (demand - kx), 0.0) * live
        primal = primal_new
    return (primal, dual)


def solution(mesh):
    placed = (
        P("plant", "col", None, None, None),
        P("plant", "col", None),
        P("plant", "col", None),
        P("plant"),
        P(None, "col"),
        P(None, "plant"),
        P("col"),
        P("col"),
        P(None, "plant"),
        P(),
        P(),
    )
    return jax.shard_map(
        body,
        mesh=mesh,
        in_specs=placed,
        out_specs=(P(None, "col"), P(None, "plant")),
        check_vma=False,
    )
```

profile of v0, /device:TPU:0, one launch (start us, length us, event | category | flops | bytes accessed | tf_op | source)
XLA Modules:
  0.0 428.5 jit_solution(13103330824339237959)
XLA Ops:
  11.0 4.0 fusion.24
  15.0 2.1 fusion.22
  17.1 2.5 copy.31
  19.8 67.6 %all-reduce.7.cloned.1.call-done = f32[32,16384]{1,0:T(8,128)} async-done(((f32[32,16384]{1,0:T(8,128)}), f32[32,16384]{1,0:T(8,128)}) %all-reduce.7.cloned.1.call-update) | async-done | bytes 2097168 | tf_op jit(solution)/shard_map/psum | solution.py:34
  87.4 2.2 subtract_convert_fusion.2
  90.7 1.8 gather_fusion.1
  92.6 4.7 %fusion.27 = f32[32,48,256]{2,0,1:T(8,128)S(1)} fusion(bf16[1,1,48,256,256]{4,3,2,1,0:T(8,128)(2,1)} %param.15, bf16[48,32,256]{2,1,0:T(8,128)(2,1)S(1)} %gather_fusion.1, pred[48]{0:T(512)(128)(4,1)S(1)} %compare_and_fusion), kind=kOutput, calls=%fused_computation.37 | convolution fusion | flops 201719808 | bytes 8650800 | tf_op jit(solution)/shard_map/stc,trc->str/dot_general | solution.py:44
  97.4 1.5 fusion.20
  100.2 44.9 %all-reduce.9.cloned.1.call-done = f32[32,4096]{1,0:T(8,128)} async-done(((f32[32,4096]{1,0:T(8,128)}), f32[32,4096]{1,0:T(8,128)}) %all-reduce.9.cloned.1.call-update) | async-done | bytes 524304 | tf_op jit(solution)/shard_map/psum | solution.py:48
  145.2 1.2 fusion.88
  146.4 1.7 gather_fusion.2
  148.1 4.3 fusion.30
  152.4 2.2 fusion.18
  154.5 2.5 copy.33
  157.1 65.0 %all-reduce.11.cloned.1.call-done = f32[32,16384]{1,0:T(8,128)} async-done(((f32[32,16384]{1,0:T(8,128)}), f32[32,16384]{1,0:T(8,128)}) %all-reduce.11.cloned.1.call-update) | async-done | bytes 2097168 | tf_op jit(solution)/shard_map/psum | solution.py:34
  222.1 3.1 subtract_convert_fusion.1
  226.4 2.9 gather_fusion.3
  229.3 5.0 %fusion.33 = f32[32,48,256]{2,0,1:T(8,128)S(1)} fusion(bf16[1,1,48,256,256]{4,3,2,1,0:T(8,128)(2,1)} %param.15, bf16[48,32,256]{2,1,0:T(8,128)(2,1)} %gather_fusion.3, pred[48]{0:T(512)(128)(4,1)S(1)} %copy-done.12), kind=kOutput, calls=%fused_computation.39 | convolution fusion | flops 201719808 | bytes 8650800 | tf_op jit(solution)/shard_map/stc,trc->str/dot_general | solution.py:44
  234.3 1.5 fusion.16
  237.2 44.9 %all-reduce.13.cloned.1.call-done = f32[32,4096]{1,0:T(8,128)} async-done(((f32[32,4096]{1,0:T(8,128)}), f32[32,4096]{1,0:T(8,128)}) %all-reduce.13.cloned.1.call-update) | async-done | bytes 524304 | tf_op jit(solution)/shard_map/psum | solution.py:48
  282.1 1.5 fusion.87
  283.6 1.7 gather_fusion.4
  285.2 4.3 fusion.36
  289.5 2.1 fusion.14
  291.6 2.5 copy.35
  294.3 65.0 %all-reduce.15.cloned.1.call-done = f32[32,16384]{1,0:T(8,128)} async-done(((f32[32,16384]{1,0:T(8,128)}), f32[32,16384]{1,0:T(8,128)}) %all-reduce.15.cloned.1.call-update) | async-done | bytes 2097168 | tf_op jit(solution)/shard_map/psum | solution.py:34
  359.3 5.4 %subtract_convert_fusion = (bf16[32,16384]{1,0:T(8,128)(2,1)S(1)}, f32[32,16384]{1,0:T(8,128)}) fusion(f32[32,16384]{1,0:T(8,128)} %all-reduce.11.cloned.1.call-done, f32[16384]{0:T(1024)S(1)} %copy-done.4, f32[32,16384]{1,0:T(8,128)S(1)} %copy-done, f32[32,16384]{1,0:T(8,128)} %all-reduce.7.cloned.1.call-done, f32[16384]{0:T(1024)S(1)} %copy-done.5, ...), kind=kLoop, calls=%fused_computation.18 | loop fusion | flops 9437184 | bytes 11665536 | tf_op jit(solution)/shard_map/convert_element_type | solution.py:40
  364.8 1.7 gather_fusion.5
  366.5 5.0 %fusion.39 = f32[32,48,256]{2,0,1:T(8,128)S(1)} fusion(bf16[1,1,48,256,256]{4,3,2,1,0:T(8,128)(2,1)} %param.15, bf16[48,32,256]{2,1,0:T(8,128)(2,1)} %gather_fusion.5, pred[48]{0:T(512)(128)(4,1)S(1)} %copy-done.13), kind=kOutput, calls=%fused_computation.41 | convolution fusion | flops 201719808 | bytes 8650800 | tf_op jit(solution)/shard_map/stc,trc->str/dot_general | solution.py:44
  371.5 1.5 fusion.12
  374.2 45.1 %all-reduce.17.cloned.1.call-done = f32[32,4096]{1,0:T(8,128)} async-done(((f32[32,4096]{1,0:T(8,128)}), f32[32,4096]{1,0:T(8,128)}) %all-reduce.17.cloned.1.call-update) | async-done | bytes 524304 | tf_op jit(solution)/shard_map/psum | solution.py:48
  419.3 2.3 maximum_multiply_fusion
  (78 shorter events, 9.6 us)
Async XLA Ops:
  7.2 80.3 %all-reduce.7.cloned.1.call-start = ((), (), s32[]{:S(2)}) async-start(), calls=%async_computation | async-start | bytes 4194304 | tf_op jit(solution)/shard_map/psum | solution.py:34
  7.9 7.1 %copy-start.14 = (pred[48]{0:T(512)(128)(4,1)}, pred[48]{0:T(512)(128)(4,1)S(1)}, u32[]{:S(2)}) copy-start(pred[48]{0:T(512)(128)(4,1)S(1)} %compare_and_fusion.1) | copy-start | bytes 148
  9.2 5.8 %copy-start.7 = (s32[1024]{0:T(1024)}, s32[1024]{0:T(1024)S(1)}, u32[]{:S(2)}) copy-start(s32[1024]{0:T(1024)S(1)} %pad_clamp_fusion.1) | copy-start | bytes 12292
  11.0 4.0 copy-start.21
  17.1 70.3 %copy-start.4 = (f32[16384]{0:T(1024)S(1)}, f32[16384]{0:T(1024)}, u32[]{:S(2)}) copy-start(f32[16384]{0:T(1024)} %param.22) | copy-start | bytes 196612
  17.1 70.3 %copy-start.5 = (f32[16384]{0:T(1024)S(1)}, f32[16384]{0:T(1024)}, u32[]{:S(2)}) copy-start(f32[16384]{0:T(1024)} %param.21) | copy-start | bytes 196612
  19.7 67.8 %copy-start = (f32[32,16384]{1,0:T(8,128)S(1)}, f32[32,16384]{1,0:T(8,128)}, u32[]{:S(2)}) copy-start(f32[32,16384]{1,0:T(8,128)} %param.19) | copy-start | bytes 6291460
  19.7 67.8 %copy-start.18 = (f32[32]{0:T(128)S(1)}, f32[32]{0:T(128)}, u32[]{:S(2)}) copy-start(f32[32]{0:T(128)} %param.24) | copy-start | bytes 388
  19.7 125.4 %all-reduce.9.cloned.1.call-start = ((), (), s32[]{:S(2)}) async-start(), calls=%async_computation.1 | async-start | bytes 1048576 | tf_op jit(solution)/shard_map/psum | solution.py:48
  19.8 70.9 %copy-start.6 = (s32[1024]{0:T(1024)}, s32[1024]{0:T(1024)S(1)}, u32[]{:S(2)}) copy-start(s32[1024]{0:T(1024)S(1)} %pad_clamp_fusion) | copy-start | bytes 12292
  19.8 72.8 %copy-start.11 = (pred[48]{0:T(512)(128)(4,1)}, pred[48]{0:T(512)(128)(4,1)S(1)}, u32[]{:S(2)}) copy-start(pred[48]{0:T(512)(128)(4,1)S(1)} %compare_and_fusion) | copy-start | bytes 148
  92.6 4.8 %copy-start.8 = (s32[1,1,48]{2,1,0:T(1,128)S(1)}, s32[1,1,48]{2,1,0:T(1,128)}, u32[]{:S(2)}) copy-start(s32[1,1,48]{2,1,0:T(1,128)} %param.16) | copy-start | bytes 580
  97.3 47.8 %copy-start.1 = (f32[32,4096]{1,0:T(8,128)S(1)}, f32[32,4096]{1,0:T(8,128)}, u32[]{:S(2)}) copy-start(f32[32,4096]{1,0:T(8,128)} %param.20) | copy-start | bytes 1572868
  97.3 47.8 %copy-start.2 = (f32[32,4096]{1,0:T(8,128)S(1)}, f32[32,4096]{1,0:T(8,128)}, u32[]{:S(2)}) copy-start(f32[32,4096]{1,0:T(8,128)} %param.23) | copy-start | bytes 1572868
  97.3 47.8 %copy-start.15 = (f32[32]{0:T(128)S(1)}, f32[32]{0:T(128)}, u32[]{:S(2)}) copy-start(f32[32]{0:T(128)} %param.25) | copy-start | bytes 388
  100.0 122.1 %all-reduce.11.cloned.1.call-start = ((), (), s32[]{:S(2)}) async-start(), calls=%async_computation.2 | async-start | bytes 4194304 | tf_op jit(solution)/shard_map/psum | solution.py:34
  148.1 4.3 copy-start.22
  157.0 65.1 %copy-start.19 = (f32[32]{0:T(128)S(1)}, f32[32]{0:T(128)}, u32[]{:S(2)}) copy-start(f32[32]{0:T(128)} %param.24) | copy-start | bytes 388
  157.1 125.0 %all-reduce.13.cloned.1.call-start = ((), (), s32[]{:S(2)}) async-start(), calls=%async_computation.3 | async-start | bytes 1048576 | tf_op jit(solution)/shard_map/psum | solution.py:48
  225.3 4.0 copy-start.12
  229.3 5.0 %copy-start.9 = (s32[1,1,48]{2,1,0:T(1,128)S(1)}, s32[1,1,48]{2,1,0:T(1,128)}, u32[]{:S(2)}) copy-start(s32[1,1,48]{2,1,0:T(1,128)} %param.16) | copy-start | bytes 580
  234.3 47.8 %copy-start.16 = (f32[32]{0:T(128)S(1)}, f32[32]{0:T(128)}, u32[]{:S(2)}) copy-start(f32[32]{0:T(128)} %param.25) | copy-start | bytes 388
  236.9 122.3 %all-reduce.15.cloned.1.call-start = ((), (), s32[]{:S(2)}) async-start(), calls=%async_computation.4 | async-start | bytes 4194304 | tf_op jit(solution)/shard_map/psum | solution.py:34
  285.2 4.3 copy-start.23
  294.2 65.1 %copy-start.20 = (f32[32]{0:T(128)S(1)}, f32[32]{0:T(128)}, u32[]{:S(2)}) copy-start(f32[32]{0:T(128)} %param.24) | copy-start | bytes 388
  294.2 125.1 %all-reduce.17.cloned.1.call-start = ((), (), s32[]{:S(2)}) async-start(), calls=%async_computation.5 | async-start | bytes 1048576 | tf_op jit(solution)/shard_map/psum | solution.py:48
  364.7 1.8 copy-start.13
  366.5 5.0 %copy-start.10 = (s32[1,1,48]{2,1,0:T(1,128)S(1)}, s32[1,1,48]{2,1,0:T(1,128)}, u32[]{:S(2)}) copy-start(s32[1,1,48]{2,1,0:T(1,128)} %param.16) | copy-start | bytes 580
  371.5 47.8 %copy-start.3 = (f32[32,4096]{1,0:T(8,128)S(1)}, f32[32,4096]{1,0:T(8,128)}, u32[]{:S(2)}) copy-start(f32[32,4096]{1,0:T(8,128)} %all-reduce.9.cloned.1.call-done) | copy-start | bytes 1572868
  371.5 47.8 %copy-start.17 = (f32[32]{0:T(128)S(1)}, f32[32]{0:T(128)}, u32[]{:S(2)}) copy-start(f32[32]{0:T(128)} %param.25) | copy-start | bytes 388
Sparse Core Ops, SparseCore 0:
  19.8 67.5 all-reduce.6
  100.1 44.9 all-reduce.8
  157.2 64.8 all-reduce.10
  237.1 44.9 all-reduce.12
  294.3 64.8 all-reduce.14
  374.3 44.9 all-reduce.16
where the time goes:
time: 429 us; the launch traced here: 428 us
  waiting for transfers between devices  333 us (78%)
  matrix products  38.2 us (9%)
  local copies, waits for them, and re-layouts  23.7 us (6%)
  other arithmetic  18.2 us (4%)
  between operations  15.1 us (4%)
    psum x3, waiting for transfers between devices, body(): kty = lax.psum(kty_part, 'plant')  198 us
    psum x3, waiting for transfers between devices, body(): kx = lax.psum(kx_part, 'col')  135 us
    dot_general x3, matrix products, body(): jnp.einsum('stc,trc->str', chosen, blocks, preferred_element_type=jnp.flo...  14.7 us
    dot_general x3, matrix products, body(): jnp.einsum('str,trc->stc', picked, blocks, preferred_element_type=jnp.flo...  12.5 us
    unnamed x54, local copies, waits for them, and re-layouts  11 us
    convert_element_type x3, other arithmetic, body(): extra = (2.0 * primal_new - primal).astype(jnp.bfloat16).reshape(scenario...  10.7 us
  transfers between devices with their start and end apart: 6, of which 6 were waited for; matrix products, arithmetic and copies ran while one was open for 0% of the time, Pallas kernels for 0%

commit v1 on v0

v1 whole, which is shorter than its diff:
```python
import functools

import jax
import jax.numpy as jnp
from jax import lax
from jax.experimental import pallas as pl
from jax.experimental.pallas import tpu as pltpu
from jax.sharding import PartitionSpec as P

ITERS = 3
GROUPS = 2
VMEM_LIMIT = 40 << 20


def vmem():
    return pl.BlockSpec(memory_space=pltpu.VMEM)


def smem():
    return pl.BlockSpec(memory_space=pltpu.SMEM)


def row_block(rows, width, group):
    return pl.BlockSpec((rows, width), lambda i: (group, 0))


def whole(shape):
    return pl.BlockSpec(shape, lambda i: (0,) * len(shape))


def scalars():
    return pl.BlockSpec(memory_space=pltpu.SMEM)


def dual_kernel(first, n_tiles, tile_rows, tile_cols, width, *refs):
    if first:
        (rows_ref, cols_ref, info_ref, tiles_ref, y_ref,
         dual_ref, q0, q1, q2, q3, low, prods, acc) = refs
    else:
        (rows_ref, cols_ref, info_ref, tiles_ref, y_ref, demand_ref, sigma_ref,
         l_ref, l2_ref, r_ref, r2_ref,
         dual_ref, q0, q1, q2, q3, low, prods, acc) = refs
    scen = y_ref.shape[0]
    count, core, parity = info_ref[0], info_ref[1], info_ref[2]
    lane = lax.broadcasted_iota(jnp.int32, (scen, width), 1)
    half = tile_rows // 2
    if not first:
        sigma = jnp.broadcast_to(sigma_ref[...], (scen, width))
    for j in range(tile_rows):
        at = pl.ds(j * width, width)
        live = (lane < count - j * width).astype(jnp.float32)
        if first:
            dual = y_ref[:, at] * live
        else:
            if j < half:
                kx = l_ref[j] + l2_ref[j]
            else:
                kx = r_ref[j - half] + r2_ref[j - half]
            dual = jnp.maximum(y_ref[:, at] + sigma * (demand_ref[:, at] - kx), 0.0) * live
        dual_ref[:, at] = dual
        low[j] = dual.astype(jnp.bfloat16)
    for t in range(n_tiles):
        prods[t] = jnp.dot(low[rows_ref[t]], tiles_ref[t], preferred_element_type=jnp.float32)
    acc[...] = jnp.zeros(acc.shape, jnp.float32)
    quarter = tile_cols // 4
    for t in range(n_tiles):
        col = cols_ref[t]
        part = col // quarter
        slot = (part ^ (core * 2 + parity)) * quarter + col % quarter
        acc[slot] += prods[t]
    for i, ref in enumerate((q0, q1, q2, q3)):
        ref[...] = acc[pl.ds(i * quarter, quarter)]


def last_dual_kernel(tile_rows, width, info_ref, y_ref, demand_ref, sigma_ref, l_ref, l2_ref, r_ref, r2_ref, *rest):
    dual_ref = rest[-1]
    scen = y_ref.shape[0]
    count = info_ref[0]
    lane = lax.broadcasted_iota(jnp.int32, (scen, width), 1)
    half = tile_rows // 2
    sigma = jnp.broadcast_to(sigma_ref[...], (scen, width))
    for j in range(tile_rows):
        at = pl.ds(j * width, width)
        live = (lane < count - j * width).astype(jnp.float32)
        if j < half:
            kx = l_ref[j] + l2_ref[j]
        else:
            kx = r_ref[j - half] + r2_ref[j - half]
        dual_ref[:, at] = jnp.maximum(y_ref[:, at] + sigma * (demand_ref[:, at] - kx), 0.0) * live


def primal_kernel(n_tiles, tile_rows, tile_cols, width, has_into, *refs):
    (rows_ref, cols_ref, info_ref, tiles_ref, x_ref, cost_ref, upper_ref, tau_ref,
     k0, k1, k2, k3) = refs[:12]
    refs = refs[12 + has_into:]
    primal_ref, l_ref, r_ref, extra, prods, acc = refs
    scen = x_ref.shape[0]
    core, parity = info_ref[1], info_ref[2]
    quarter = tile_cols // 4
    half = tile_rows // 2
    tau = jnp.broadcast_to(tau_ref[...], (scen, width))
    for i, ref in enumerate((k0, k1, k2, k3)):
        base = ((core * 2 + parity) ^ i) * quarter
        for j in range(quarter):
            at = pl.ds(pl.multiple_of((base + j) * width, width), width)
            old = x_ref[:, at]
            new = jnp.minimum(
                jnp.maximum(old - tau * (cost_ref[:, at] - ref[j]), 0.0), upper_ref[:, at]
            )
            primal_ref[:, at] = new
            extra[base + j] = (2.0 * new - old).astype(jnp.bfloat16)
    for t in range(n_tiles):
        prods[t] = lax.dot_general(
            extra[cols_ref[t]], tiles_ref[t], (((1,), (1,)), ((), ())),
            preferred_element_type=jnp.float32,
        )
    acc[...] = jnp.zeros(acc.shape, jnp.float32)
    for t in range(n_tiles):
        acc[rows_ref[t]] += prods[t]
    l_ref[...] = acc[pl.ds(0, half)]
    r_ref[...] = acc[pl.ds(half, half)]


def body(tiles, tile_row, tile_col, row_count, x_start, y_start, cost, upper, demand, tau, sigma,
         *, n_plant, n_col):
    f32 = jnp.float32
    blocks = tiles[0, 0]
    rows = tile_row[0, 0]
    cols = tile_col[0, 0]
    n_tiles, width, _ = blocks.shape
    scenarios, rows_dev = y_start.shape
    col_width = x_start.shape[1]
    tile_rows = rows_dev // width
    tile_cols = col_width // width
    quarter = tile_cols // 4
    half = tile_rows // 2
    m = scenarios // GROUPS
    plant = lax.axis_index("plant")
    info = jnp.stack([row_count[0], plant & 1, (plant >> 1) & 1]).astype(jnp.int32)
    cost_row = cost[None, :]
    upper_row = upper[None, :]
    tau_col = tau[:, None]
    sigma_col = sigma[:, None]
    params = pltpu.CompilerParams(vmem_limit_bytes=VMEM_LIMIT)
    quarters = [jax.ShapeDtypeStruct((quarter, m, width), f32)] * 4
    halves = [jax.ShapeDtypeStruct((half, m, width), f32)] * 2
    flops = 2 * n_tiles * m * width * width
    estimate = pl.CostEstimate(flops=flops, bytes_accessed=n_tiles * width * width * 2, transcendentals=0)

    def swap(value, axis, size, bit):
        return lax.ppermute(value, axis, [(i, i ^ bit) for i in range(size)])

    def y_spec(arr, group):
        return row_block(m, rows_dev, group if arr.shape[0] == scenarios else 0)

    def x_spec(arr, group):
        return row_block(m, col_width, group if arr.shape[0] == scenarios else 0)

    def step_dual(group, dual, parts):
        first = parts is None
        args = [rows, cols, info, blocks, dual]
        specs = [scalars(), scalars(), scalars(), whole(blocks.shape), y_spec(dual, group)]
        if not first:
            args += [demand, sigma_col, *parts]
            specs += [y_spec(demand, group), row_block(m, 1, group)] + [whole((half, m, width))] * 4
        return pl.pallas_call(
            functools.partial(dual_kernel, first, n_tiles, tile_rows, tile_cols, width),
            grid=(1,),
            in_specs=specs,
            out_shape=[jax.ShapeDtypeStruct((m, rows_dev), f32)] + quarters,
            out_specs=[whole((m, rows_dev))] + [whole((quarter, m, width))] * 4,
            scratch_shapes=[
                pltpu.VMEM((tile_rows, m, width), jnp.bfloat16),
                pltpu.VMEM((n_tiles, m, width), f32),
                pltpu.VMEM((tile_cols, m, width), f32),
            ],
            compiler_params=params,
            cost_estimate=estimate,
            name="dual_step",
        )(*args)

    def step_primal(group, primal, kty, into, last):
        args = [rows, cols, info, blocks, primal, cost_row, upper_row, tau_col, *kty]
        specs = [scalars(), scalars(), scalars(), whole(blocks.shape), x_spec(primal, group),
                 whole((1, col_width)), whole((1, col_width)), row_block(m, 1, group)]
        specs += [whole((quarter, m, width))] * 4
        aliases = {}
        if into is not None:
            aliases = {len(args): 0}
            args.append(into)
            specs.append(pl.BlockSpec(memory_space=pl.ANY))
        out = jax.ShapeDtypeStruct((scenarios if last else m, col_width), f32)
        return pl.pallas_call(
            functools.partial(primal_kernel, n_tiles, tile_rows, tile_cols, width, int(into is not None)),
            grid=(1,),
            in_specs=specs,
            out_shape=[out] + halves,
            out_specs=[row_block(m, col_width, group if last else 0)] + [whole((half, m, width))] * 2,
            scratch_shapes=[
                pltpu.VMEM((tile_cols, m, width), jnp.bfloat16),
                pltpu.VMEM((n_tiles, m, width), f32),
                pltpu.VMEM((tile_rows, m, width), f32),
            ],
            input_output_aliases=aliases,
            compiler_params=params,
            cost_estimate=estimate,
            name="primal_step",
        )(*args)

    def finish_dual(group, dual, parts, into):
        args = [info, dual, demand, sigma_col, *parts]
        specs = [scalars(), y_spec(dual, group), y_spec(demand, group), row_block(m, 1, group)]
        specs += [whole((half, m, width))] * 4
        aliases = {}
        if into is not None:
            aliases = {len(args): 0}
            args.append(into)
            specs.append(pl.BlockSpec(memory_space=pl.ANY))
        return pl.pallas_call(
            functools.partial(last_dual_kernel, tile_rows, width),
            grid=(1,),
            in_specs=specs,
            out_shape=jax.ShapeDtypeStruct((scenarios, rows_dev), f32),
            out_specs=row_block(m, rows_dev, group),
            input_output_aliases=aliases,
            compiler_params=params,
            name="dual_end",
        )(*args)

    def over_plant(q0, q1, q2, q3):
        g1 = swap(q3, "plant", n_plant, 1)
        g0 = swap(q2, "plant", n_plant, 1)
        own = q0 + g0 + swap(q1 + g1, "plant", n_plant, 2)
        bit = 4
        while bit < n_plant:
            own = own + swap(own, "plant", n_plant, bit)
            bit *= 2
        pair = swap(own, "plant", n_plant, 2)
        return own, pair, swap(own, "plant", n_plant, 1), swap(pair, "plant", n_plant, 1)

    def over_col(l, r):
        bits = []
        bit = 1
        while bit < n_col:
            bits.append(bit)
            bit *= 2
        turned = bits[len(bits) // 2:] + bits[:len(bits) // 2]
        for a, b in zip(bits[:-1], turned[:-1]):
            l, r = l + swap(l, "col", n_col, a), r + swap(r, "col", n_col, b)
        return l, swap(l, "col", n_col, bits[-1]), r, swap(r, "col", n_col, turned[-1])

    duals = [y_start] * GROUPS
    primals = [x_start] * GROUPS
    parts = [None] * GROUPS
    primal_out = None
    for iteration in range(ITERS):
        last = iteration == ITERS - 1
        for g in range(GROUPS):
            duals[g], *qs = step_dual(g, duals[g], parts[g])
            kty = over_plant(*qs)
            primals[g], l, r = step_primal(g, primals[g], kty, primal_out if last else None, last)
            if last:
                primal_out = primals[g]
            parts[g] = over_col(l, r)
    dual_out = None
    for g in range(GROUPS):
        dual_out = finish_dual(g, duals[g], parts[g], dual_out)
    return primal_out, dual_out


def solution(mesh):
    placed = (
        P("plant", "col", None, None, None),
        P("plant", "col", None),
        P("plant", "col", None),
        P("plant"),
        P(None, "col"),
        P(None, "plant"),
        P("col"),
        P("col"),
        P(None, "plant"),
        P(),
        P(),
    )
    return jax.shard_map(
        functools.partial(body, n_plant=mesh.shape["plant"], n_col=mesh.shape["col"]),
        mesh=mesh,
        in_specs=placed,
        out_specs=(P(None, "col"), P(None, "plant")),
        check_vma=False,
    )
```

time: 429 us -> 243 us (0.57)
  waiting for transfers between devices: 333 us -> 137 us
  starting transfers between devices: 0.65 us -> 49.9 us
  matrix products: 38.2 us -> 0 us
  Pallas kernels: 0 us -> 32.5 us
  other arithmetic: 18.2 us -> 2.92 us
  between operations: 15.1 us -> 1.7 us
  local copies, waits for them, and re-layouts: 23.7 us -> 19 us
    psum x6 -> x0, waiting for transfers between devices: 333 us -> none  [the longest x3 198 us: body(): kty = lax.psum(kty_part, 'plant')]
    ppermute x0 -> x66, waiting for transfers between devices: none -> 137 us  [swap(): return lax.ppermute(value, axis, [(i, i ^ bit) for i in range(size)])]
    ppermute x0 -> x66, starting transfers between devices: none -> 49.9 us  [swap(): return lax.ppermute(value, axis, [(i, i ^ bit) for i in range(size)])]
    dot_general x12 -> x0, matrix products: 38.2 us -> none  [the longest x3 14.7 us: body(): jnp.einsum('stc,trc->str', chosen, blocks, preferred_element_type=jnp.flo...]
    pallas_call x0 -> x14, Pallas kernels: none -> 32.5 us  [the longest x6 19.2 us: step_primal(): pl.pallas_call(functools.partial(primal_kernel, n_tiles, tile_rows, tile_...]
    convert_element_type x7 -> x0, other arithmetic: 14.5 us -> none  [the longest x3 10.7 us: body(): extra = (2.0 * primal_new - primal).astype(jnp.bfloat16).reshape(scenario...]
    gather x6 -> x0, local copies, waits for them, and re-layouts: 10.3 us -> none  [the longest x3 6.36 us: body(): chosen = jnp.take(extra, cols, axis=1)]
    unnamed x54 -> x48, local copies, waits for them, and re-layouts: 11 us -> 17.6 us
  transfers between devices with their start and end apart: 6 -> 66, of which waited for: 6 -> 32; matrix products, arithmetic and copies ran while one was open for 0% -> 2% of each run, Pallas kernels for 0% -> 12%
where the time goes in v1:
time: 243 us
  waiting for transfers between devices  137 us (56%)
  starting transfers between devices  49.9 us (21%)
  Pallas kernels  32.5 us (13%)
  local copies, waits for them, and re-layouts  19 us (8%)
  other arithmetic  2.92 us (1%)
    ppermute x66, waiting for transfers between devices, swap(): return lax.ppermute(value, axis, [(i, i ^ bit) for i in range(size)])  137 us
    ppermute x66, starting transfers between devices, swap(): return lax.ppermute(value, axis, [(i, i ^ bit) for i in range(size)])  49.9 us
    pallas_call x6, Pallas kernels, step_primal(): pl.pallas_call(functools.partial(primal_kernel, n_tiles, tile_rows, tile_...  19.2 us
    unnamed x48, local copies, waits for them, and re-layouts  17.6 us
    pallas_call x6, Pallas kernels, step_dual(): pl.pallas_call(functools.partial(dual_kernel, first, n_tiles, tile_rows,...  10.6 us
  transfers between devices with their start and end apart: 66, of which 32 were waited for; matrix products, arithmetic and copies ran while one was open for 2% of the time, Pallas kernels for 12%

profile of v1, /device:TPU:0, one launch (start us, length us, event | category | flops | bytes accessed | tf_op | source)
XLA Modules:
  0.0 242.5 jit_solution(12022873154523249311)
XLA Ops:
  1.4 2.8 %copy-done = bf16[1,1,48,256,256]{4,3,2,1,0:T(8,128)(2,1)S(1)} copy-done((bf16[1,1,48,256,256]{4,3,2,1,0:T(8,128)(2,1)S(1)}, bf16[1,1,48,256,256]{4,3,2,1,0:T(8,128)(2,1)}, u32[]{:S(2)}) %copy-start) | copy-done | bytes 6291480
  10.9 2.7 %collective-permute-start.31 = (f32[16,16,256]{2,1,0:T(8,128)S(1)}, f32[16,16,256]{2,1,0:T(8,128)S(1)}, u32[]{:S(2)}, u32[]{:S(2)}) collective-permute-start(f32[16,16,256]{2,1,0:T(8,128)S(1)} %add.125), channel_id=1, source_target_pairs={{0,8},{4,12},{8,0},{12,4},{16,24},{20,28},{24,16},{28,20},{1,9},{5... | collective-permute-start | bytes 786440 | tf_op jit(solution)/shard_map/ppermute | solution.py:151
  14.8 6.1 %collective-permute-done.31 = f32[16,16,256]{2,1,0:T(8,128)S(1)} collective-permute-done((f32[16,16,256]{2,1,0:T(8,128)S(1)}, f32[16,16,256]{2,1,0:T(8,128)S(1)}, u32[]{:S(2)}, u32[]{:S(2)}) %collective-permute-start.31) | collective-permute-done | bytes 262176 | tf_op jit(solution)/shard_map/ppermute | solution.py:151
  20.9 3.0 %collective-permute-start.32 = (f32[16,16,256]{2,1,0:T(8,128)S(1)}, f32[16,16,256]{2,1,0:T(8,128)S(1)}, u32[]{:S(2)}, u32[]{:S(2)}) collective-permute-start(f32[16,16,256]{2,1,0:T(8,128)S(1)} %add_add_fusion.2), channel_id=1, source_target_pairs={{0,16},{4,20},{8,24},{12,28},{16,0},{20,4},{24,8},{28,12},{1,17},{... | collective-permute-start | bytes 786440 | tf_op jit(solution)/shard_map/ppermute | solution.py:151
  23.9 6.7 %collective-permute-done.2 = f32[16,16,256]{2,1,0:T(8,128)S(1)} collective-permute-done((f32[16,16,256]{2,1,0:T(8,128)S(1)}, f32[16,16,256]{2,1,0:T(8,128)S(1)}, u32[]{:S(2)}, u32[]{:S(2)}) %collective-permute-start.2) | collective-permute-done | bytes 262176 | tf_op jit(solution)/shard_map/ppermute | solution.py:151
  30.7 11.5 %collective-permute-done.32 = f32[16,16,256]{2,1,0:T(8,128)S(1)} collective-permute-done((f32[16,16,256]{2,1,0:T(8,128)S(1)}, f32[16,16,256]{2,1,0:T(8,128)S(1)}, u32[]{:S(2)}, u32[]{:S(2)}) %collective-permute-start.32) | collective-permute-done | bytes 262176 | tf_op jit(solution)/shard_map/ppermute | solution.py:151
  43.5 3.1 %collective-permute-done.3 = f32[16,16,256]{2,1,0:T(8,128)S(1)} collective-permute-done((f32[16,16,256]{2,1,0:T(8,128)S(1)}, f32[16,16,256]{2,1,0:T(8,128)S(1)}, u32[]{:S(2)}, u32[]{:S(2)}) %collective-permute-start.3) | collective-permute-done | bytes 262176 | tf_op jit(solution)/shard_map/ppermute | solution.py:151
  47.5 4.8 %collective-permute-done.33.refs_9_ = f32[16,16,256]{2,1,0:T(8,128)S(1)} collective-permute-done((f32[16,16,256]{2,1,0:T(8,128)S(1)}, f32[16,16,256]{2,1,0:T(8,128)S(1)}, u32[]{:S(2)}, u32[]{:S(2)}) %collective-permute-start.33) | collective-permute-done | bytes 262176 | tf_op jit(solution)/shard_map/ppermute | solution.py:151
  52.8 5.1 %collective-permute-done.4.refs_9_ = f32[16,16,256]{2,1,0:T(8,128)} collective-permute-done((f32[16,16,256]{2,1,0:T(8,128)S(1)}, f32[16,16,256]{2,1,0:T(8,128)}, u32[]{:S(2)}, u32[]{:S(2)}) %collective-permute-start.4) | collective-permute-done | bytes 262176 | tf_op jit(solution)/shard_map/ppermute | solution.py:151
  58.7 2.8 %copy-done.1 = bf16[1,1,48,256,256]{4,3,2,1,0:T(8,128)(2,1)S(1)} copy-done((bf16[1,1,48,256,256]{4,3,2,1,0:T(8,128)(2,1)S(1)}, bf16[1,1,48,256,256]{4,3,2,1,0:T(8,128)(2,1)}, u32[]{:S(2)}) %copy-start.1) | copy-done | bytes 6291480
  63.4 3.0 %primal_step.8 = (f32[16,16384]{1,0:T(8,128)S(1)}, f32[8,16,256]{2,1,0:T(8,128)S(1)}, f32[8,16,256]{2,1,0:T(8,128)S(1)}) custom-call(s32[48]{0:T(128)S(1)} %bitcast.35, s32[48]{0:T(128)S(1)} %bitcast.47, s32[3]{0:T(128)S(1)} %copy-done.15, bf16[48,256,256]{2,1,0:T(8,128)(2,1)S(1)} %bitcast.11, f32[32,16384]{1,0:T(8,128)S(1)} %copy-done.4, ...), custom_call_target="tpu_custom_call" | custom-call | flops 100663296 | bytes 6291456 | tf_op jit(solution)/shard_map/primal_step/pallas_call | solution.py:193
  70.4 2.9 %collective-permute-done.36 = f32[8,16,256]{2,1,0:T(8,128)S(1)} collective-permute-done((f32[8,16,256]{2,1,0:T(8,128)S(1)}, f32[8,16,256]{2,1,0:T(8,128)S(1)}, u32[]{:S(2)}, u32[]{:S(2)}) %collective-permute-start.36) | collective-permute-done | bytes 131104 | tf_op jit(solution)/shard_map/ppermute | solution.py:151
  76.5 3.9 %primal_step.6 = (f32[16,16384]{1,0:T(8,128)S(1)}, f32[8,16,256]{2,1,0:T(8,128)}, f32[8,16,256]{2,1,0:T(8,128)}) custom-call(s32[48]{0:T(128)S(1)} %bitcast.36, s32[48]{0:T(128)S(1)} %bitcast.48, s32[3]{0:T(128)S(1)} %copy-done.15, bf16[48,256,256]{2,1,0:T(8,128)(2,1)S(1)} %bitcast.12, f32[32,16384]{1,0:T(8,128)S(1)} %copy-done.4, f32[1,16384]{1,0:T(1,128)S(1)} %bitcast.22, ...), custom_call_target="tpu_custom_call" | custom-call | flops 100663296 | bytes 6291456 | tf_op jit(solution)/shard_map/primal_step/pallas_call | solution.py:193
  83.8 2.8 %copy-done.2 = bf16[1,1,48,256,256]{4,3,2,1,0:T(8,128)(2,1)S(1)} copy-done((bf16[1,1,48,256,256]{4,3,2,1,0:T(8,128)(2,1)S(1)}, bf16[1,1,48,256,256]{4,3,2,1,0:T(8,128)(2,1)}, u32[]{:S(2)}) %copy-start.2) | copy-done | bytes 6291480
  104.8 7.0 %collective-permute-done.42 = f32[16,16,256]{2,1,0:T(8,128)S(1)} collective-permute-done((f32[16,16,256]{2,1,0:T(8,128)S(1)}, f32[16,16,256]{2,1,0:T(8,128)S(1)}, u32[]{:S(2)}, u32[]{:S(2)}) %collective-permute-start.42) | collective-permute-done | bytes 262176 | tf_op jit(solution)/shard_map/ppermute | solution.py:151
  114.0 7.1 %collective-permute-done.13 = f32[16,16,256]{2,1,0:T(8,128)S(1)} collective-permute-done((f32[16,16,256]{2,1,0:T(8,128)S(1)}, f32[16,16,256]{2,1,0:T(8,128)S(1)}, u32[]{:S(2)}, u32[]{:S(2)}) %collective-permute-start.13) | collective-permute-done | bytes 262176 | tf_op jit(solution)/shard_map/ppermute | solution.py:151
  121.2 10.6 %collective-permute-done.43 = f32[16,16,256]{2,1,0:T(8,128)S(1)} collective-permute-done((f32[16,16,256]{2,1,0:T(8,128)S(1)}, f32[16,16,256]{2,1,0:T(8,128)S(1)}, u32[]{:S(2)}, u32[]{:S(2)}) %collective-permute-start.43) | collective-permute-done | bytes 262176 | tf_op jit(solution)/shard_map/ppermute | solution.py:151
  132.9 3.6 %collective-permute-done.14 = f32[16,16,256]{2,1,0:T(8,128)S(1)} collective-permute-done((f32[16,16,256]{2,1,0:T(8,128)S(1)}, f32[16,16,256]{2,1,0:T(8,128)S(1)}, u32[]{:S(2)}, u32[]{:S(2)}) %collective-permute-start.14) | collective-permute-done | bytes 262176 | tf_op jit(solution)/shard_map/ppermute | solution.py:151
  137.2 4.9 %collective-permute-done.44.refs_9_ = f32[16,16,256]{2,1,0:T(8,128)S(1)} collective-permute-done((f32[16,16,256]{2,1,0:T(8,128)S(1)}, f32[16,16,256]{2,1,0:T(8,128)S(1)}, u32[]{:S(2)}, u32[]{:S(2)}) %collective-permute-start.44) | collective-permute-done | bytes 262176 | tf_op jit(solution)/shard_map/ppermute | solution.py:151
  142.6 5.0 %collective-permute-done.15.refs_9_ = f32[16,16,256]{2,1,0:T(8,128)S(1)} collective-permute-done((f32[16,16,256]{2,1,0:T(8,128)S(1)}, f32[16,16,256]{2,1,0:T(8,128)S(1)}, u32[]{:S(2)}, u32[]{:S(2)}) %collective-permute-start.15) | collective-permute-done | bytes 262176 | tf_op jit(solution)/shard_map/ppermute | solution.py:151
  147.7 2.6 %primal_step.9 = (f32[16,16384]{1,0:T(8,128)S(1)}, f32[8,16,256]{2,1,0:T(8,128)S(1)}, f32[8,16,256]{2,1,0:T(8,128)S(1)}) custom-call(s32[48]{0:T(128)S(1)} %bitcast.39, s32[48]{0:T(128)S(1)} %bitcast.51, s32[3]{0:T(128)S(1)} %copy-done.16, bf16[48,256,256]{2,1,0:T(8,128)(2,1)S(1)} %bitcast.15, f32[16,16384]{1,0:T(8,128)S(1)} %copy-done.11, ...), custom_call_target="tpu_custom_call" | custom-call | flops 100663296 | bytes 6291456 | tf_op jit(solution)/shard_map/primal_step/pallas_call | solution.py:193
  152.4 3.9 %collective-permute-done.47 = f32[8,16,256]{2,1,0:T(8,128)S(1)} collective-permute-done((f32[8,16,256]{2,1,0:T(8,128)S(1)}, f32[8,16,256]{2,1,0:T(8,128)S(1)}, u32[]{:S(2)}, u32[]{:S(2)}) %collective-permute-start.47) | collective-permute-done | bytes 131104 | tf_op jit(solution)/shard_map/ppermute | solution.py:151
  158.4 2.8 %primal_step.7 = (f32[16,16384]{1,0:T(8,128)S(1)}, f32[8,16,256]{2,1,0:T(8,128)S(1)}, f32[8,16,256]{2,1,0:T(8,128)S(1)}) custom-call(s32[48]{0:T(128)S(1)} %bitcast.40, s32[48]{0:T(128)S(1)} %bitcast.52, s32[3]{0:T(128)S(1)} %copy-done.16, bf16[48,256,256]{2,1,0:T(8,128)(2,1)S(1)} %bitcast.16, f32[16,16384]{1,0:T(8,128)S(1)} %copy-done.9, ...), custom_call_target="tpu_custom_call" | custom-call | flops 100663296 | bytes 6291456 | tf_op jit(solution)/shard_map/primal_step/pallas_call | solution.py:193
  168.5 2.8 %collective-permute-done.19.refs_8_ = f32[8,16,256]{2,1,0:T(8,128)S(1)} collective-permute-done((f32[8,16,256]{2,1,0:T(8,128)S(1)}, f32[8,16,256]{2,1,0:T(8,128)S(1)}, u32[]{:S(2)}, u32[]{:S(2)}) %collective-permute-start.19) | collective-permute-done | bytes 131104 | tf_op jit(solution)/shard_map/ppermute | solution.py:151
  177.5 7.0 %collective-permute-done.53 = f32[16,16,256]{2,1,0:T(8,128)S(1)} collective-permute-done((f32[16,16,256]{2,1,0:T(8,128)S(1)}, f32[16,16,256]{2,1,0:T(8,128)S(1)}, u32[]{:S(2)}, u32[]{:S(2)}) %collective-permute-start.53) | collective-permute-done | bytes 262176 | tf_op jit(solution)/shard_map/ppermute | solution.py:151
  186.6 7.2 %collective-permute-done.24 = f32[16,16,256]{2,1,0:T(8,128)S(1)} collective-permute-done((f32[16,16,256]{2,1,0:T(8,128)S(1)}, f32[16,16,256]{2,1,0:T(8,128)S(1)}, u32[]{:S(2)}, u32[]{:S(2)}) %collective-permute-start.24) | collective-permute-done | bytes 262176 | tf_op jit(solution)/shard_map/ppermute | solution.py:151
  193.9 10.6 %collective-permute-done.54 = f32[16,16,256]{2,1,0:T(8,128)S(1)} collective-permute-done((f32[16,16,256]{2,1,0:T(8,128)S(1)}, f32[16,16,256]{2,1,0:T(8,128)S(1)}, u32[]{:S(2)}, u32[]{:S(2)}) %collective-permute-start.54) | collective-permute-done | bytes 262176 | tf_op jit(solution)/shard_map/ppermute | solution.py:151
  205.7 3.5 %collective-permute-done.25 = f32[16,16,256]{2,1,0:T(8,128)S(1)} collective-permute-done((f32[16,16,256]{2,1,0:T(8,128)S(1)}, f32[16,16,256]{2,1,0:T(8,128)S(1)}, u32[]{:S(2)}, u32[]{:S(2)}) %collective-permute-start.25) | collective-permute-done | bytes 262176 | tf_op jit(solution)/shard_map/ppermute | solution.py:151
  209.8 5.0 %collective-permute-done.55.refs_9_ = f32[16,16,256]{2,1,0:T(8,128)S(1)} collective-permute-done((f32[16,16,256]{2,1,0:T(8,128)S(1)}, f32[16,16,256]{2,1,0:T(8,128)S(1)}, u32[]{:S(2)}, u32[]{:S(2)}) %collective-permute-start.55) | collective-permute-done | bytes 262176 | tf_op jit(solution)/shard_map/ppermute | solution.py:151
  215.3 5.0 %collective-permute-done.26.refs_9_ = f32[16,16,256]{2,1,0:T(8,128)S(1)} collective-permute-done((f32[16,16,256]{2,1,0:T(8,128)S(1)}, f32[16,16,256]{2,1,0:T(8,128)S(1)}, u32[]{:S(2)}, u32[]{:S(2)}) %collective-permute-start.26) | collective-permute-done | bytes 262176 | tf_op jit(solution)/shard_map/ppermute | solution.py:151
  220.3 3.4 %primal_step.10 = (f32[32,16384]{1,0:T(8,128)}, f32[8,16,256]{2,1,0:T(8,128)S(1)}, f32[8,16,256]{2,1,0:T(8,128)S(1)}) custom-call(s32[48]{0:T(128)S(1)} %bitcast.43, s32[48]{0:T(128)S(1)} %bitcast.55, s32[3]{0:T(128)S(1)} %copy-done.16, bf16[48,256,256]{2,1,0:T(8,128)(2,1)S(1)} %bitcast.19, f32[16,16384]{1,0:T(8,128)S(1)} %get-tuple-element.82.refs_4_, ...), custom_call_target="tpu_custom_call" | custom-call | flops 100663296 | bytes 6291456 | tf_op jit(solution)/shard_map/primal_step/pallas_call | solution.py:193
  225.6 3.4 %primal_step.11 = (f32[32,16384]{1,0:T(8,128)}, f32[8,16,256]{2,1,0:T(8,128)S(1)}, f32[8,16,256]{2,1,0:T(8,128)S(1)}) custom-call(s32[48]{0:T(128)S(1)} %bitcast.44, s32[48]{0:T(128)S(1)} %bitcast.56, s32[3]{0:T(128)S(1)} %copy-done.16, bf16[48,256,256]{2,1,0:T(8,128)(2,1)S(1)} %bitcast.20, ...), custom_call_target="tpu_custom_call", output_to_operand_aliasing={{0}: (12, {})} | custom-call | flops 100663296 | bytes 6291456 | tf_op jit(solution)/shard_map/primal_step/pallas_call | solution.py:193
  (195 shorter events, 84.3 us)
Async XLA Ops:
  10.9 9.9 %collective-permute-start.31 = (f32[16,16,256]{2,1,0:T(8,128)S(1)}, f32[16,16,256]{2,1,0:T(8,128)S(1)}, u32[]{:S(2)}, u32[]{:S(2)}) collective-permute-start(f32[16,16,256]{2,1,0:T(8,128)S(1)} %add.125), channel_id=1, source_target_pairs={{0,8},{4,12},{8,0},{12,4},{16,24},{20,28},{24,16},{28,20},{1,9},{5... | collective-permute-start | bytes 786440 | tf_op jit(solution)/shard_map/ppermute | solution.py:151
  13.6 10.2 %collective-permute-start = (f32[16,16,256]{2,1,0:T(8,128)S(1)}, f32[16,16,256]{2,1,0:T(8,128)S(1)}, u32[]{:S(2)}, u32[]{:S(2)}) collective-permute-start(f32[16,16,256]{2,1,0:T(8,128)S(1)} %get-tuple-element.51), channel_id=1, source_target_pairs={{0,4},{4,0},{8,12},{12,8},{16,20},{20,16},{24,28},{28,24},{1,5},{5... | collective-permute-start | bytes 786440 | tf_op jit(solution)/shard_map/ppermute | solution.py:151
  13.9 16.7 %collective-permute-start.2 = (f32[16,16,256]{2,1,0:T(8,128)S(1)}, f32[16,16,256]{2,1,0:T(8,128)S(1)}, u32[]{:S(2)}, u32[]{:S(2)}) collective-permute-start(f32[16,16,256]{2,1,0:T(8,128)S(1)} %add.109), channel_id=1, source_target_pairs={{0,8},{4,12},{8,0},{12,4},{16,24},{20,28},{24,16},{28,20},{1,9},{5... | collective-permute-start | bytes 786440 | tf_op jit(solution)/shard_map/ppermute | solution.py:151
  20.9 21.3 %collective-permute-start.32 = (f32[16,16,256]{2,1,0:T(8,128)S(1)}, f32[16,16,256]{2,1,0:T(8,128)S(1)}, u32[]{:S(2)}, u32[]{:S(2)}) collective-permute-start(f32[16,16,256]{2,1,0:T(8,128)S(1)} %add_add_fusion.2), channel_id=1, source_target_pairs={{0,16},{4,20},{8,24},{12,28},{16,0},{20,4},{24,8},{28,12},{1,17},{... | collective-permute-start | bytes 786440 | tf_op jit(solution)/shard_map/ppermute | solution.py:151
  30.6 16.0 %collective-permute-start.3 = (f32[16,16,256]{2,1,0:T(8,128)S(1)}, f32[16,16,256]{2,1,0:T(8,128)S(1)}, u32[]{:S(2)}, u32[]{:S(2)}) collective-permute-start(f32[16,16,256]{2,1,0:T(8,128)S(1)} %add_add_fusion.5), channel_id=1, source_target_pairs={{0,16},{4,20},{8,24},{12,28},{16,0},{20,4},{24,8},{28,12},{1,17},{... | collective-permute-start | bytes 786440 | tf_op jit(solution)/shard_map/ppermute | solution.py:151
  42.2 10.0 %collective-permute-start.33 = (f32[16,16,256]{2,1,0:T(8,128)S(1)}, f32[16,16,256]{2,1,0:T(8,128)S(1)}, u32[]{:S(2)}, u32[]{:S(2)}) collective-permute-start(f32[16,16,256]{2,1,0:T(8,128)S(1)} %add.127.refs_8_), channel_id=1, source_target_pairs={{0,8},{4,12},{8,0},{12,4},{16,24},{20,28},{24,16},{28,20},{1,9},{5... | collective-permute-start | bytes 786440 | tf_op jit(solution)/shard_map/ppermute | solution.py:151
  46.7 11.2 %collective-permute-start.4 = (f32[16,16,256]{2,1,0:T(8,128)S(1)}, f32[16,16,256]{2,1,0:T(8,128)}, u32[]{:S(2)}, u32[]{:S(2)}) collective-permute-start(f32[16,16,256]{2,1,0:T(8,128)S(1)} %add.111.refs_8_), channel_id=1, source_target_pairs={{0,8},{4,12},{8,0},{12,4},{16,24},{20,28},{24,16},{28,20},{1,9},{5... | collective-permute-start | bytes 786440 | tf_op jit(solution)/shard_map/ppermute | solution.py:151
  47.5 11.2 %collective-permute-start.34 = (f32[16,16,256]{2,1,0:T(8,128)S(1)}, f32[16,16,256]{2,1,0:T(8,128)S(1)}, u32[]{:S(2)}, u32[]{:S(2)}) collective-permute-start(f32[16,16,256]{2,1,0:T(8,128)S(1)} %add.127.refs_8_), channel_id=1, source_target_pairs={{0,4},{4,0},{8,12},{12,8},{16,20},{20,16},{24,28},{28,24},{1,5},{5... | collective-permute-start | bytes 786440 | tf_op jit(solution)/shard_map/ppermute | solution.py:151
  52.3 24.3 %collective-permute-start.5 = (f32[16,16,256]{2,1,0:T(8,128)S(1)}, f32[16,16,256]{2,1,0:T(8,128)}, u32[]{:S(2)}, u32[]{:S(2)}) collective-permute-start(f32[16,16,256]{2,1,0:T(8,128)S(1)} %add.111.refs_8_), channel_id=1, source_target_pairs={{0,4},{4,0},{8,12},{12,8},{16,20},{20,16},{24,28},{28,24},{1,5},{5... | collective-permute-start | bytes 786440 | tf_op jit(solution)/shard_map/ppermute | solution.py:151
  57.9 18.6 %collective-permute-start.6 = (f32[16,16,256]{2,1,0:T(8,128)}, f32[16,16,256]{2,1,0:T(8,128)}, u32[]{:S(2)}, u32[]{:S(2)}) collective-permute-start(f32[16,16,256]{2,1,0:T(8,128)} %collective-permute-done.4.refs_9_), channel_id=1, source_target_pairs={{0,4},{4,0},{8,12},{12,8},{16,20},{20,16},{24,28},{28,24},{1,5},{5... | collective-permute-start | bytes 786440 | tf_op jit(solution)/shard_map/ppermute | solution.py:151
  73.3 10.4 %collective-permute-start.37 = (f32[8,16,256]{2,1,0:T(8,128)S(1)}, f32[8,16,256]{2,1,0:T(8,128)}, u32[]{:S(2)}, u32[]{:S(2)}) collective-permute-start(f32[8,16,256]{2,1,0:T(8,128)S(1)} %add.128.refs_7_), channel_id=1, source_target_pairs={{0,2},{1,3},{2,0},{3,1},{4,6},{5,7},{6,4},{7,5},{8,10},{9,11},{10,... | collective-permute-start | bytes 393224 | tf_op jit(solution)/shard_map/ppermute | solution.py:151
  81.4 10.4 %collective-permute-start.7 = (f32[8,16,256]{2,1,0:T(8,128)}, f32[8,16,256]{2,1,0:T(8,128)S(1)}, u32[]{:S(2)}, u32[]{:S(2)}) collective-permute-start(f32[8,16,256]{2,1,0:T(8,128)} %get-tuple-element.56), channel_id=1, source_target_pairs={{0,1},{1,0},{2,3},{3,2},{4,5},{5,4},{6,7},{7,6},{8,9},{9,8},{10,11... | collective-permute-start | bytes 393224 | tf_op jit(solution)/shard_map/ppermute | solution.py:151
  81.9 11.7 %collective-permute-start.9 = (f32[8,16,256]{2,1,0:T(8,128)}, f32[8,16,256]{2,1,0:T(8,128)S(1)}, u32[]{:S(2)}, u32[]{:S(2)}) collective-permute-start(f32[8,16,256]{2,1,0:T(8,128)} %get-tuple-element.57), channel_id=1, source_target_pairs={{0,2},{1,3},{2,0},{3,1},{4,6},{5,7},{6,4},{7,5},{8,10},{9,11},{10,... | collective-permute-start | bytes 393224 | tf_op jit(solution)/shard_map/ppermute | solution.py:151
  91.6 10.9 %collective-permute-start.41 = (f32[16,16,256]{2,1,0:T(8,128)S(1)}, f32[16,16,256]{2,1,0:T(8,128)S(1)}, u32[]{:S(2)}, u32[]{:S(2)}) collective-permute-start(f32[16,16,256]{2,1,0:T(8,128)S(1)} %get-tuple-element.81), channel_id=1, source_target_pairs={{0,4},{4,0},{8,12},{12,8},{16,20},{20,16},{24,28},{28,24},{1,5},{5... | collective-permute-start | bytes 786440 | tf_op jit(solution)/shard_map/ppermute | solution.py:151
  102.6 11.4 %collective-permute-start.11 = (f32[16,16,256]{2,1,0:T(8,128)S(1)}, f32[16,16,256]{2,1,0:T(8,128)S(1)}, u32[]{:S(2)}, u32[]{:S(2)}) collective-permute-start(f32[16,16,256]{2,1,0:T(8,128)S(1)} %get-tuple-element.59), channel_id=1, source_target_pairs={{0,4},{4,0},{8,12},{12,8},{16,20},{20,16},{24,28},{28,24},{1,5},{5... | collective-permute-start | bytes 786440 | tf_op jit(solution)/shard_map/ppermute | solution.py:151
  103.6 17.5 %collective-permute-start.13 = (f32[16,16,256]{2,1,0:T(8,128)S(1)}, f32[16,16,256]{2,1,0:T(8,128)S(1)}, u32[]{:S(2)}, u32[]{:S(2)}) collective-permute-start(f32[16,16,256]{2,1,0:T(8,128)S(1)} %add.115), channel_id=1, source_target_pairs={{0,8},{4,12},{8,0},{12,4},{16,24},{20,28},{24,16},{28,20},{1,9},{5... | collective-permute-start | bytes 786440 | tf_op jit(solution)/shard_map/ppermute | solution.py:151
  111.9 20.0 %collective-permute-start.43 = (f32[16,16,256]{2,1,0:T(8,128)S(1)}, f32[16,16,256]{2,1,0:T(8,128)S(1)}, u32[]{:S(2)}, u32[]{:S(2)}) collective-permute-start(f32[16,16,256]{2,1,0:T(8,128)S(1)} %add_add_fusion.1), channel_id=1, source_target_pairs={{0,16},{4,20},{8,24},{12,28},{16,0},{20,4},{24,8},{28,12},{1,17},{... | collective-permute-start | bytes 786440 | tf_op jit(solution)/shard_map/ppermute | solution.py:151
  121.2 15.3 %collective-permute-start.14 = (f32[16,16,256]{2,1,0:T(8,128)S(1)}, f32[16,16,256]{2,1,0:T(8,128)S(1)}, u32[]{:S(2)}, u32[]{:S(2)}) collective-permute-start(f32[16,16,256]{2,1,0:T(8,128)S(1)} %add_add_fusion.4), channel_id=1, source_target_pairs={{0,16},{4,20},{8,24},{12,28},{16,0},{20,4},{24,8},{28,12},{1,17},{... | collective-permute-start | bytes 786440 | tf_op jit(solution)/shard_map/ppermute | solution.py:151
  131.9 10.2 %collective-permute-start.44 = (f32[16,16,256]{2,1,0:T(8,128)S(1)}, f32[16,16,256]{2,1,0:T(8,128)S(1)}, u32[]{:S(2)}, u32[]{:S(2)}) collective-permute-start(f32[16,16,256]{2,1,0:T(8,128)S(1)} %add.133.refs_8_), channel_id=1, source_target_pairs={{0,8},{4,12},{8,0},{12,4},{16,24},{20,28},{24,16},{28,20},{1,9},{5... | collective-permute-start | bytes 786440 | tf_op jit(solution)/shard_map/ppermute | solution.py:151
  136.5 11.1 %collective-permute-start.15 = (f32[16,16,256]{2,1,0:T(8,128)S(1)}, f32[16,16,256]{2,1,0:T(8,128)S(1)}, u32[]{:S(2)}, u32[]{:S(2)}) collective-permute-start(f32[16,16,256]{2,1,0:T(8,128)S(1)} %add.117.refs_8_), channel_id=1, source_target_pairs={{0,8},{4,12},{8,0},{12,4},{16,24},{20,28},{24,16},{28,20},{1,9},{5... | collective-permute-start | bytes 786440 | tf_op jit(solution)/shard_map/ppermute | solution.py:151
  137.2 10.5 %collective-permute-start.45 = (f32[16,16,256]{2,1,0:T(8,128)S(1)}, f32[16,16,256]{2,1,0:T(8,128)S(1)}, u32[]{:S(2)}, u32[]{:S(2)}) collective-permute-start(f32[16,16,256]{2,1,0:T(8,128)S(1)} %add.133.refs_8_), channel_id=1, source_target_pairs={{0,4},{4,0},{8,12},{12,8},{16,20},{20,16},{24,28},{28,24},{1,5},{5... | collective-permute-start | bytes 786440 | tf_op jit(solution)/shard_map/ppermute | solution.py:151
  142.1 16.3 %collective-permute-start.16 = (f32[16,16,256]{2,1,0:T(8,128)S(1)}, f32[16,16,256]{2,1,0:T(8,128)S(1)}, u32[]{:S(2)}, u32[]{:S(2)}) collective-permute-start(f32[16,16,256]{2,1,0:T(8,128)S(1)} %add.117.refs_8_), channel_id=1, source_target_pairs={{0,4},{4,0},{8,12},{12,8},{16,20},{20,16},{24,28},{28,24},{1,5},{5... | collective-permute-start | bytes 786440 | tf_op jit(solution)/shard_map/ppermute | solution.py:151
  147.6 10.8 %collective-permute-start.17 = (f32[16,16,256]{2,1,0:T(8,128)S(1)}, f32[16,16,256]{2,1,0:T(8,128)S(1)}, u32[]{:S(2)}, u32[]{:S(2)}) collective-permute-start(f32[16,16,256]{2,1,0:T(8,128)S(1)} %collective-permute-done.15.refs_9_), channel_id=1, source_target_pairs={{0,4},{4,0},{8,12},{12,8},{16,20},{20,16},{24,28},{28,24},{1,5},{5... | collective-permute-start | bytes 786440 | tf_op jit(solution)/shard_map/ppermute | solution.py:151
  165.1 10.2 %collective-permute-start.52 = (f32[16,16,256]{2,1,0:T(8,128)S(1)}, f32[16,16,256]{2,1,0:T(8,128)S(1)}, u32[]{:S(2)}, u32[]{:S(2)}) collective-permute-start(f32[16,16,256]{2,1,0:T(8,128)S(1)} %get-tuple-element.89), channel_id=1, source_target_pairs={{0,4},{4,0},{8,12},{12,8},{16,20},{20,16},{24,28},{28,24},{1,5},{5... | collective-permute-start | bytes 786440 | tf_op jit(solution)/shard_map/ppermute | solution.py:151
  175.4 11.2 %collective-permute-start.22 = (f32[16,16,256]{2,1,0:T(8,128)S(1)}, f32[16,16,256]{2,1,0:T(8,128)S(1)}, u32[]{:S(2)}, u32[]{:S(2)}) collective-permute-start(f32[16,16,256]{2,1,0:T(8,128)S(1)} %get-tuple-element.67), channel_id=1, source_target_pairs={{0,4},{4,0},{8,12},{12,8},{16,20},{20,16},{24,28},{28,24},{1,5},{5... | collective-permute-start | bytes 786440 | tf_op jit(solution)/shard_map/ppermute | solution.py:151
  176.3 17.5 %collective-permute-start.24 = (f32[16,16,256]{2,1,0:T(8,128)S(1)}, f32[16,16,256]{2,1,0:T(8,128)S(1)}, u32[]{:S(2)}, u32[]{:S(2)}) collective-permute-start(f32[16,16,256]{2,1,0:T(8,128)S(1)} %add.121), channel_id=1, source_target_pairs={{0,8},{4,12},{8,0},{12,4},{16,24},{20,28},{24,16},{28,20},{1,9},{5... | collective-permute-start | bytes 786440 | tf_op jit(solution)/shard_map/ppermute | solution.py:151
  184.6 20.0 %collective-permute-start.54 = (f32[16,16,256]{2,1,0:T(8,128)S(1)}, f32[16,16,256]{2,1,0:T(8,128)S(1)}, u32[]{:S(2)}, u32[]{:S(2)}) collective-permute-start(f32[16,16,256]{2,1,0:T(8,128)S(1)} %add_add_fusion), channel_id=1, source_target_pairs={{0,16},{4,20},{8,24},{12,28},{16,0},{20,4},{24,8},{28,12},{1,17},{... | collective-permute-start | bytes 786440 | tf_op jit(solution)/shard_map/ppermute | solution.py:151
  193.9 15.3 %collective-permute-start.25 = (f32[16,16,256]{2,1,0:T(8,128)S(1)}, f32[16,16,256]{2,1,0:T(8,128)S(1)}, u32[]{:S(2)}, u32[]{:S(2)}) collective-permute-start(f32[16,16,256]{2,1,0:T(8,128)S(1)} %add_add_fusion.3), channel_id=1, source_target_pairs={{0,16},{4,20},{8,24},{12,28},{16,0},{20,4},{24,8},{28,12},{1,17},{... | collective-permute-start | bytes 786440 | tf_op jit(solution)/shard_map/ppermute | solution.py:151
  204.6 10.2 %collective-permute-start.55 = (f32[16,16,256]{2,1,0:T(8,128)S(1)}, f32[16,16,256]{2,1,0:T(8,128)S(1)}, u32[]{:S(2)}, u32[]{:S(2)}) collective-permute-start(f32[16,16,256]{2,1,0:T(8,128)S(1)} %add.139.refs_8_), channel_id=1, source_target_pairs={{0,8},{4,12},{8,0},{12,4},{16,24},{20,28},{24,16},{28,20},{1,9},{5... | collective-permute-start | bytes 786440 | tf_op jit(solution)/shard_map/ppermute | solution.py:151
  209.2 11.1 %collective-permute-start.26 = (f32[16,16,256]{2,1,0:T(8,128)S(1)}, f32[16,16,256]{2,1,0:T(8,128)S(1)}, u32[]{:S(2)}, u32[]{:S(2)}) collective-permute-start(f32[16,16,256]{2,1,0:T(8,128)S(1)} %add.123.refs_8_), channel_id=1, source_target_pairs={{0,8},{4,12},{8,0},{12,4},{16,24},{20,28},{24,16},{28,20},{1,9},{5... | collective-permute-start | bytes 786440 | tf_op jit(solution)/shard_map/ppermute | solution.py:151
  209.8 10.5 %collective-permute-start.56 = (f32[16,16,256]{2,1,0:T(8,128)S(1)}, f32[16,16,256]{2,1,0:T(8,128)S(1)}, u32[]{:S(2)}, u32[]{:S(2)}) collective-permute-start(f32[16,16,256]{2,1,0:T(8,128)S(1)} %add.139.refs_8_), channel_id=1, source_target_pairs={{0,4},{4,0},{8,12},{12,8},{16,20},{20,16},{24,28},{28,24},{1,5},{5... | collective-permute-start | bytes 786440 | tf_op jit(solution)/shard_map/ppermute | solution.py:151
  214.7 10.9 %collective-permute-start.27 = (f32[16,16,256]{2,1,0:T(8,128)S(1)}, f32[16,16,256]{2,1,0:T(8,128)S(1)}, u32[]{:S(2)}, u32[]{:S(2)}) collective-permute-start(f32[16,16,256]{2,1,0:T(8,128)S(1)} %add.123.refs_8_), channel_id=1, source_target_pairs={{0,4},{4,0},{8,12},{12,8},{16,20},{20,16},{24,28},{28,24},{1,5},{5... | collective-permute-start | bytes 786440 | tf_op jit(solution)/shard_map/ppermute | solution.py:151
  (58 other events, 429.0 us)

commit v2 on v1

v2 whole, which is shorter than its diff:
```python
import functools

import jax
import jax.numpy as jnp
from jax import lax
from jax.experimental import pallas as pl
from jax.experimental.pallas import tpu as pltpu
from jax.sharding import PartitionSpec as P

ITERS = 3
GROUPS = 2
VMEM_LIMIT = 24 << 20
LAG = 10.0
TIE = True


def row_block(rows, width, group):
    return pl.BlockSpec((rows, width), lambda i: (group, 0))


def whole(shape):
    return pl.BlockSpec(shape, lambda i: (0,) * len(shape))


def scalars():
    return pl.BlockSpec(memory_space=pltpu.SMEM)


def dual_kernel(first, n_tiles, tile_rows, tile_cols, width, *refs):
    if first:
        (meta_ref, tiles_ref, y_ref,
         dual_ref, q0, q1, q2, q3, low, prods, acc) = refs
    else:
        (meta_ref, tiles_ref, y_ref, demand_ref, sigma_ref,
         l_ref, l2_ref, r_ref, r2_ref,
         dual_ref, q0, q1, q2, q3, low, prods, acc) = refs
    scen = y_ref.shape[0]
    count = meta_ref[3, 0]
    lane = lax.broadcasted_iota(jnp.int32, (scen, width), 1)
    half = tile_rows // 2
    if not first:
        sigma = sigma_ref[...]
    for j in range(tile_rows):
        at = pl.ds(j * width, width)
        live = (lane < count - j * width).astype(jnp.float32)
        if first:
            dual = y_ref[:, at] * live
        else:
            if j < half:
                kx = l_ref[j] + l2_ref[j]
            else:
                kx = r_ref[j - half] + r2_ref[j - half]
            dual = jnp.maximum(y_ref[:, at] + sigma * (demand_ref[:, at] - kx), 0.0) * live
        dual_ref[:, at] = dual
        low[j] = dual.astype(jnp.bfloat16)
    for t in range(n_tiles):
        prods[t] = jnp.dot(low[meta_ref[0, t]], tiles_ref[t], preferred_element_type=jnp.float32)
    acc[...] = jnp.zeros(acc.shape, jnp.float32)
    quarter = tile_cols // 4
    for t in range(n_tiles):
        acc[meta_ref[2, t]] += prods[t]
    for i, ref in enumerate((q0, q1, q2, q3)):
        ref[...] = acc[pl.ds(i * quarter, quarter)]


def last_dual_kernel(tile_rows, width, meta_ref, y_ref, demand_ref, sigma_ref, l_ref, l2_ref, r_ref, r2_ref, *rest):
    dual_ref = rest[-1]
    scen = y_ref.shape[0]
    count = meta_ref[3, 0]
    lane = lax.broadcasted_iota(jnp.int32, (scen, width), 1)
    half = tile_rows // 2
    sigma = sigma_ref[...]
    for j in range(tile_rows):
        at = pl.ds(j * width, width)
        live = (lane < count - j * width).astype(jnp.float32)
        if j < half:
            kx = l_ref[j] + l2_ref[j]
        else:
            kx = r_ref[j - half] + r2_ref[j - half]
        dual_ref[:, at] = jnp.maximum(y_ref[:, at] + sigma * (demand_ref[:, at] - kx), 0.0) * live


def primal_kernel(n_tiles, tile_rows, tile_cols, width, has_into, *refs):
    (meta_ref, tiles_ref, x_ref, cost_ref, upper_ref, tau_ref,
     k0, k1, k2, k3) = refs[:10]
    refs = refs[10 + has_into:]
    primal_ref, l_ref, r_ref, extra, prods, acc = refs
    scen = x_ref.shape[0]
    place = meta_ref[3, 1]
    quarter = tile_cols // 4
    half = tile_rows // 2
    tau = tau_ref[...]
    for i, ref in enumerate((k0, k1, k2, k3)):
        base = (place ^ i) * quarter
        for j in range(quarter):
            at = pl.ds(pl.multiple_of((base + j) * width, width), width)
            old = x_ref[:, at]
            new = jnp.minimum(
                jnp.maximum(old - tau * (cost_ref[:, at] - ref[j]), 0.0), upper_ref[:, at]
            )
            primal_ref[:, at] = new
            extra[base + j] = (2.0 * new - old).astype(jnp.bfloat16)
    for t in range(n_tiles):
        prods[t] = lax.dot_general(
            extra[meta_ref[1, t]], tiles_ref[t], (((1,), (1,)), ((), ())),
            preferred_element_type=jnp.float32,
        )
    acc[...] = jnp.zeros(acc.shape, jnp.float32)
    for t in range(n_tiles):
        acc[meta_ref[0, t]] += prods[t]
    l_ref[...] = acc[pl.ds(0, half)]
    r_ref[...] = acc[pl.ds(half, half)]


def body(tiles, tile_row, tile_col, row_count, x_start, y_start, cost, upper, demand, tau, sigma,
         *, n_plant, n_col):
    f32 = jnp.float32
    blocks = tiles[0, 0]
    rows = tile_row[0, 0]
    cols = tile_col[0, 0]
    n_tiles, width, _ = blocks.shape
    scenarios, rows_dev = y_start.shape
    col_width = x_start.shape[1]
    tile_rows = rows_dev // width
    tile_cols = col_width // width
    quarter = tile_cols // 4
    half = tile_rows // 2
    m = scenarios // GROUPS
    plant = lax.axis_index("plant")
    place = (plant & 1) * 2 + (plant >> 1) % 2
    slots = ((cols // quarter) ^ place) * quarter + cols % quarter
    lane = lax.iota(jnp.int32, n_tiles)
    info = jnp.where(lane == 0, row_count[0], place)
    meta = jnp.stack([rows, cols, slots, info]).astype(jnp.int32)
    cost_row = cost[None, :]
    upper_row = upper[None, :]
    tau_col = jnp.broadcast_to(tau[:, None], (scenarios, width))
    sigma_col = jnp.broadcast_to(sigma[:, None], (scenarios, width))
    params = pltpu.CompilerParams(vmem_limit_bytes=VMEM_LIMIT)
    quarters = [jax.ShapeDtypeStruct((quarter, m, width), f32)] * 4
    halves = [jax.ShapeDtypeStruct((half, m, width), f32)] * 2
    flops = 2 * n_tiles * m * width * width
    estimate = pl.CostEstimate(flops=10**11, bytes_accessed=10**9, transcendentals=0)

    def swap(value, axis, size, bit):
        return lax.ppermute(value, axis, [(i, i ^ bit) for i in range(size)])

    def y_spec(arr, group):
        return row_block(m, rows_dev, group if arr.shape[0] == scenarios else 0)

    def x_spec(arr, group):
        return row_block(m, col_width, group if arr.shape[0] == scenarios else 0)

    def step_dual(group, dual, parts):
        first = parts is None
        args = [meta, blocks, dual]
        specs = [scalars(), whole(blocks.shape), y_spec(dual, group)]
        if not first:
            args += [demand, sigma_col, *parts]
            specs += [y_spec(demand, group), row_block(m, width, group)] + [whole((half, m, width))] * 4
        return pl.pallas_call(
            functools.partial(dual_kernel, first, n_tiles, tile_rows, tile_cols, width),
            grid=(1,),
            in_specs=specs,
            out_shape=[jax.ShapeDtypeStruct((m, rows_dev), f32)] + quarters,
            out_specs=[whole((m, rows_dev))] + [whole((quarter, m, width))] * 4,
            scratch_shapes=[
                pltpu.VMEM((tile_rows, m, width), jnp.bfloat16),
                pltpu.VMEM((n_tiles, m, width), f32),
                pltpu.VMEM((tile_cols, m, width), f32),
            ],
            compiler_params=params,
            cost_estimate=estimate,
            name="dual_step",
        )(*args)

    def step_primal(group, primal, kty, into, last):
        args = [meta, blocks, primal, cost_row, upper_row, tau_col, *kty]
        specs = [scalars(), whole(blocks.shape), x_spec(primal, group),
                 whole((1, col_width)), whole((1, col_width)), row_block(m, width, group)]
        specs += [whole((quarter, m, width))] * 4
        aliases = {}
        if into is not None:
            aliases = {len(args): 0}
            args.append(into)
            specs.append(pl.BlockSpec(memory_space=pl.ANY))
        out = jax.ShapeDtypeStruct((scenarios if last else m, col_width), f32)
        return pl.pallas_call(
            functools.partial(primal_kernel, n_tiles, tile_rows, tile_cols, width, int(into is not None)),
            grid=(1,),
            in_specs=specs,
            out_shape=[out] + halves,
            out_specs=[row_block(m, col_width, group if last else 0)] + [whole((half, m, width))] * 2,
            scratch_shapes=[
                pltpu.VMEM((tile_cols, m, width), jnp.bfloat16),
                pltpu.VMEM((n_tiles, m, width), f32),
                pltpu.VMEM((tile_rows, m, width), f32),
            ],
            input_output_aliases=aliases,
            compiler_params=params,
            cost_estimate=estimate,
            name="primal_step",
        )(*args)

    def finish_dual(group, dual, parts, into):
        args = [meta, dual, demand, sigma_col, *parts]
        specs = [scalars(), y_spec(dual, group), y_spec(demand, group), row_block(m, width, group)]
        specs += [whole((half, m, width))] * 4
        aliases = {}
        if into is not None:
            aliases = {len(args): 0}
            args.append(into)
            specs.append(pl.BlockSpec(memory_space=pl.ANY))
        return pl.pallas_call(
            functools.partial(last_dual_kernel, tile_rows, width),
            grid=(1,),
            in_specs=specs,
            out_shape=jax.ShapeDtypeStruct((scenarios, rows_dev), f32),
            out_specs=row_block(m, rows_dev, group),
            input_output_aliases=aliases,
            compiler_params=params,
            name="dual_end",
        )(*args)

    final = {"primal": None, "dual": None}

    def run(group):
        dual, primal, parts = y_start, x_start, None
        for iteration in range(ITERS):
            last = iteration == ITERS - 1
            dual, q0, q1, q2, q3 = step_dual(group, dual, parts)
            g1 = swap(q3, "plant", n_plant, 1)
            g0 = swap(q2, "plant", n_plant, 1)
            q1, g1 = yield q1, g1
            q1 = swap(q1 + g1, "plant", n_plant, 2)
            q0, g0, q1 = yield q0, g0, q1
            own = q0 + g0 + q1
            bit = 4
            while bit < n_plant:
                near = swap(own, "plant", n_plant, bit)
                bit *= 2
                own, near = yield own, near
                own = own + near
            pair = swap(own, "plant", n_plant, 2)
            other = swap(own, "plant", n_plant, 1)
            own, pair = yield own, pair
            across = swap(pair, "plant", n_plant, 1)
            own, pair, other, across = yield own, pair, other, across
            kty = (own, pair, other, across)
            into = final["primal"] if last else None
            primal, l, r = step_primal(group, primal, kty, into, last)
            if last:
                final["primal"] = primal
            for a, b in zip(bits, turned):
                l2, r2 = swap(l, "col", n_col, a), swap(r, "col", n_col, b)
                l, l2, r, r2 = yield l, l2, r, r2
                if a != bits[-1]:
                    l, r = l + l2, r + r2
            parts = (l, l2, r, r2)
        final["dual"] = finish_dual(group, dual, parts, final["dual"])

    bits = []
    bit = 1
    while bit < n_col:
        bits.append(bit)
        bit *= 2
    turned = bits[len(bits) // 2:] + bits[:len(bits) // 2]
    runs = [run(g) for g in range(GROUPS)]
    held = [next(r) for r in runs]
    token = None
    for g in order(GROUPS, n_plant, n_col):
        values = held[g]
        if TIE:
            if token is not None:
                *values, token = lax.optimization_barrier((*values, token))
            else:
                token = values[0]
                values = list(values)
        try:
            held[g] = runs[g].send(tuple(values))
            if TIE:
                token, _ = lax.optimization_barrier((token, held[g][0]))
        except StopIteration:
            pass
    return final["primal"], final["dual"]


def order(groups, n_plant, n_col):
    mids = max(n_plant.bit_length() - 3, 0)
    lengths = [4.0, 9.5] + [15.0] * mids + [8.0, 2.0] + [8.0] * (n_col.bit_length() - 1)
    events = []
    for g in range(groups):
        at = LAG * g
        for i in range(ITERS):
            for j, length in enumerate(lengths):
                at += length
                events.append((at, g))
    return [g for _, g in sorted(events)]


def solution(mesh):
    placed = (
        P("plant", "col", None, None, None),
        P("plant", "col", None),
        P("plant", "col", None),
        P("plant"),
        P(None, "col"),
        P(None, "plant"),
        P("col"),
        P("col"),
        P(None, "plant"),
        P(),
        P(),
    )
    return jax.shard_map(
        functools.partial(body, n_plant=mesh.shape["plant"], n_col=mesh.shape["col"]),
        mesh=mesh,
        in_specs=placed,
        out_specs=(P(None, "col"), P(None, "plant")),
        check_vma=False,
    )
```

time: 243 us -> 213 us (0.88)
  local copies, waits for them, and re-layouts: 19 us -> 4 us
  waiting for transfers between devices: 137 us -> 128 us
  starting transfers between devices: 49.9 us -> 46.9 us
  Pallas kernels: 32.5 us -> 30 us
    unnamed x48 -> x16, local copies, waits for them, and re-layouts: 17.6 us -> 3.86 us
    ppermute x66, waiting for transfers between devices: 137 us -> 128 us  [swap(): return lax.ppermute(value, axis, [(i, i ^ bit) for i in range(size)])]
    ppermute x66, starting transfers between devices: 49.9 us -> 46.9 us  [swap(): return lax.ppermute(value, axis, [(i, i ^ bit) for i in range(size)])]
  transfers between devices with their start and end apart: 66 -> 66, of which waited for: 32 -> 37; matrix products, arithmetic and copies ran while one was open for 2% -> 1% of each run, Pallas kernels for 12% -> 11%
where the time goes in v2:
time: 213 us
  waiting for transfers between devices  128 us (60%)
  starting transfers between devices  46.9 us (22%)
  Pallas kernels  30 us (14%)
  local copies, waits for them, and re-layouts  4 us (2%)
  other arithmetic  2.36 us (1%)
    ppermute x66, waiting for transfers between devices, swap(): return lax.ppermute(value, axis, [(i, i ^ bit) for i in range(size)])  128 us
    ppermute x66, starting transfers between devices, swap(): return lax.ppermute(value, axis, [(i, i ^ bit) for i in range(size)])  46.9 us
    pallas_call x6, Pallas kernels, step_primal(): pl.pallas_call(functools.partial(primal_kernel, n_tiles, tile_rows, tile_...  17.2 us
    pallas_call x6, Pallas kernels, step_dual(): pl.pallas_call(functools.partial(dual_kernel, first, n_tiles, tile_rows,...  10.1 us
  transfers between devices with their start and end apart: 66, of which 37 were waited for; matrix products, arithmetic and copies ran while one was open for 1% of the time, Pallas kernels for 11%

profile of v2, /device:TPU:0, one launch (start us, length us, event | category | flops | bytes accessed | tf_op | source)
XLA Modules:
  0.0 212.8 jit_solution(5151630067199489907)
XLA Ops:
  2.6 2.8 %copy-done.1 = bf16[1,1,48,256,256]{4,3,2,1,0:T(8,128)(2,1)S(1)} copy-done((bf16[1,1,48,256,256]{4,3,2,1,0:T(8,128)(2,1)S(1)}, bf16[1,1,48,256,256]{4,3,2,1,0:T(8,128)(2,1)}, u32[]{:S(2)}) %copy-start.1) | copy-done | bytes 6291480
  9.8 3.0 %collective-permute-start.4 = (f32[16,16,256]{2,1,0:T(8,128)S(1)}, f32[16,16,256]{2,1,0:T(8,128)S(1)}, u32[]{:S(2)}, u32[]{:S(2)}) collective-permute-start(f32[16,16,256]{2,1,0:T(8,128)S(1)} %add.150), channel_id=1, source_target_pairs={{0,8},{4,12},{8,0},{12,4},{16,24},{20,28},{24,16},{28,20},{1,9},{5... | collective-permute-start | bytes 786440 | tf_op jit(solution)/shard_map/ppermute | solution.py:146
  15.1 4.3 %collective-permute-done.4 = f32[16,16,256]{2,1,0:T(8,128)S(1)} collective-permute-done((f32[16,16,256]{2,1,0:T(8,128)S(1)}, f32[16,16,256]{2,1,0:T(8,128)S(1)}, u32[]{:S(2)}, u32[]{:S(2)}) %collective-permute-start.4) | collective-permute-done | bytes 262176 | tf_op jit(solution)/shard_map/ppermute | solution.py:146
  21.4 2.6 %collective-permute-start.7 = (f32[16,16,256]{2,1,0:T(8,128)S(1)}, f32[16,16,256]{2,1,0:T(8,128)S(1)}, u32[]{:S(2)}, u32[]{:S(2)}) collective-permute-start(f32[16,16,256]{2,1,0:T(8,128)S(1)} %add_add_fusion.5), channel_id=1, source_target_pairs={{0,16},{4,20},{8,24},{12,28},{16,0},{20,4},{24,8},{28,12},{1,17},{... | collective-permute-start | bytes 786440 | tf_op jit(solution)/shard_map/ppermute | solution.py:146
  24.0 9.0 %collective-permute-done.5 = f32[16,16,256]{2,1,0:T(8,128)S(1)} collective-permute-done((f32[16,16,256]{2,1,0:T(8,128)S(1)}, f32[16,16,256]{2,1,0:T(8,128)S(1)}, u32[]{:S(2)}, u32[]{:S(2)}) %collective-permute-start.5) | collective-permute-done | bytes 262176 | tf_op jit(solution)/shard_map/ppermute | solution.py:146
  33.0 2.3 %collective-permute-done.7 = f32[16,16,256]{2,1,0:T(8,128)S(1)} collective-permute-done((f32[16,16,256]{2,1,0:T(8,128)S(1)}, f32[16,16,256]{2,1,0:T(8,128)S(1)}, u32[]{:S(2)}, u32[]{:S(2)}) %collective-permute-start.7) | collective-permute-done | bytes 262176 | tf_op jit(solution)/shard_map/ppermute | solution.py:146
  35.7 6.0 %collective-permute-done.8.refs_7_ = f32[16,16,256]{2,1,0:T(8,128)S(1)} collective-permute-done((f32[16,16,256]{2,1,0:T(8,128)S(1)}, f32[16,16,256]{2,1,0:T(8,128)S(1)}, u32[]{:S(2)}, u32[]{:S(2)}) %collective-permute-start.8) | collective-permute-done | bytes 262176 | tf_op jit(solution)/shard_map/ppermute | solution.py:146
  43.4 2.6 %primal_step.6 = (f32[16,16384]{1,0:T(8,128)S(1)}, f32[8,16,256]{2,1,0:T(8,128)S(1)}, f32[8,16,256]{2,1,0:T(8,128)S(1)}) custom-call(s32[4,48]{1,0:T(4,128)S(1)} %pad_add_fusion.refs_0_.meta_ref, bf16[48,256,256]{2,1,0:T(8,128)(2,1)S(1)} %bitcast.10, f32[32,16384]{1,0:T(8,128)S(1)} %copy-done.2, f32[1,16384]{1,0:T(1,128)S(1)} %bitcast.20, ...), custom_call_target="tpu_custom_call" | custom-call | flops 99999997952 | bytes 1000000000 | tf_op jit(solution)/shard_map/primal_step/pallas_call | solution.py:188
  49.1 7.9 %collective-permute-done.6 = f32[16,16,256]{2,1,0:T(8,128)S(1)} collective-permute-done((f32[16,16,256]{2,1,0:T(8,128)S(1)}, f32[16,16,256]{2,1,0:T(8,128)S(1)}, u32[]{:S(2)}, u32[]{:S(2)}) %collective-permute-start.6) | collective-permute-done | bytes 262176 | tf_op jit(solution)/shard_map/ppermute | solution.py:146
  60.2 2.4 %collective-permute-done.19.refs_8_ = f32[8,16,256]{2,1,0:T(8,128)S(1)} collective-permute-done((f32[8,16,256]{2,1,0:T(8,128)S(1)}, f32[8,16,256]{2,1,0:T(8,128)S(1)}, u32[]{:S(2)}, u32[]{:S(2)}) %collective-permute-start.19) | collective-permute-done | bytes 131104 | tf_op jit(solution)/shard_map/ppermute | solution.py:146
  65.7 3.2 %collective-permute-done.11.refs_7_ = f32[16,16,256]{2,1,0:T(8,128)S(1)} collective-permute-done((f32[16,16,256]{2,1,0:T(8,128)S(1)}, f32[16,16,256]{2,1,0:T(8,128)S(1)}, u32[]{:S(2)}, u32[]{:S(2)}) %collective-permute-start.11) | collective-permute-done | bytes 262176 | tf_op jit(solution)/shard_map/ppermute | solution.py:146
  70.5 2.6 %primal_step.7 = (f32[16,16384]{1,0:T(8,128)S(1)}, f32[8,16,256]{2,1,0:T(8,128)S(1)}, f32[8,16,256]{2,1,0:T(8,128)S(1)}) custom-call(s32[4,48]{1,0:T(4,128)S(1)} %pad_add_fusion.refs_0_.meta_ref, bf16[48,256,256]{2,1,0:T(8,128)(2,1)S(1)} %bitcast.12, f32[32,16384]{1,0:T(8,128)S(1)} %copy-done.2, f32[1,16384]{1,0:T(1,128)S(1)} %bitcast.21, ...), custom_call_target="tpu_custom_call" | custom-call | flops 99999997952 | bytes 1000000000 | tf_op jit(solution)/shard_map/primal_step/pallas_call | solution.py:188
  74.2 4.5 %collective-permute-done.16 = f32[8,16,256]{2,1,0:T(8,128)S(1)} collective-permute-done((f32[8,16,256]{2,1,0:T(8,128)S(1)}, f32[8,16,256]{2,1,0:T(8,128)S(1)}, u32[]{:S(2)}, u32[]{:S(2)}) %collective-permute-start.16) | collective-permute-done | bytes 131104 | tf_op jit(solution)/shard_map/ppermute | solution.py:146
  87.3 6.9 %collective-permute-done.29 = f32[16,16,256]{2,1,0:T(8,128)S(1)} collective-permute-done((f32[16,16,256]{2,1,0:T(8,128)S(1)}, f32[16,16,256]{2,1,0:T(8,128)S(1)}, u32[]{:S(2)}, u32[]{:S(2)}) %collective-permute-start.29) | collective-permute-done | bytes 262176 | tf_op jit(solution)/shard_map/ppermute | solution.py:146
  94.5 2.0 collective-permute-start.27
  96.7 6.8 %collective-permute-done.30.refs_7_ = f32[16,16,256]{2,1,0:T(8,128)S(1)} collective-permute-done((f32[16,16,256]{2,1,0:T(8,128)S(1)}, f32[16,16,256]{2,1,0:T(8,128)S(1)}, u32[]{:S(2)}, u32[]{:S(2)}) %collective-permute-start.30) | collective-permute-done | bytes 262176 | tf_op jit(solution)/shard_map/ppermute | solution.py:146
  103.5 4.7 %collective-permute-done.27 = f32[16,16,256]{2,1,0:T(8,128)S(1)} collective-permute-done((f32[16,16,256]{2,1,0:T(8,128)S(1)}, f32[16,16,256]{2,1,0:T(8,128)S(1)}, u32[]{:S(2)}, u32[]{:S(2)}) %collective-permute-start.27) | collective-permute-done | bytes 262176 | tf_op jit(solution)/shard_map/ppermute | solution.py:146
  109.1 2.6 %primal_step.8 = (f32[16,16384]{1,0:T(8,128)S(1)}, f32[8,16,256]{2,1,0:T(8,128)S(1)}, f32[8,16,256]{2,1,0:T(8,128)S(1)}) custom-call(s32[4,48]{1,0:T(4,128)S(1)} %pad_add_fusion.refs_0_.meta_ref, bf16[48,256,256]{2,1,0:T(8,128)(2,1)S(1)} %bitcast.14, f32[16,16384]{1,0:T(8,128)S(1)} %get-tuple-element.344.refs_2_, f32[1,16384]{1,0:T(1,128)S(1)} %bitcast.22, ...), custom_call_target="tpu_custom_call" | custom-call | flops 99999997952 | bytes 1000000000 | tf_op jit(solution)/shard_map/primal_step/pallas_call | solution.py:188
  113.8 8.4 %collective-permute-done.28 = f32[16,16,256]{2,1,0:T(8,128)S(1)} collective-permute-done((f32[16,16,256]{2,1,0:T(8,128)S(1)}, f32[16,16,256]{2,1,0:T(8,128)S(1)}, u32[]{:S(2)}, u32[]{:S(2)}) %collective-permute-start.28) | collective-permute-done | bytes 262176 | tf_op jit(solution)/shard_map/ppermute | solution.py:146
  124.6 3.2 %collective-permute-done.40.refs_6_ = f32[8,16,256]{2,1,0:T(8,128)S(1)} collective-permute-done((f32[8,16,256]{2,1,0:T(8,128)S(1)}, f32[8,16,256]{2,1,0:T(8,128)S(1)}, u32[]{:S(2)}, u32[]{:S(2)}) %collective-permute-start.40) | collective-permute-done | bytes 131104 | tf_op jit(solution)/shard_map/ppermute | solution.py:146
  130.5 1.9 dual_step.10
  132.4 2.6 %primal_step.9 = (f32[16,16384]{1,0:T(8,128)S(1)}, f32[8,16,256]{2,1,0:T(8,128)S(1)}, f32[8,16,256]{2,1,0:T(8,128)S(1)}) custom-call(s32[4,48]{1,0:T(4,128)S(1)} %pad_add_fusion.refs_0_.meta_ref, bf16[48,256,256]{2,1,0:T(8,128)(2,1)S(1)} %bitcast.16, f32[16,16384]{1,0:T(8,128)S(1)} %get-tuple-element.282.refs_2_, f32[1,16384]{1,0:T(1,128)S(1)} %bitcast.23, ...), custom_call_target="tpu_custom_call" | custom-call | flops 99999997952 | bytes 1000000000 | tf_op jit(solution)/shard_map/primal_step/pallas_call | solution.py:188
  137.1 3.8 %collective-permute-done.38 = f32[8,16,256]{2,1,0:T(8,128)S(1)} collective-permute-done((f32[8,16,256]{2,1,0:T(8,128)S(1)}, f32[8,16,256]{2,1,0:T(8,128)S(1)}, u32[]{:S(2)}, u32[]{:S(2)}) %collective-permute-start.38) | collective-permute-done | bytes 131104 | tf_op jit(solution)/shard_map/ppermute | solution.py:146
  149.6 3.6 %collective-permute-done.53 = f32[16,16,256]{2,1,0:T(8,128)S(1)} collective-permute-done((f32[16,16,256]{2,1,0:T(8,128)S(1)}, f32[16,16,256]{2,1,0:T(8,128)S(1)}, u32[]{:S(2)}, u32[]{:S(2)}) %collective-permute-start.53) | collective-permute-done | bytes 262176 | tf_op jit(solution)/shard_map/ppermute | solution.py:146
  156.0 11.7 %collective-permute-done.54 = f32[16,16,256]{2,1,0:T(8,128)S(1)} collective-permute-done((f32[16,16,256]{2,1,0:T(8,128)S(1)}, f32[16,16,256]{2,1,0:T(8,128)S(1)}, u32[]{:S(2)}, u32[]{:S(2)}) %collective-permute-start.54) | collective-permute-done | bytes 262176 | tf_op jit(solution)/shard_map/ppermute | solution.py:146
  168.6 1.8 collective-permute-start.47
  170.4 9.8 %collective-permute-done.55.refs_7_ = f32[16,16,256]{2,1,0:T(8,128)S(1)} collective-permute-done((f32[16,16,256]{2,1,0:T(8,128)S(1)}, f32[16,16,256]{2,1,0:T(8,128)S(1)}, u32[]{:S(2)}, u32[]{:S(2)}) %collective-permute-start.55) | collective-permute-done | bytes 262176 | tf_op jit(solution)/shard_map/ppermute | solution.py:146
  180.2 2.9 %collective-permute-done.47 = f32[16,16,256]{2,1,0:T(8,128)S(1)} collective-permute-done((f32[16,16,256]{2,1,0:T(8,128)S(1)}, f32[16,16,256]{2,1,0:T(8,128)S(1)}, u32[]{:S(2)}, u32[]{:S(2)}) %collective-permute-start.47) | collective-permute-done | bytes 262176 | tf_op jit(solution)/shard_map/ppermute | solution.py:146
  183.4 7.0 %collective-permute-done.48.refs_7_ = f32[16,16,256]{2,1,0:T(8,128)S(1)} collective-permute-done((f32[16,16,256]{2,1,0:T(8,128)S(1)}, f32[16,16,256]{2,1,0:T(8,128)S(1)}, u32[]{:S(2)}, u32[]{:S(2)}) %collective-permute-start.48) | collective-permute-done | bytes 262176 | tf_op jit(solution)/shard_map/ppermute | solution.py:146
  190.4 3.4 %primal_step.10 = (f32[32,16384]{1,0:T(8,128)}, f32[8,16,256]{2,1,0:T(8,128)S(1)}, f32[8,16,256]{2,1,0:T(8,128)S(1)}) custom-call(s32[4,48]{1,0:T(4,128)S(1)} %pad_add_fusion.refs_0_.meta_ref, bf16[48,256,256]{2,1,0:T(8,128)(2,1)S(1)} %bitcast.18, f32[16,16384]{1,0:T(8,128)S(1)} %get-tuple-element.409.refs_2_, f32[1,16384]{1,0:T(1,128)S(1)} %bitcast.24, ...), custom_call_target="tpu_custom_call" | custom-call | flops 99999997952 | bytes 1000000000 | tf_op jit(solution)/shard_map/primal_step/pallas_call | solution.py:188
  195.0 3.4 %primal_step.11 = (f32[32,16384]{1,0:T(8,128)}, f32[8,16,256]{2,1,0:T(8,128)S(1)}, f32[8,16,256]{2,1,0:T(8,128)S(1)}) custom-call(s32[4,48]{1,0:T(4,128)S(1)} %pad_add_fusion.refs_0_.meta_ref, bf16[48,256,256]{2,1,0:T(8,128)(2,1)S(1)} %bitcast.19, f32[16,16384]{1,0:T(8,128)S(1)} %get-tuple-element.368.refs_2_, ...), custom_call_target="tpu_custom_call", output_to_operand_aliasing={{0}: (10, {})} | custom-call | flops 99999997952 | bytes 1000000000 | tf_op jit(solution)/shard_map/primal_step/pallas_call | solution.py:188
  204.1 2.1 %collective-permute-done.59 = f32[8,16,256]{2,1,0:T(8,128)S(1)} collective-permute-done((f32[8,16,256]{2,1,0:T(8,128)S(1)}, f32[8,16,256]{2,1,0:T(8,128)S(1)}, u32[]{:S(2)}, u32[]{:S(2)}) %collective-permute-start.59) | collective-permute-done | bytes 131104 | tf_op jit(solution)/shard_map/ppermute | solution.py:146
  (164 shorter events, 69.1 us)
Async XLA Ops:
  9.8 9.6 %collective-permute-start.4 = (f32[16,16,256]{2,1,0:T(8,128)S(1)}, f32[16,16,256]{2,1,0:T(8,128)S(1)}, u32[]{:S(2)}, u32[]{:S(2)}) collective-permute-start(f32[16,16,256]{2,1,0:T(8,128)S(1)} %add.150), channel_id=1, source_target_pairs={{0,8},{4,12},{8,0},{12,4},{16,24},{20,28},{24,16},{28,20},{1,9},{5... | collective-permute-start | bytes 786440 | tf_op jit(solution)/shard_map/ppermute | solution.py:146
  14.6 9.3 %collective-permute-start = (f32[16,16,256]{2,1,0:T(8,128)S(1)}, f32[16,16,256]{2,1,0:T(8,128)S(1)}, u32[]{:S(2)}, u32[]{:S(2)}) collective-permute-start(f32[16,16,256]{2,1,0:T(8,128)S(1)} %get-tuple-element.228), channel_id=1, source_target_pairs={{0,4},{4,0},{8,12},{12,8},{16,20},{20,16},{24,28},{28,24},{1,5},{5... | collective-permute-start | bytes 786440 | tf_op jit(solution)/shard_map/ppermute | solution.py:146
  19.6 13.4 %collective-permute-start.5 = (f32[16,16,256]{2,1,0:T(8,128)S(1)}, f32[16,16,256]{2,1,0:T(8,128)S(1)}, u32[]{:S(2)}, u32[]{:S(2)}) collective-permute-start(f32[16,16,256]{2,1,0:T(8,128)S(1)} %add.153), channel_id=1, source_target_pairs={{0,8},{4,12},{8,0},{12,4},{16,24},{20,28},{24,16},{28,20},{1,9},{5... | collective-permute-start | bytes 786440 | tf_op jit(solution)/shard_map/ppermute | solution.py:146
  21.4 13.9 %collective-permute-start.7 = (f32[16,16,256]{2,1,0:T(8,128)S(1)}, f32[16,16,256]{2,1,0:T(8,128)S(1)}, u32[]{:S(2)}, u32[]{:S(2)}) collective-permute-start(f32[16,16,256]{2,1,0:T(8,128)S(1)} %add_add_fusion.5), channel_id=1, source_target_pairs={{0,16},{4,20},{8,24},{12,28},{16,0},{20,4},{24,8},{28,12},{1,17},{... | collective-permute-start | bytes 786440 | tf_op jit(solution)/shard_map/ppermute | solution.py:146
  41.8 15.2 %collective-permute-start.6 = (f32[16,16,256]{2,1,0:T(8,128)S(1)}, f32[16,16,256]{2,1,0:T(8,128)S(1)}, u32[]{:S(2)}, u32[]{:S(2)}) collective-permute-start(f32[16,16,256]{2,1,0:T(8,128)S(1)} %add_add_fusion.4), channel_id=1, source_target_pairs={{0,16},{4,20},{8,24},{12,28},{16,0},{20,4},{24,8},{28,12},{1,17},{... | collective-permute-start | bytes 786440 | tf_op jit(solution)/shard_map/ppermute | solution.py:146
  46.0 11.0 %collective-permute-start.13 = (f32[8,16,256]{2,1,0:T(8,128)S(1)}, f32[8,16,256]{2,1,0:T(8,128)S(1)}, u32[]{:S(2)}, u32[]{:S(2)}) collective-permute-start(f32[8,16,256]{2,1,0:T(8,128)S(1)} %get-tuple-element.286), channel_id=1, source_target_pairs={{0,2},{1,3},{2,0},{3,1},{4,6},{5,7},{6,4},{7,5},{8,10},{9,11},{10,... | collective-permute-start | bytes 393224 | tf_op jit(solution)/shard_map/ppermute | solution.py:146
  47.6 9.4 %collective-permute-start.12 = (f32[8,16,256]{2,1,0:T(8,128)S(1)}, f32[8,16,256]{2,1,0:T(8,128)S(1)}, u32[]{:S(2)}, u32[]{:S(2)}) collective-permute-start(f32[8,16,256]{2,1,0:T(8,128)S(1)} %get-tuple-element.271), channel_id=1, source_target_pairs={{0,1},{1,0},{2,3},{3,2},{4,5},{5,4},{6,7},{7,6},{8,9},{9,8},{10,11... | collective-permute-start | bytes 393224 | tf_op jit(solution)/shard_map/ppermute | solution.py:146
  60.2 9.6 %collective-permute-start.14 = (f32[16,16,256]{2,1,0:T(8,128)S(1)}, f32[16,16,256]{2,1,0:T(8,128)S(1)}, u32[]{:S(2)}, u32[]{:S(2)}) collective-permute-start(f32[16,16,256]{2,1,0:T(8,128)S(1)} %add.157.refs_6_), channel_id=1, source_target_pairs={{0,4},{4,0},{8,12},{12,8},{16,20},{20,16},{24,28},{28,24},{1,5},{5... | collective-permute-start | bytes 786440 | tf_op jit(solution)/shard_map/ppermute | solution.py:146
  60.2 8.7 %collective-permute-start.11 = (f32[16,16,256]{2,1,0:T(8,128)S(1)}, f32[16,16,256]{2,1,0:T(8,128)S(1)}, u32[]{:S(2)}, u32[]{:S(2)}) collective-permute-start(f32[16,16,256]{2,1,0:T(8,128)S(1)} %add.157.refs_6_), channel_id=1, source_target_pairs={{0,8},{4,12},{8,0},{12,4},{16,24},{20,28},{24,16},{28,20},{1,9},{5... | collective-permute-start | bytes 786440 | tf_op jit(solution)/shard_map/ppermute | solution.py:146
  68.9 12.2 %collective-permute-start.25 = (f32[16,16,256]{2,1,0:T(8,128)S(1)}, f32[16,16,256]{2,1,0:T(8,128)S(1)}, u32[]{:S(2)}, u32[]{:S(2)}) collective-permute-start(f32[16,16,256]{2,1,0:T(8,128)S(1)} %get-tuple-element.316), channel_id=1, source_target_pairs={{0,4},{4,0},{8,12},{12,8},{16,20},{20,16},{24,28},{28,24},{1,5},{5... | collective-permute-start | bytes 786440 | tf_op jit(solution)/shard_map/ppermute | solution.py:146
  69.5 11.6 %collective-permute-start.26 = (f32[16,16,256]{2,1,0:T(8,128)S(1)}, f32[16,16,256]{2,1,0:T(8,128)S(1)}, u32[]{:S(2)}, u32[]{:S(2)}) collective-permute-start(f32[16,16,256]{2,1,0:T(8,128)S(1)} %add.162), channel_id=1, source_target_pairs={{0,8},{4,12},{8,0},{12,4},{16,24},{20,28},{24,16},{28,20},{1,9},{5... | collective-permute-start | bytes 786440 | tf_op jit(solution)/shard_map/ppermute | solution.py:146
  81.2 13.1 %collective-permute-start.29 = (f32[16,16,256]{2,1,0:T(8,128)S(1)}, f32[16,16,256]{2,1,0:T(8,128)S(1)}, u32[]{:S(2)}, u32[]{:S(2)}) collective-permute-start(f32[16,16,256]{2,1,0:T(8,128)S(1)} %add_add_fusion.3), channel_id=1, source_target_pairs={{0,16},{4,20},{8,24},{12,28},{16,0},{20,4},{24,8},{28,12},{1,17},{... | collective-permute-start | bytes 786440 | tf_op jit(solution)/shard_map/ppermute | solution.py:146
  87.2 7.2 %collective-permute-start.24 = (f32[16,16,256]{2,1,0:T(8,128)S(1)}, f32[16,16,256]{2,1,0:T(8,128)S(1)}, u32[]{:S(2)}, u32[]{:S(2)}) collective-permute-start(f32[16,16,256]{2,1,0:T(8,128)S(1)} %get-tuple-element.315), channel_id=1, source_target_pairs={{0,4},{4,0},{8,12},{12,8},{16,20},{20,16},{24,28},{28,24},{1,5},{5... | collective-permute-start | bytes 786440 | tf_op jit(solution)/shard_map/ppermute | solution.py:146
  94.3 9.2 %collective-permute-start.30 = (f32[16,16,256]{2,1,0:T(8,128)S(1)}, f32[16,16,256]{2,1,0:T(8,128)S(1)}, u32[]{:S(2)}, u32[]{:S(2)}) collective-permute-start(f32[16,16,256]{2,1,0:T(8,128)S(1)} %add.168.refs_6_), channel_id=1, source_target_pairs={{0,8},{4,12},{8,0},{12,4},{16,24},{20,28},{24,16},{28,20},{1,9},{5... | collective-permute-start | bytes 786440 | tf_op jit(solution)/shard_map/ppermute | solution.py:146
  94.4 9.2 %collective-permute-start.23 = (f32[16,16,256]{2,1,0:T(8,128)S(1)}, f32[16,16,256]{2,1,0:T(8,128)S(1)}, u32[]{:S(2)}, u32[]{:S(2)}) collective-permute-start(f32[16,16,256]{2,1,0:T(8,128)S(1)} %get-tuple-element.313), channel_id=1, source_target_pairs={{0,4},{4,0},{8,12},{12,8},{16,20},{20,16},{24,28},{28,24},{1,5},{5... | collective-permute-start | bytes 786440 | tf_op jit(solution)/shard_map/ppermute | solution.py:146
  94.5 13.7 %collective-permute-start.27 = (f32[16,16,256]{2,1,0:T(8,128)S(1)}, f32[16,16,256]{2,1,0:T(8,128)S(1)}, u32[]{:S(2)}, u32[]{:S(2)}) collective-permute-start(f32[16,16,256]{2,1,0:T(8,128)S(1)} %add.165), channel_id=1, source_target_pairs={{0,8},{4,12},{8,0},{12,4},{16,24},{20,28},{24,16},{28,20},{1,9},{5... | collective-permute-start | bytes 786440 | tf_op jit(solution)/shard_map/ppermute | solution.py:146
  96.5 12.6 %collective-permute-start.31 = (f32[16,16,256]{2,1,0:T(8,128)S(1)}, f32[16,16,256]{2,1,0:T(8,128)S(1)}, u32[]{:S(2)}, u32[]{:S(2)}) collective-permute-start(f32[16,16,256]{2,1,0:T(8,128)S(1)} %add.168.refs_6_), channel_id=1, source_target_pairs={{0,4},{4,0},{8,12},{12,8},{16,20},{20,16},{24,28},{28,24},{1,5},{5... | collective-permute-start | bytes 786440 | tf_op jit(solution)/shard_map/ppermute | solution.py:146
  108.3 14.0 %collective-permute-start.28 = (f32[16,16,256]{2,1,0:T(8,128)S(1)}, f32[16,16,256]{2,1,0:T(8,128)S(1)}, u32[]{:S(2)}, u32[]{:S(2)}) collective-permute-start(f32[16,16,256]{2,1,0:T(8,128)S(1)} %add_add_fusion.2), channel_id=1, source_target_pairs={{0,16},{4,20},{8,24},{12,28},{16,0},{20,4},{24,8},{28,12},{1,17},{... | collective-permute-start | bytes 786440 | tf_op jit(solution)/shard_map/ppermute | solution.py:146
  111.7 10.7 %collective-permute-start.34 = (f32[8,16,256]{2,1,0:T(8,128)S(1)}, f32[8,16,256]{2,1,0:T(8,128)S(1)}, u32[]{:S(2)}, u32[]{:S(2)}) collective-permute-start(f32[8,16,256]{2,1,0:T(8,128)S(1)} %get-tuple-element.357), channel_id=1, source_target_pairs={{0,1},{1,0},{2,3},{3,2},{4,5},{5,4},{6,7},{7,6},{8,9},{9,8},{10,11... | collective-permute-start | bytes 393224 | tf_op jit(solution)/shard_map/ppermute | solution.py:146
  112.3 10.1 %collective-permute-start.35 = (f32[8,16,256]{2,1,0:T(8,128)S(1)}, f32[8,16,256]{2,1,0:T(8,128)S(1)}, u32[]{:S(2)}, u32[]{:S(2)}) collective-permute-start(f32[8,16,256]{2,1,0:T(8,128)S(1)} %get-tuple-element.372), channel_id=1, source_target_pairs={{0,2},{1,3},{2,0},{3,1},{4,6},{5,7},{6,4},{7,5},{8,10},{9,11},{10,... | collective-permute-start | bytes 393224 | tf_op jit(solution)/shard_map/ppermute | solution.py:146
  122.3 8.2 %collective-permute-start.33 = (f32[16,16,256]{2,1,0:T(8,128)S(1)}, f32[16,16,256]{2,1,0:T(8,128)S(1)}, u32[]{:S(2)}, u32[]{:S(2)}) collective-permute-start(f32[16,16,256]{2,1,0:T(8,128)S(1)} %add.169.refs_6_), channel_id=1, source_target_pairs={{0,8},{4,12},{8,0},{12,4},{16,24},{20,28},{24,16},{28,20},{1,9},{5... | collective-permute-start | bytes 786440 | tf_op jit(solution)/shard_map/ppermute | solution.py:146
  124.6 7.8 %collective-permute-start.36 = (f32[16,16,256]{2,1,0:T(8,128)S(1)}, f32[16,16,256]{2,1,0:T(8,128)S(1)}, u32[]{:S(2)}, u32[]{:S(2)}) collective-permute-start(f32[16,16,256]{2,1,0:T(8,128)S(1)} %add.169.refs_6_), channel_id=1, source_target_pairs={{0,4},{4,0},{8,12},{12,8},{16,20},{20,16},{24,28},{28,24},{1,5},{5... | collective-permute-start | bytes 786440 | tf_op jit(solution)/shard_map/ppermute | solution.py:146
  137.1 7.3 %collective-permute-start.52 = (f32[16,16,256]{2,1,0:T(8,128)S(1)}, f32[16,16,256]{2,1,0:T(8,128)S(1)}, u32[]{:S(2)}, u32[]{:S(2)}) collective-permute-start(f32[16,16,256]{2,1,0:T(8,128)S(1)} %get-tuple-element.412), channel_id=1, source_target_pairs={{0,4},{4,0},{8,12},{12,8},{16,20},{20,16},{24,28},{28,24},{1,5},{5... | collective-permute-start | bytes 786440 | tf_op jit(solution)/shard_map/ppermute | solution.py:146
  144.5 8.8 %collective-permute-start.53 = (f32[16,16,256]{2,1,0:T(8,128)S(1)}, f32[16,16,256]{2,1,0:T(8,128)S(1)}, u32[]{:S(2)}, u32[]{:S(2)}) collective-permute-start(f32[16,16,256]{2,1,0:T(8,128)S(1)} %add.178), channel_id=1, source_target_pairs={{0,8},{4,12},{8,0},{12,4},{16,24},{20,28},{24,16},{28,20},{1,9},{5... | collective-permute-start | bytes 786440 | tf_op jit(solution)/shard_map/ppermute | solution.py:146
  153.3 14.3 %collective-permute-start.54 = (f32[16,16,256]{2,1,0:T(8,128)S(1)}, f32[16,16,256]{2,1,0:T(8,128)S(1)}, u32[]{:S(2)}, u32[]{:S(2)}) collective-permute-start(f32[16,16,256]{2,1,0:T(8,128)S(1)} %add_add_fusion), channel_id=1, source_target_pairs={{0,16},{4,20},{8,24},{12,28},{16,0},{20,4},{24,8},{28,12},{1,17},{... | collective-permute-start | bytes 786440 | tf_op jit(solution)/shard_map/ppermute | solution.py:146
  154.1 13.6 %collective-permute-start.44 = (f32[16,16,256]{2,1,0:T(8,128)S(1)}, f32[16,16,256]{2,1,0:T(8,128)S(1)}, u32[]{:S(2)}, u32[]{:S(2)}) collective-permute-start(f32[16,16,256]{2,1,0:T(8,128)S(1)} %get-tuple-element.393), channel_id=1, source_target_pairs={{0,4},{4,0},{8,12},{12,8},{16,20},{20,16},{24,28},{28,24},{1,5},{5... | collective-permute-start | bytes 786440 | tf_op jit(solution)/shard_map/ppermute | solution.py:146
  154.2 14.3 %collective-permute-start.46 = (f32[16,16,256]{2,1,0:T(8,128)S(1)}, f32[16,16,256]{2,1,0:T(8,128)S(1)}, u32[]{:S(2)}, u32[]{:S(2)}) collective-permute-start(f32[16,16,256]{2,1,0:T(8,128)S(1)} %add.174), channel_id=1, source_target_pairs={{0,8},{4,12},{8,0},{12,4},{16,24},{20,28},{24,16},{28,20},{1,9},{5... | collective-permute-start | bytes 786440 | tf_op jit(solution)/shard_map/ppermute | solution.py:146
  167.7 12.5 %collective-permute-start.55 = (f32[16,16,256]{2,1,0:T(8,128)S(1)}, f32[16,16,256]{2,1,0:T(8,128)S(1)}, u32[]{:S(2)}, u32[]{:S(2)}) collective-permute-start(f32[16,16,256]{2,1,0:T(8,128)S(1)} %add.181.refs_6_), channel_id=1, source_target_pairs={{0,8},{4,12},{8,0},{12,4},{16,24},{20,28},{24,16},{28,20},{1,9},{5... | collective-permute-start | bytes 786440 | tf_op jit(solution)/shard_map/ppermute | solution.py:146
  168.6 14.6 %collective-permute-start.47 = (f32[16,16,256]{2,1,0:T(8,128)S(1)}, f32[16,16,256]{2,1,0:T(8,128)S(1)}, u32[]{:S(2)}, u32[]{:S(2)}) collective-permute-start(f32[16,16,256]{2,1,0:T(8,128)S(1)} %add_add_fusion.1), channel_id=1, source_target_pairs={{0,16},{4,20},{8,24},{12,28},{16,0},{20,4},{24,8},{28,12},{1,17},{... | collective-permute-start | bytes 786440 | tf_op jit(solution)/shard_map/ppermute | solution.py:146
  170.4 12.9 %collective-permute-start.56 = (f32[16,16,256]{2,1,0:T(8,128)S(1)}, f32[16,16,256]{2,1,0:T(8,128)S(1)}, u32[]{:S(2)}, u32[]{:S(2)}) collective-permute-start(f32[16,16,256]{2,1,0:T(8,128)S(1)} %add.181.refs_6_), channel_id=1, source_target_pairs={{0,4},{4,0},{8,12},{12,8},{16,20},{20,16},{24,28},{28,24},{1,5},{5... | collective-permute-start | bytes 786440 | tf_op jit(solution)/shard_map/ppermute | solution.py:146
  183.3 11.7 %collective-permute-start.49 = (f32[16,16,256]{2,1,0:T(8,128)S(1)}, f32[16,16,256]{2,1,0:T(8,128)S(1)}, u32[]{:S(2)}, u32[]{:S(2)}) collective-permute-start(f32[16,16,256]{2,1,0:T(8,128)S(1)} %add.177.refs_6_), channel_id=1, source_target_pairs={{0,4},{4,0},{8,12},{12,8},{16,20},{20,16},{24,28},{28,24},{1,5},{5... | collective-permute-start | bytes 786440 | tf_op jit(solution)/shard_map/ppermute | solution.py:146
  193.8 7.5 %collective-permute-start.62 = (f32[8,16,256]{2,1,0:T(8,128)S(1)}, f32[8,16,256]{2,1,0:T(8,128)S(1)}, u32[]{:S(2)}, u32[]{:S(2)}) collective-permute-start(f32[8,16,256]{2,1,0:T(8,128)S(1)} %get-tuple-element.444), channel_id=1, source_target_pairs={{0,1},{1,0},{2,3},{3,2},{4,5},{5,4},{6,7},{7,6},{8,9},{9,8},{10,11... | collective-permute-start | bytes 393224 | tf_op jit(solution)/shard_map/ppermute | solution.py:146
  (42 other events, 332.6 us)

commit v3 on v2

--- a/solution.py
+++ b/solution.py
@@ -10,7 +10,10 @@
 ITERS = 3
 GROUPS = 2
 VMEM_LIMIT = 24 << 20
-LAG = 10.0
+LAG = 19.4
+STEPS = [4.0, 11.1, 15.0, 8.9, 2.0, 8.0, 8.4]
+DUAL_COST = 10**11
+PRIMAL_COST = 10**11
 TIE = True
 
 
@@ -24,6 +27,13 @@
 
 def scalars():
     return pl.BlockSpec(memory_space=pltpu.SMEM)
+
+
+def spread(col, place, quarter):
+    if quarter & (quarter - 1):
+        part = lax.div(col, quarter)
+        return (part ^ place) * quarter + (col - part * quarter)
+    return col ^ (place * quarter)
 
 
 def dual_kernel(first, n_tiles, tile_rows, tile_cols, width, *refs):
@@ -35,7 +45,7 @@
          l_ref, l2_ref, r_ref, r2_ref,
          dual_ref, q0, q1, q2, q3, low, prods, acc) = refs
     scen = y_ref.shape[0]
-    count = meta_ref[3, 0]
+    count, place = meta_ref[2, 0], meta_ref[2, 1]
     lane = lax.broadcasted_iota(jnp.int32, (scen, width), 1)
     half = tile_rows // 2
     if not first:
@@ -58,7 +68,7 @@
     acc[...] = jnp.zeros(acc.shape, jnp.float32)
     quarter = tile_cols // 4
     for t in range(n_tiles):
-        acc[meta_ref[2, t]] += prods[t]
+        acc[spread(meta_ref[1, t], place, quarter)] += prods[t]
     for i, ref in enumerate((q0, q1, q2, q3)):
         ref[...] = acc[pl.ds(i * quarter, quarter)]
 
@@ -66,7 +76,7 @@
 def last_dual_kernel(tile_rows, width, meta_ref, y_ref, demand_ref, sigma_ref, l_ref, l2_ref, r_ref, r2_ref, *rest):
     dual_ref = rest[-1]
     scen = y_ref.shape[0]
-    count = meta_ref[3, 0]
+    count = meta_ref[2, 0]
     lane = lax.broadcasted_iota(jnp.int32, (scen, width), 1)
     half = tile_rows // 2
     sigma = sigma_ref[...]
@@ -80,13 +90,17 @@
         dual_ref[:, at] = jnp.maximum(y_ref[:, at] + sigma * (demand_ref[:, at] - kx), 0.0) * live
 
 
-def primal_kernel(n_tiles, tile_rows, tile_cols, width, has_into, *refs):
+def primal_kernel(n_tiles, tile_rows, tile_cols, width, has_into, out_at, *refs):
     (meta_ref, tiles_ref, x_ref, cost_ref, upper_ref, tau_ref,
      k0, k1, k2, k3) = refs[:10]
     refs = refs[10 + has_into:]
+    if out_at is not None:
+        *refs, new_ref, sem = refs
     primal_ref, l_ref, r_ref, extra, prods, acc = refs
+    if out_at is not None:
+        out_ref, primal_ref = primal_ref, new_ref
     scen = x_ref.shape[0]
-    place = meta_ref[3, 1]
+    place = meta_ref[2, 1]
     quarter = tile_cols // 4
     half = tile_rows // 2
     tau = tau_ref[...]
@@ -100,6 +114,9 @@
             )
             primal_ref[:, at] = new
             extra[base + j] = (2.0 * new - old).astype(jnp.bfloat16)
+    if out_at is not None:
+        out = pltpu.make_async_copy(new_ref, out_ref.at[pl.ds(out_at, scen)], sem)
+        out.start()
     for t in range(n_tiles):
         prods[t] = lax.dot_general(
             extra[meta_ref[1, t]], tiles_ref[t], (((1,), (1,)), ((), ())),
@@ -110,6 +127,8 @@
         acc[meta_ref[0, t]] += prods[t]
     l_ref[...] = acc[pl.ds(0, half)]
     r_ref[...] = acc[pl.ds(half, half)]
+    if out_at is not None:
+        out.wait()
 
 
 def body(tiles, tile_row, tile_col, row_count, x_start, y_start, cost, upper, demand, tau, sigma,
@@ -127,11 +146,9 @@
     half = tile_rows // 2
     m = scenarios // GROUPS
     plant = lax.axis_index("plant")
-    place = (plant & 1) * 2 + (plant >> 1) % 2
-    slots = ((cols // quarter) ^ place) * quarter + cols % quarter
+    place = ((plant & 1) << 1) | ((plant >> 1) & 1)
     lane = lax.iota(jnp.int32, n_tiles)
-    info = jnp.where(lane == 0, row_count[0], place)
-    meta = jnp.stack([rows, cols, slots, info]).astype(jnp.int32)
+    meta = jnp.stack([rows, cols, jnp.where(lane == 0, row_count[0], place)])
     cost_row = cost[None, :]
     upper_row = upper[None, :]
     tau_col = jnp.broadcast_to(tau[:, None], (scenarios, width))
@@ -140,7 +157,8 @@
     quarters = [jax.ShapeDtypeStruct((quarter, m, width), f32)] * 4
     halves = [jax.ShapeDtypeStruct((half, m, width), f32)] * 2
     flops = 2 * n_tiles * m * width * width
-    estimate = pl.CostEstimate(flops=10**11, bytes_accessed=10**9, transcendentals=0)
+    dual_estimate = pl.CostEstimate(flops=DUAL_COST, bytes_accessed=DUAL_COST // 100, transcendentals=0)
+    primal_estimate = pl.CostEstimate(flops=PRIMAL_COST, bytes_accessed=PRIMAL_COST // 100, transcendentals=0)
 
     def swap(value, axis, size, bit):
         return lax.ppermute(value, axis, [(i, i ^ bit) for i in range(size)])
@@ -170,7 +188,7 @@
                 pltpu.VMEM((tile_cols, m, width), f32),
             ],
             compiler_params=params,
-            cost_estimate=estimate,
+            cost_estimate=dual_estimate,
             name="dual_step",
         )(*args)
 
@@ -186,19 +204,21 @@
             specs.append(pl.BlockSpec(memory_space=pl.ANY))
         out = jax.ShapeDtypeStruct((scenarios if last else m, col_width), f32)
         return pl.pallas_call(
-            functools.partial(primal_kernel, n_tiles, tile_rows, tile_cols, width, int(into is not None)),
+            functools.partial(primal_kernel, n_tiles, tile_rows, tile_cols, width, int(into is not None),
+                              group * m if last else None),
             grid=(1,),
             in_specs=specs,
             out_shape=[out] + halves,
-            out_specs=[row_block(m, col_width, group if last else 0)] + [whole((half, m, width))] * 2,
+            out_specs=[pl.BlockSpec(memory_space=pltpu.HBM) if last else whole((m, col_width))]
+            + [whole((half, m, width))] * 2,
             scratch_shapes=[
                 pltpu.VMEM((tile_cols, m, width), jnp.bfloat16),
                 pltpu.VMEM((n_tiles, m, width), f32),
                 pltpu.VMEM((tile_rows, m, width), f32),
-            ],
+            ] + ([pltpu.VMEM((m, col_width), f32), pltpu.SemaphoreType.DMA] if last else []),
             input_output_aliases=aliases,
             compiler_params=params,
-            cost_estimate=estimate,
+            cost_estimate=primal_estimate,
             name="primal_step",
         )(*args)
 
@@ -287,7 +307,7 @@
 
 def order(groups, n_plant, n_col):
     mids = max(n_plant.bit_length() - 3, 0)
-    lengths = [4.0, 9.5] + [15.0] * mids + [8.0, 2.0] + [8.0] * (n_col.bit_length() - 1)
+    lengths = STEPS[:2] + STEPS[2:3] * mids + STEPS[3:5] + STEPS[5:6] * (n_col.bit_length() - 2) + STEPS[6:]
     events = []
     for g in range(groups):
         at = LAG * g

time: 213 us -> 211 us (level)
  waiting for transfers between devices: 128 us -> 111 us
  starting transfers between devices: 46.9 us -> 62.7 us
    ppermute x66, waiting for transfers between devices: 128 us -> 111 us  [swap(): return lax.ppermute(value, axis, [(i, i ^ bit) for i in range(size)])]
    ppermute x66, starting transfers between devices: 46.9 us -> 62.7 us  [swap(): return lax.ppermute(value, axis, [(i, i ^ bit) for i in range(size)])]
  transfers between devices with their start and end apart: 66 -> 66, of which waited for: 37 -> 36; matrix products, arithmetic and copies ran while one was open for 1% -> 1% of each run, Pallas kernels for 11% -> 12%
where the time goes in v3:
time: 211 us
  waiting for transfers between devices  111 us (53%)
  starting transfers between devices  62.7 us (30%)
  Pallas kernels  30.1 us (14%)
  local copies, waits for them, and re-layouts  4 us (2%)
    ppermute x66, waiting for transfers between devices, swap(): return lax.ppermute(value, axis, [(i, i ^ bit) for i in range(size)])  111 us
    ppermute x66, starting transfers between devices, swap(): return lax.ppermute(value, axis, [(i, i ^ bit) for i in range(size)])  62.7 us
    pallas_call x6, Pallas kernels, step_primal(): pl.pallas_call(functools.partial(primal_kernel, n_tiles, tile_rows, tile_...  17.3 us
    pallas_call x6, Pallas kernels, step_dual(): pl.pallas_call(functools.partial(dual_kernel, first, n_tiles, tile_rows,...  10.2 us
  transfers between devices with their start and end apart: 66, of which 36 were waited for; matrix products, arithmetic and copies ran while one was open for 1% of the time, Pallas kernels for 12%

profile of v3, /device:TPU:0, one launch (start us, length us, event | category | flops | bytes accessed | tf_op | source)
XLA Modules:
  0.0 211.1 jit_solution(8999086932938683485)
XLA Ops:
  2.0 2.8 %copy-done.1 = bf16[1,1,48,256,256]{4,3,2,1,0:T(8,128)(2,1)S(1)} copy-done((bf16[1,1,48,256,256]{4,3,2,1,0:T(8,128)(2,1)S(1)}, bf16[1,1,48,256,256]{4,3,2,1,0:T(8,128)(2,1)}, u32[]{:S(2)}) %copy-start.1) | copy-done | bytes 6291480
  9.2 3.0 %collective-permute-start.4 = (f32[16,16,256]{2,1,0:T(8,128)S(1)}, f32[16,16,256]{2,1,0:T(8,128)S(1)}, u32[]{:S(2)}, u32[]{:S(2)}) collective-permute-start(f32[16,16,256]{2,1,0:T(8,128)S(1)} %add.108), channel_id=1, source_target_pairs={{0,8},{4,12},{8,0},{12,4},{16,24},{20,28},{24,16},{28,20},{1,9},{5... | collective-permute-start | bytes 786440 | tf_op jit(solution)/shard_map/ppermute | solution.py:164
  14.0 4.8 %collective-permute-done.4 = f32[16,16,256]{2,1,0:T(8,128)S(1)} collective-permute-done((f32[16,16,256]{2,1,0:T(8,128)S(1)}, f32[16,16,256]{2,1,0:T(8,128)S(1)}, u32[]{:S(2)}, u32[]{:S(2)}) %collective-permute-start.4) | collective-permute-done | bytes 262176 | tf_op jit(solution)/shard_map/ppermute | solution.py:164
  18.8 2.8 %collective-permute-start.6 = (f32[16,16,256]{2,1,0:T(8,128)S(1)}, f32[16,16,256]{2,1,0:T(8,128)S(1)}, u32[]{:S(2)}, u32[]{:S(2)}) collective-permute-start(f32[16,16,256]{2,1,0:T(8,128)S(1)} %add_add_fusion.5), channel_id=1, source_target_pairs={{0,16},{4,20},{8,24},{12,28},{16,0},{20,4},{24,8},{28,12},{1,17},{... | collective-permute-start | bytes 786440 | tf_op jit(solution)/shard_map/ppermute | solution.py:164
  23.4 10.0 %collective-permute-done.6 = f32[16,16,256]{2,1,0:T(8,128)S(1)} collective-permute-done((f32[16,16,256]{2,1,0:T(8,128)S(1)}, f32[16,16,256]{2,1,0:T(8,128)S(1)}, u32[]{:S(2)}, u32[]{:S(2)}) %collective-permute-start.6) | collective-permute-done | bytes 262176 | tf_op jit(solution)/shard_map/ppermute | solution.py:164
  35.2 5.6 %collective-permute-done.8.refs_7_ = f32[16,16,256]{2,1,0:T(8,128)S(1)} collective-permute-done((f32[16,16,256]{2,1,0:T(8,128)S(1)}, f32[16,16,256]{2,1,0:T(8,128)S(1)}, u32[]{:S(2)}, u32[]{:S(2)}) %collective-permute-start.8) | collective-permute-done | bytes 262176 | tf_op jit(solution)/shard_map/ppermute | solution.py:164
  40.8 3.0 %collective-permute-start.7 = (f32[16,16,256]{2,1,0:T(8,128)S(1)}, f32[16,16,256]{2,1,0:T(8,128)S(1)}, u32[]{:S(2)}, u32[]{:S(2)}) collective-permute-start(f32[16,16,256]{2,1,0:T(8,128)S(1)} %add_add_fusion.4), channel_id=1, source_target_pairs={{0,16},{4,20},{8,24},{12,28},{16,0},{20,4},{24,8},{28,12},{1,17},{... | collective-permute-start | bytes 786440 | tf_op jit(solution)/shard_map/ppermute | solution.py:164
  43.9 2.6 %primal_step.6 = (f32[16,16384]{1,0:T(8,128)S(1)}, f32[8,16,256]{2,1,0:T(8,128)S(1)}, f32[8,16,256]{2,1,0:T(8,128)S(1)}) custom-call(s32[3,48]{1,0:T(4,128)S(1)} %pad_add_fusion.refs_0_.meta_ref, bf16[48,256,256]{2,1,0:T(8,128)(2,1)S(1)} %bitcast.9, f32[32,16384]{1,0:T(8,128)S(1)} %copy-done.2, f32[1,16384]{1,0:T(1,128)S(1)} %bitcast.19, ...), custom_call_target="tpu_custom_call" | custom-call | flops 99999997952 | bytes 1000000000 | tf_op jit(solution)/shard_map/primal_step/pallas_call | solution.py:206
  49.6 2.6 %collective-permute-done.12 = f32[8,16,256]{2,1,0:T(8,128)S(1)} collective-permute-done((f32[8,16,256]{2,1,0:T(8,128)S(1)}, f32[8,16,256]{2,1,0:T(8,128)S(1)}, u32[]{:S(2)}, u32[]{:S(2)}) %collective-permute-start.12) | collective-permute-done | bytes 131104 | tf_op jit(solution)/shard_map/ppermute | solution.py:164
  62.5 2.2 %collective-permute-done.13.refs_7_ = f32[16,16,256]{2,1,0:T(8,128)S(1)} collective-permute-done((f32[16,16,256]{2,1,0:T(8,128)S(1)}, f32[16,16,256]{2,1,0:T(8,128)S(1)}, u32[]{:S(2)}, u32[]{:S(2)}) %collective-permute-start.13) | collective-permute-done | bytes 262176 | tf_op jit(solution)/shard_map/ppermute | solution.py:164
  66.2 2.6 %primal_step.7 = (f32[16,16384]{1,0:T(8,128)S(1)}, f32[8,16,256]{2,1,0:T(8,128)S(1)}, f32[8,16,256]{2,1,0:T(8,128)S(1)}) custom-call(s32[3,48]{1,0:T(4,128)S(1)} %pad_add_fusion.refs_0_.meta_ref, bf16[48,256,256]{2,1,0:T(8,128)(2,1)S(1)} %bitcast.11, f32[32,16384]{1,0:T(8,128)S(1)} %copy-done.2, f32[1,16384]{1,0:T(1,128)S(1)} %bitcast.20, ...), custom_call_target="tpu_custom_call" | custom-call | flops 99999997952 | bytes 1000000000 | tf_op jit(solution)/shard_map/primal_step/pallas_call | solution.py:206
  77.9 3.1 %collective-permute-start.28 = (f32[16,16,256]{2,1,0:T(8,128)S(1)}, f32[16,16,256]{2,1,0:T(8,128)S(1)}, u32[]{:S(2)}, u32[]{:S(2)}) collective-permute-start(f32[16,16,256]{2,1,0:T(8,128)S(1)} %add_add_fusion.3), channel_id=1, source_target_pairs={{0,16},{4,20},{8,24},{12,28},{16,0},{20,4},{24,8},{28,12},{1,17},{... | collective-permute-start | bytes 786440 | tf_op jit(solution)/shard_map/ppermute | solution.py:164
  83.0 8.1 %collective-permute-done.28 = f32[16,16,256]{2,1,0:T(8,128)S(1)} collective-permute-done((f32[16,16,256]{2,1,0:T(8,128)S(1)}, f32[16,16,256]{2,1,0:T(8,128)S(1)}, u32[]{:S(2)}, u32[]{:S(2)}) %collective-permute-start.28) | collective-permute-done | bytes 262176 | tf_op jit(solution)/shard_map/ppermute | solution.py:164
  93.7 6.9 %collective-permute-done.30.refs_7_ = f32[16,16,256]{2,1,0:T(8,128)S(1)} collective-permute-done((f32[16,16,256]{2,1,0:T(8,128)S(1)}, f32[16,16,256]{2,1,0:T(8,128)S(1)}, u32[]{:S(2)}, u32[]{:S(2)}) %collective-permute-start.30) | collective-permute-done | bytes 262176 | tf_op jit(solution)/shard_map/ppermute | solution.py:164
  100.5 3.5 %collective-permute-done.27 = f32[16,16,256]{2,1,0:T(8,128)S(1)} collective-permute-done((f32[16,16,256]{2,1,0:T(8,128)S(1)}, f32[16,16,256]{2,1,0:T(8,128)S(1)}, u32[]{:S(2)}, u32[]{:S(2)}) %collective-permute-start.27) | collective-permute-done | bytes 262176 | tf_op jit(solution)/shard_map/ppermute | solution.py:164
  104.1 3.4 %collective-permute-start.29 = (f32[16,16,256]{2,1,0:T(8,128)S(1)}, f32[16,16,256]{2,1,0:T(8,128)S(1)}, u32[]{:S(2)}, u32[]{:S(2)}) collective-permute-start(f32[16,16,256]{2,1,0:T(8,128)S(1)} %add_add_fusion.2), channel_id=1, source_target_pairs={{0,16},{4,20},{8,24},{12,28},{16,0},{20,4},{24,8},{28,12},{1,17},{... | collective-permute-start | bytes 786440 | tf_op jit(solution)/shard_map/ppermute | solution.py:164
  107.6 2.6 %primal_step.8 = (f32[16,16384]{1,0:T(8,128)S(1)}, f32[8,16,256]{2,1,0:T(8,128)S(1)}, f32[8,16,256]{2,1,0:T(8,128)S(1)}) custom-call(s32[3,48]{1,0:T(4,128)S(1)} %pad_add_fusion.refs_0_.meta_ref, bf16[48,256,256]{2,1,0:T(8,128)(2,1)S(1)} %bitcast.13, f32[16,16384]{1,0:T(8,128)S(1)} %get-tuple-element.337.refs_2_, f32[1,16384]{1,0:T(1,128)S(1)} %bitcast.21, ...), custom_call_target="tpu_custom_call" | custom-call | flops 99999997952 | bytes 1000000000 | tf_op jit(solution)/shard_map/primal_step/pallas_call | solution.py:206
  112.2 6.9 %collective-permute-done.29 = f32[16,16,256]{2,1,0:T(8,128)S(1)} collective-permute-done((f32[16,16,256]{2,1,0:T(8,128)S(1)}, f32[16,16,256]{2,1,0:T(8,128)S(1)}, u32[]{:S(2)}, u32[]{:S(2)}) %collective-permute-start.29) | collective-permute-done | bytes 262176 | tf_op jit(solution)/shard_map/ppermute | solution.py:164
  122.1 3.0 %collective-permute-done.36.refs_6_ = f32[8,16,256]{2,1,0:T(8,128)S(1)} collective-permute-done((f32[8,16,256]{2,1,0:T(8,128)S(1)}, f32[8,16,256]{2,1,0:T(8,128)S(1)}, u32[]{:S(2)}, u32[]{:S(2)}) %collective-permute-start.36) | collective-permute-done | bytes 131104 | tf_op jit(solution)/shard_map/ppermute | solution.py:164
  128.5 2.6 %primal_step.9 = (f32[16,16384]{1,0:T(8,128)S(1)}, f32[8,16,256]{2,1,0:T(8,128)S(1)}, f32[8,16,256]{2,1,0:T(8,128)S(1)}) custom-call(s32[3,48]{1,0:T(4,128)S(1)} %pad_add_fusion.refs_0_.meta_ref, bf16[48,256,256]{2,1,0:T(8,128)(2,1)S(1)} %bitcast.15, f32[16,16384]{1,0:T(8,128)S(1)} %get-tuple-element.292.refs_2_, f32[1,16384]{1,0:T(1,128)S(1)} %bitcast.22, ...), custom_call_target="tpu_custom_call" | custom-call | flops 99999997952 | bytes 1000000000 | tf_op jit(solution)/shard_map/primal_step/pallas_call | solution.py:206
  133.2 3.9 %collective-permute-done.40 = f32[8,16,256]{2,1,0:T(8,128)S(1)} collective-permute-done((f32[8,16,256]{2,1,0:T(8,128)S(1)}, f32[8,16,256]{2,1,0:T(8,128)S(1)}, u32[]{:S(2)}, u32[]{:S(2)}) %collective-permute-start.40) | collective-permute-done | bytes 131104 | tf_op jit(solution)/shard_map/ppermute | solution.py:164
  141.1 2.2 %collective-permute-done.44.refs_8_ = f32[8,16,256]{2,1,0:T(8,128)S(1)} collective-permute-done((f32[8,16,256]{2,1,0:T(8,128)S(1)}, f32[8,16,256]{2,1,0:T(8,128)S(1)}, u32[]{:S(2)}, u32[]{:S(2)}) %collective-permute-start.44) | collective-permute-done | bytes 131104 | tf_op jit(solution)/shard_map/ppermute | solution.py:164
  145.7 2.6 %collective-permute-done.53 = f32[16,16,256]{2,1,0:T(8,128)S(1)} collective-permute-done((f32[16,16,256]{2,1,0:T(8,128)S(1)}, f32[16,16,256]{2,1,0:T(8,128)S(1)}, u32[]{:S(2)}, u32[]{:S(2)}) %collective-permute-start.53) | collective-permute-done | bytes 262176 | tf_op jit(solution)/shard_map/ppermute | solution.py:164
  148.4 3.4 %collective-permute-start.54 = (f32[16,16,256]{2,1,0:T(8,128)S(1)}, f32[16,16,256]{2,1,0:T(8,128)S(1)}, u32[]{:S(2)}, u32[]{:S(2)}) collective-permute-start(f32[16,16,256]{2,1,0:T(8,128)S(1)} %add_add_fusion), channel_id=1, source_target_pairs={{0,16},{4,20},{8,24},{12,28},{16,0},{20,4},{24,8},{28,12},{1,17},{... | collective-permute-start | bytes 786440 | tf_op jit(solution)/shard_map/ppermute | solution.py:164
  153.5 10.3 %collective-permute-done.54 = f32[16,16,256]{2,1,0:T(8,128)S(1)} collective-permute-done((f32[16,16,256]{2,1,0:T(8,128)S(1)}, f32[16,16,256]{2,1,0:T(8,128)S(1)}, u32[]{:S(2)}, u32[]{:S(2)}) %collective-permute-start.54) | collective-permute-done | bytes 262176 | tf_op jit(solution)/shard_map/ppermute | solution.py:164
  165.3 2.8 %collective-permute-start.48 = (f32[16,16,256]{2,1,0:T(8,128)S(1)}, f32[16,16,256]{2,1,0:T(8,128)S(1)}, u32[]{:S(2)}, u32[]{:S(2)}) collective-permute-start(f32[16,16,256]{2,1,0:T(8,128)S(1)} %add_add_fusion.1), channel_id=1, source_target_pairs={{0,16},{4,20},{8,24},{12,28},{16,0},{20,4},{24,8},{28,12},{1,17},{... | collective-permute-start | bytes 786440 | tf_op jit(solution)/shard_map/ppermute | solution.py:164
  168.1 8.3 %collective-permute-done.55.refs_7_ = f32[16,16,256]{2,1,0:T(8,128)S(1)} collective-permute-done((f32[16,16,256]{2,1,0:T(8,128)S(1)}, f32[16,16,256]{2,1,0:T(8,128)S(1)}, u32[]{:S(2)}, u32[]{:S(2)}) %collective-permute-start.55) | collective-permute-done | bytes 262176 | tf_op jit(solution)/shard_map/ppermute | solution.py:164
  176.4 3.5 %collective-permute-done.48 = f32[16,16,256]{2,1,0:T(8,128)S(1)} collective-permute-done((f32[16,16,256]{2,1,0:T(8,128)S(1)}, f32[16,16,256]{2,1,0:T(8,128)S(1)}, u32[]{:S(2)}, u32[]{:S(2)}) %collective-permute-start.48) | collective-permute-done | bytes 262176 | tf_op jit(solution)/shard_map/ppermute | solution.py:164
  180.2 6.2 %collective-permute-done.49.refs_7_ = f32[16,16,256]{2,1,0:T(8,128)S(1)} collective-permute-done((f32[16,16,256]{2,1,0:T(8,128)S(1)}, f32[16,16,256]{2,1,0:T(8,128)S(1)}, u32[]{:S(2)}, u32[]{:S(2)}) %collective-permute-start.49) | collective-permute-done | bytes 262176 | tf_op jit(solution)/shard_map/ppermute | solution.py:164
  186.4 3.4 %primal_step.10 = (f32[32,16384]{1,0:T(8,128)}, f32[8,16,256]{2,1,0:T(8,128)S(1)}, f32[8,16,256]{2,1,0:T(8,128)S(1)}) custom-call(s32[3,48]{1,0:T(4,128)S(1)} %pad_add_fusion.refs_0_.meta_ref, bf16[48,256,256]{2,1,0:T(8,128)(2,1)S(1)} %bitcast.17, f32[16,16384]{1,0:T(8,128)S(1)} %get-tuple-element.413.refs_2_, f32[1,16384]{1,0:T(1,128)S(1)} %bitcast.23, ...), custom_call_target="tpu_custom_call" | custom-call | flops 99999997952 | bytes 1000000000 | tf_op jit(solution)/shard_map/primal_step/pallas_call | solution.py:206
  192.7 3.4 %primal_step.11 = (f32[32,16384]{1,0:T(8,128)}, f32[8,16,256]{2,1,0:T(8,128)S(1)}, f32[8,16,256]{2,1,0:T(8,128)S(1)}) custom-call(s32[3,48]{1,0:T(4,128)S(1)} %pad_add_fusion.refs_0_.meta_ref, bf16[48,256,256]{2,1,0:T(8,128)(2,1)S(1)} %bitcast.18, f32[16,16384]{1,0:T(8,128)S(1)} %get-tuple-element.378.refs_2_, ...), custom_call_target="tpu_custom_call", output_to_operand_aliasing={{0}: (10, {})} | custom-call | flops 99999997952 | bytes 1000000000 | tf_op jit(solution)/shard_map/primal_step/pallas_call | solution.py:206
  200.4 2.1 %collective-permute-done.58 = f32[8,16,256]{2,1,0:T(8,128)S(1)} collective-permute-done((f32[8,16,256]{2,1,0:T(8,128)S(1)}, f32[8,16,256]{2,1,0:T(8,128)S(1)}, u32[]{:S(2)}, u32[]{:S(2)}) %collective-permute-start.58) | collective-permute-done | bytes 131104 | tf_op jit(solution)/shard_map/ppermute | solution.py:164
  (164 shorter events, 75.0 us)
Async XLA Ops:
  9.2 9.6 %collective-permute-start.4 = (f32[16,16,256]{2,1,0:T(8,128)S(1)}, f32[16,16,256]{2,1,0:T(8,128)S(1)}, u32[]{:S(2)}, u32[]{:S(2)}) collective-permute-start(f32[16,16,256]{2,1,0:T(8,128)S(1)} %add.108), channel_id=1, source_target_pairs={{0,8},{4,12},{8,0},{12,4},{16,24},{20,28},{24,16},{28,20},{1,9},{5... | collective-permute-start | bytes 786440 | tf_op jit(solution)/shard_map/ppermute | solution.py:164
  13.9 7.8 %collective-permute-start.1 = (f32[16,16,256]{2,1,0:T(8,128)S(1)}, f32[16,16,256]{2,1,0:T(8,128)S(1)}, u32[]{:S(2)}, u32[]{:S(2)}) collective-permute-start(f32[16,16,256]{2,1,0:T(8,128)S(1)} %get-tuple-element.230), channel_id=1, source_target_pairs={{0,4},{4,0},{8,12},{12,8},{16,20},{20,16},{24,28},{28,24},{1,5},{5... | collective-permute-start | bytes 786440 | tf_op jit(solution)/shard_map/ppermute | solution.py:164
  18.8 14.5 %collective-permute-start.6 = (f32[16,16,256]{2,1,0:T(8,128)S(1)}, f32[16,16,256]{2,1,0:T(8,128)S(1)}, u32[]{:S(2)}, u32[]{:S(2)}) collective-permute-start(f32[16,16,256]{2,1,0:T(8,128)S(1)} %add_add_fusion.5), channel_id=1, source_target_pairs={{0,16},{4,20},{8,24},{12,28},{16,0},{20,4},{24,8},{28,12},{1,17},{... | collective-permute-start | bytes 786440 | tf_op jit(solution)/shard_map/ppermute | solution.py:164
  21.7 12.3 %collective-permute-start = (f32[16,16,256]{2,1,0:T(8,128)S(1)}, f32[16,16,256]{2,1,0:T(8,128)S(1)}, u32[]{:S(2)}, u32[]{:S(2)}) collective-permute-start(f32[16,16,256]{2,1,0:T(8,128)S(1)} %get-tuple-element.228), channel_id=1, source_target_pairs={{0,4},{4,0},{8,12},{12,8},{16,20},{20,16},{24,28},{28,24},{1,5},{5... | collective-permute-start | bytes 786440 | tf_op jit(solution)/shard_map/ppermute | solution.py:164
  21.7 13.4 %collective-permute-start.5 = (f32[16,16,256]{2,1,0:T(8,128)S(1)}, f32[16,16,256]{2,1,0:T(8,128)S(1)}, u32[]{:S(2)}, u32[]{:S(2)}) collective-permute-start(f32[16,16,256]{2,1,0:T(8,128)S(1)} %add.111), channel_id=1, source_target_pairs={{0,8},{4,12},{8,0},{12,4},{16,24},{20,28},{24,16},{28,20},{1,9},{5... | collective-permute-start | bytes 786440 | tf_op jit(solution)/shard_map/ppermute | solution.py:164
  33.4 7.4 %collective-permute-start.8 = (f32[16,16,256]{2,1,0:T(8,128)S(1)}, f32[16,16,256]{2,1,0:T(8,128)S(1)}, u32[]{:S(2)}, u32[]{:S(2)}) collective-permute-start(f32[16,16,256]{2,1,0:T(8,128)S(1)} %add.112.refs_6_), channel_id=1, source_target_pairs={{0,8},{4,12},{8,0},{12,4},{16,24},{20,28},{24,16},{28,20},{1,9},{5... | collective-permute-start | bytes 786440 | tf_op jit(solution)/shard_map/ppermute | solution.py:164
  33.9 9.9 %collective-permute-start.9 = (f32[16,16,256]{2,1,0:T(8,128)S(1)}, f32[16,16,256]{2,1,0:T(8,128)S(1)}, u32[]{:S(2)}, u32[]{:S(2)}) collective-permute-start(f32[16,16,256]{2,1,0:T(8,128)S(1)} %add.112.refs_6_), channel_id=1, source_target_pairs={{0,4},{4,0},{8,12},{12,8},{16,20},{20,16},{24,28},{28,24},{1,5},{5... | collective-permute-start | bytes 786440 | tf_op jit(solution)/shard_map/ppermute | solution.py:164
  40.8 15.6 %collective-permute-start.7 = (f32[16,16,256]{2,1,0:T(8,128)S(1)}, f32[16,16,256]{2,1,0:T(8,128)S(1)}, u32[]{:S(2)}, u32[]{:S(2)}) collective-permute-start(f32[16,16,256]{2,1,0:T(8,128)S(1)} %add_add_fusion.4), channel_id=1, source_target_pairs={{0,16},{4,20},{8,24},{12,28},{16,0},{20,4},{24,8},{28,12},{1,17},{... | collective-permute-start | bytes 786440 | tf_op jit(solution)/shard_map/ppermute | solution.py:164
  56.4 8.2 %collective-permute-start.13 = (f32[16,16,256]{2,1,0:T(8,128)S(1)}, f32[16,16,256]{2,1,0:T(8,128)S(1)}, u32[]{:S(2)}, u32[]{:S(2)}) collective-permute-start(f32[16,16,256]{2,1,0:T(8,128)S(1)} %add.116.refs_6_), channel_id=1, source_target_pairs={{0,8},{4,12},{8,0},{12,4},{16,24},{20,28},{24,16},{28,20},{1,9},{5... | collective-permute-start | bytes 786440 | tf_op jit(solution)/shard_map/ppermute | solution.py:164
  64.6 7.2 %collective-permute-start.23 = (f32[16,16,256]{2,1,0:T(8,128)S(1)}, f32[16,16,256]{2,1,0:T(8,128)S(1)}, u32[]{:S(2)}, u32[]{:S(2)}) collective-permute-start(f32[16,16,256]{2,1,0:T(8,128)S(1)} %get-tuple-element.306), channel_id=1, source_target_pairs={{0,4},{4,0},{8,12},{12,8},{16,20},{20,16},{24,28},{28,24},{1,5},{5... | collective-permute-start | bytes 786440 | tf_op jit(solution)/shard_map/ppermute | solution.py:164
  65.2 8.3 %collective-permute-start.24 = (f32[16,16,256]{2,1,0:T(8,128)S(1)}, f32[16,16,256]{2,1,0:T(8,128)S(1)}, u32[]{:S(2)}, u32[]{:S(2)}) collective-permute-start(f32[16,16,256]{2,1,0:T(8,128)S(1)} %add.120), channel_id=1, source_target_pairs={{0,8},{4,12},{8,0},{12,4},{16,24},{20,28},{24,16},{28,20},{1,9},{5... | collective-permute-start | bytes 786440 | tf_op jit(solution)/shard_map/ppermute | solution.py:164
  77.9 13.3 %collective-permute-start.28 = (f32[16,16,256]{2,1,0:T(8,128)S(1)}, f32[16,16,256]{2,1,0:T(8,128)S(1)}, u32[]{:S(2)}, u32[]{:S(2)}) collective-permute-start(f32[16,16,256]{2,1,0:T(8,128)S(1)} %add_add_fusion.3), channel_id=1, source_target_pairs={{0,16},{4,20},{8,24},{12,28},{16,0},{20,4},{24,8},{28,12},{1,17},{... | collective-permute-start | bytes 786440 | tf_op jit(solution)/shard_map/ppermute | solution.py:164
  83.0 9.0 %collective-permute-start.26 = (f32[16,16,256]{2,1,0:T(8,128)S(1)}, f32[16,16,256]{2,1,0:T(8,128)S(1)}, u32[]{:S(2)}, u32[]{:S(2)}) collective-permute-start(f32[16,16,256]{2,1,0:T(8,128)S(1)} %get-tuple-element.323), channel_id=1, source_target_pairs={{0,4},{4,0},{8,12},{12,8},{16,20},{20,16},{24,28},{28,24},{1,5},{5... | collective-permute-start | bytes 786440 | tf_op jit(solution)/shard_map/ppermute | solution.py:164
  91.2 9.3 %collective-permute-start.30 = (f32[16,16,256]{2,1,0:T(8,128)S(1)}, f32[16,16,256]{2,1,0:T(8,128)S(1)}, u32[]{:S(2)}, u32[]{:S(2)}) collective-permute-start(f32[16,16,256]{2,1,0:T(8,128)S(1)} %add.124.refs_6_), channel_id=1, source_target_pairs={{0,8},{4,12},{8,0},{12,4},{16,24},{20,28},{24,16},{28,20},{1,9},{5... | collective-permute-start | bytes 786440 | tf_op jit(solution)/shard_map/ppermute | solution.py:164
  91.9 8.6 %collective-permute-start.25 = (f32[16,16,256]{2,1,0:T(8,128)S(1)}, f32[16,16,256]{2,1,0:T(8,128)S(1)}, u32[]{:S(2)}, u32[]{:S(2)}) collective-permute-start(f32[16,16,256]{2,1,0:T(8,128)S(1)} %get-tuple-element.321), channel_id=1, source_target_pairs={{0,4},{4,0},{8,12},{12,8},{16,20},{20,16},{24,28},{28,24},{1,5},{5... | collective-permute-start | bytes 786440 | tf_op jit(solution)/shard_map/ppermute | solution.py:164
  92.0 12.1 %collective-permute-start.27 = (f32[16,16,256]{2,1,0:T(8,128)S(1)}, f32[16,16,256]{2,1,0:T(8,128)S(1)}, u32[]{:S(2)}, u32[]{:S(2)}) collective-permute-start(f32[16,16,256]{2,1,0:T(8,128)S(1)} %add.123), channel_id=1, source_target_pairs={{0,8},{4,12},{8,0},{12,4},{16,24},{20,28},{24,16},{28,20},{1,9},{5... | collective-permute-start | bytes 786440 | tf_op jit(solution)/shard_map/ppermute | solution.py:164
  93.4 14.1 %collective-permute-start.31 = (f32[16,16,256]{2,1,0:T(8,128)S(1)}, f32[16,16,256]{2,1,0:T(8,128)S(1)}, u32[]{:S(2)}, u32[]{:S(2)}) collective-permute-start(f32[16,16,256]{2,1,0:T(8,128)S(1)} %add.124.refs_6_), channel_id=1, source_target_pairs={{0,4},{4,0},{8,12},{12,8},{16,20},{20,16},{24,28},{28,24},{1,5},{5... | collective-permute-start | bytes 786440 | tf_op jit(solution)/shard_map/ppermute | solution.py:164
  100.5 7.0 %collective-permute-start.32 = (f32[16,16,256]{2,1,0:T(8,128)S(1)}, f32[16,16,256]{2,1,0:T(8,128)S(1)}, u32[]{:S(2)}, u32[]{:S(2)}) collective-permute-start(f32[16,16,256]{2,1,0:T(8,128)S(1)} %collective-permute-done.30.refs_7_), channel_id=1, source_target_pairs={{0,4},{4,0},{8,12},{12,8},{16,20},{20,16},{24,28},{28,24},{1,5},{5... | collective-permute-start | bytes 786440 | tf_op jit(solution)/shard_map/ppermute | solution.py:164
  104.1 15.0 %collective-permute-start.29 = (f32[16,16,256]{2,1,0:T(8,128)S(1)}, f32[16,16,256]{2,1,0:T(8,128)S(1)}, u32[]{:S(2)}, u32[]{:S(2)}) collective-permute-start(f32[16,16,256]{2,1,0:T(8,128)S(1)} %add_add_fusion.2), channel_id=1, source_target_pairs={{0,16},{4,20},{8,24},{12,28},{16,0},{20,4},{24,8},{28,12},{1,17},{... | collective-permute-start | bytes 786440 | tf_op jit(solution)/shard_map/ppermute | solution.py:164
  110.2 9.8 %collective-permute-start.33 = (f32[8,16,256]{2,1,0:T(8,128)S(1)}, f32[8,16,256]{2,1,0:T(8,128)S(1)}, u32[]{:S(2)}, u32[]{:S(2)}) collective-permute-start(f32[8,16,256]{2,1,0:T(8,128)S(1)} %get-tuple-element.353), channel_id=1, source_target_pairs={{0,1},{1,0},{2,3},{3,2},{4,5},{5,4},{6,7},{7,6},{8,9},{9,8},{10,11... | collective-permute-start | bytes 393224 | tf_op jit(solution)/shard_map/ppermute | solution.py:164
  111.7 8.2 %collective-permute-start.34 = (f32[8,16,256]{2,1,0:T(8,128)S(1)}, f32[8,16,256]{2,1,0:T(8,128)S(1)}, u32[]{:S(2)}, u32[]{:S(2)}) collective-permute-start(f32[8,16,256]{2,1,0:T(8,128)S(1)} %get-tuple-element.358), channel_id=1, source_target_pairs={{0,2},{1,3},{2,0},{3,1},{4,6},{5,7},{6,4},{7,5},{8,10},{9,11},{10,... | collective-permute-start | bytes 393224 | tf_op jit(solution)/shard_map/ppermute | solution.py:164
  119.2 7.4 %collective-permute-start.35 = (f32[16,16,256]{2,1,0:T(8,128)S(1)}, f32[16,16,256]{2,1,0:T(8,128)S(1)}, u32[]{:S(2)}, u32[]{:S(2)}) collective-permute-start(f32[16,16,256]{2,1,0:T(8,128)S(1)} %add.128.refs_6_), channel_id=1, source_target_pairs={{0,8},{4,12},{8,0},{12,4},{16,24},{20,28},{24,16},{28,20},{1,9},{5... | collective-permute-start | bytes 786440 | tf_op jit(solution)/shard_map/ppermute | solution.py:164
  139.5 8.8 %collective-permute-start.53 = (f32[16,16,256]{2,1,0:T(8,128)S(1)}, f32[16,16,256]{2,1,0:T(8,128)S(1)}, u32[]{:S(2)}, u32[]{:S(2)}) collective-permute-start(f32[16,16,256]{2,1,0:T(8,128)S(1)} %add.136), channel_id=1, source_target_pairs={{0,8},{4,12},{8,0},{12,4},{16,24},{20,28},{24,16},{28,20},{1,9},{5... | collective-permute-start | bytes 786440 | tf_op jit(solution)/shard_map/ppermute | solution.py:164
  148.4 15.4 %collective-permute-start.54 = (f32[16,16,256]{2,1,0:T(8,128)S(1)}, f32[16,16,256]{2,1,0:T(8,128)S(1)}, u32[]{:S(2)}, u32[]{:S(2)}) collective-permute-start(f32[16,16,256]{2,1,0:T(8,128)S(1)} %add_add_fusion), channel_id=1, source_target_pairs={{0,16},{4,20},{8,24},{12,28},{16,0},{20,4},{24,8},{28,12},{1,17},{... | collective-permute-start | bytes 786440 | tf_op jit(solution)/shard_map/ppermute | solution.py:164
  151.8 12.7 %collective-permute-start.45 = (f32[16,16,256]{2,1,0:T(8,128)S(1)}, f32[16,16,256]{2,1,0:T(8,128)S(1)}, u32[]{:S(2)}, u32[]{:S(2)}) collective-permute-start(f32[16,16,256]{2,1,0:T(8,128)S(1)} %get-tuple-element.397), channel_id=1, source_target_pairs={{0,4},{4,0},{8,12},{12,8},{16,20},{20,16},{24,28},{28,24},{1,5},{5... | collective-permute-start | bytes 786440 | tf_op jit(solution)/shard_map/ppermute | solution.py:164
  151.9 13.4 %collective-permute-start.47 = (f32[16,16,256]{2,1,0:T(8,128)S(1)}, f32[16,16,256]{2,1,0:T(8,128)S(1)}, u32[]{:S(2)}, u32[]{:S(2)}) collective-permute-start(f32[16,16,256]{2,1,0:T(8,128)S(1)} %add.132), channel_id=1, source_target_pairs={{0,8},{4,12},{8,0},{12,4},{16,24},{20,28},{24,16},{28,20},{1,9},{5... | collective-permute-start | bytes 786440 | tf_op jit(solution)/shard_map/ppermute | solution.py:164
  163.8 12.6 %collective-permute-start.55 = (f32[16,16,256]{2,1,0:T(8,128)S(1)}, f32[16,16,256]{2,1,0:T(8,128)S(1)}, u32[]{:S(2)}, u32[]{:S(2)}) collective-permute-start(f32[16,16,256]{2,1,0:T(8,128)S(1)} %add.139.refs_6_), channel_id=1, source_target_pairs={{0,8},{4,12},{8,0},{12,4},{16,24},{20,28},{24,16},{28,20},{1,9},{5... | collective-permute-start | bytes 786440 | tf_op jit(solution)/shard_map/ppermute | solution.py:164
  165.3 14.6 %collective-permute-start.48 = (f32[16,16,256]{2,1,0:T(8,128)S(1)}, f32[16,16,256]{2,1,0:T(8,128)S(1)}, u32[]{:S(2)}, u32[]{:S(2)}) collective-permute-start(f32[16,16,256]{2,1,0:T(8,128)S(1)} %add_add_fusion.1), channel_id=1, source_target_pairs={{0,16},{4,20},{8,24},{12,28},{16,0},{20,4},{24,8},{28,12},{1,17},{... | collective-permute-start | bytes 786440 | tf_op jit(solution)/shard_map/ppermute | solution.py:164
  168.1 12.1 %collective-permute-start.56 = (f32[16,16,256]{2,1,0:T(8,128)S(1)}, f32[16,16,256]{2,1,0:T(8,128)S(1)}, u32[]{:S(2)}, u32[]{:S(2)}) collective-permute-start(f32[16,16,256]{2,1,0:T(8,128)S(1)} %add.139.refs_6_), channel_id=1, source_target_pairs={{0,4},{4,0},{8,12},{12,8},{16,20},{20,16},{24,28},{28,24},{1,5},{5... | collective-permute-start | bytes 786440 | tf_op jit(solution)/shard_map/ppermute | solution.py:164
  180.2 12.4 %collective-permute-start.50 = (f32[16,16,256]{2,1,0:T(8,128)S(1)}, f32[16,16,256]{2,1,0:T(8,128)S(1)}, u32[]{:S(2)}, u32[]{:S(2)}) collective-permute-start(f32[16,16,256]{2,1,0:T(8,128)S(1)} %add.135.refs_6_), channel_id=1, source_target_pairs={{0,4},{4,0},{8,12},{12,8},{16,20},{20,16},{24,28},{28,24},{1,5},{5... | collective-permute-start | bytes 786440 | tf_op jit(solution)/shard_map/ppermute | solution.py:164
  189.8 7.6 %collective-permute-start.62 = (f32[8,16,256]{2,1,0:T(8,128)S(1)}, f32[8,16,256]{2,1,0:T(8,128)S(1)}, u32[]{:S(2)}, u32[]{:S(2)}) collective-permute-start(f32[8,16,256]{2,1,0:T(8,128)S(1)} %get-tuple-element.444), channel_id=1, source_target_pairs={{0,1},{1,0},{2,3},{3,2},{4,5},{5,4},{6,7},{7,6},{8,9},{9,8},{10,11... | collective-permute-start | bytes 393224 | tf_op jit(solution)/shard_map/ppermute | solution.py:164
  197.5 8.0 %collective-permute-start.65 = (f32[8,16,256]{2,1,0:T(8,128)S(1)}, f32[8,16,256]{2,1,0:T(8,128)S(1)}, u32[]{:S(2)}, u32[]{:S(2)}) collective-permute-start(f32[8,16,256]{2,1,0:T(8,128)S(1)} %add.143.r_ref), channel_id=1, source_target_pairs={{0,1},{1,0},{2,3},{3,2},{4,5},{5,4},{6,7},{7,6},{8,9},{9,8},{10,11... | collective-permute-start | bytes 393224 | tf_op jit(solution)/shard_map/ppermute | solution.py:164
  (42 other events, 329.0 us)

commit v4 on v3

--- a/solution.py
+++ b/solution.py
@@ -36,14 +36,20 @@
     return col ^ (place * quarter)
 
 
-def dual_kernel(first, n_tiles, tile_rows, tile_cols, width, *refs):
+def dual_kernel(first, y_at, n_tiles, tile_rows, tile_cols, width, *refs):
     if first:
+        *refs, y_buf, sem = refs
         (meta_ref, tiles_ref, y_ref,
          dual_ref, q0, q1, q2, q3, low, prods, acc) = refs
     else:
         (meta_ref, tiles_ref, y_ref, demand_ref, sigma_ref,
          l_ref, l2_ref, r_ref, r2_ref,
          dual_ref, q0, q1, q2, q3, low, prods, acc) = refs
+    if first:
+        copy = pltpu.make_async_copy(y_ref.at[pl.ds(y_at, y_buf.shape[0])], y_buf, sem)
+        copy.start()
+        copy.wait()
+        y_ref = y_buf
     scen = y_ref.shape[0]
     count, place = meta_ref[2, 0], meta_ref[2, 1]
     lane = lax.broadcasted_iota(jnp.int32, (scen, width), 1)
@@ -173,11 +179,13 @@
         first = parts is None
         args = [meta, blocks, dual]
         specs = [scalars(), whole(blocks.shape), y_spec(dual, group)]
-        if not first:
+        if first:
+            specs[2] = pl.BlockSpec(memory_space=pltpu.HBM)
+        else:
             args += [demand, sigma_col, *parts]
             specs += [y_spec(demand, group), row_block(m, width, group)] + [whole((half, m, width))] * 4
         return pl.pallas_call(
-            functools.partial(dual_kernel, first, n_tiles, tile_rows, tile_cols, width),
+            functools.partial(dual_kernel, first, group * m, n_tiles, tile_rows, tile_cols, width),
             grid=(1,),
             in_specs=specs,
             out_shape=[jax.ShapeDtypeStruct((m, rows_dev), f32)] + quarters,
@@ -186,7 +194,7 @@
                 pltpu.VMEM((tile_rows, m, width), jnp.bfloat16),
                 pltpu.VMEM((n_tiles, m, width), f32),
                 pltpu.VMEM((tile_cols, m, width), f32),
-            ],
+            ] + ([pltpu.VMEM((m, rows_dev), f32), pltpu.SemaphoreType.DMA] if first else []),
             compiler_params=params,
             cost_estimate=dual_estimate,
             name="dual_step",

time: 211 us -> 211 us (level)
  no operation moved by 1% of the time
where the time goes in v4:
time: 211 us
  waiting for transfers between devices  111 us (53%)
  starting transfers between devices  62.7 us (30%)
  Pallas kernels  30.2 us (14%)
  local copies, waits for them, and re-layouts  4 us (2%)
    ppermute x66, waiting for transfers between devices, swap(): return lax.ppermute(value, axis, [(i, i ^ bit) for i in range(size)])  111 us
    ppermute x66, starting transfers between devices, swap(): return lax.ppermute(value, axis, [(i, i ^ bit) for i in range(size)])  62.7 us
    pallas_call x6, Pallas kernels, step_primal(): pl.pallas_call(functools.partial(primal_kernel, n_tiles, tile_rows, tile_...  17.4 us
    pallas_call x6, Pallas kernels, step_dual(): pl.pallas_call(functools.partial(dual_kernel, first, group * m, n_tiles,...  10.1 us
  transfers between devices with their start and end apart: 66, of which 36 were waited for; matrix products, arithmetic and copies ran while one was open for 1% of the time, Pallas kernels for 12%

profile of v4, /device:TPU:0, one launch (start us, length us, event | category | flops | bytes accessed | tf_op | source)
XLA Modules:
  0.0 211.1 jit_solution(7166731295662358600)
XLA Ops:
  2.0 2.8 %copy-done.1 = bf16[1,1,48,256,256]{4,3,2,1,0:T(8,128)(2,1)S(1)} copy-done((bf16[1,1,48,256,256]{4,3,2,1,0:T(8,128)(2,1)S(1)}, bf16[1,1,48,256,256]{4,3,2,1,0:T(8,128)(2,1)}, u32[]{:S(2)}) %copy-start.1) | copy-done | bytes 6291480
  9.2 3.0 %collective-permute-start.4 = (f32[16,16,256]{2,1,0:T(8,128)S(1)}, f32[16,16,256]{2,1,0:T(8,128)S(1)}, u32[]{:S(2)}, u32[]{:S(2)}) collective-permute-start(f32[16,16,256]{2,1,0:T(8,128)S(1)} %add.108), channel_id=1, source_target_pairs={{0,8},{4,12},{8,0},{12,4},{16,24},{20,28},{24,16},{28,20},{1,9},{5... | collective-permute-start | bytes 786440 | tf_op jit(solution)/shard_map/ppermute | solution.py:170
  14.0 4.8 %collective-permute-done.4 = f32[16,16,256]{2,1,0:T(8,128)S(1)} collective-permute-done((f32[16,16,256]{2,1,0:T(8,128)S(1)}, f32[16,16,256]{2,1,0:T(8,128)S(1)}, u32[]{:S(2)}, u32[]{:S(2)}) %collective-permute-start.4) | collective-permute-done | bytes 262176 | tf_op jit(solution)/shard_map/ppermute | solution.py:170
  18.9 2.8 %collective-permute-start.6 = (f32[16,16,256]{2,1,0:T(8,128)S(1)}, f32[16,16,256]{2,1,0:T(8,128)S(1)}, u32[]{:S(2)}, u32[]{:S(2)}) collective-permute-start(f32[16,16,256]{2,1,0:T(8,128)S(1)} %add_add_fusion.5), channel_id=1, source_target_pairs={{0,16},{4,20},{8,24},{12,28},{16,0},{20,4},{24,8},{28,12},{1,17},{... | collective-permute-start | bytes 786440 | tf_op jit(solution)/shard_map/ppermute | solution.py:170
  23.4 10.0 %collective-permute-done.6 = f32[16,16,256]{2,1,0:T(8,128)S(1)} collective-permute-done((f32[16,16,256]{2,1,0:T(8,128)S(1)}, f32[16,16,256]{2,1,0:T(8,128)S(1)}, u32[]{:S(2)}, u32[]{:S(2)}) %collective-permute-start.6) | collective-permute-done | bytes 262176 | tf_op jit(solution)/shard_map/ppermute | solution.py:170
  35.2 5.6 %collective-permute-done.8.refs_7_ = f32[16,16,256]{2,1,0:T(8,128)S(1)} collective-permute-done((f32[16,16,256]{2,1,0:T(8,128)S(1)}, f32[16,16,256]{2,1,0:T(8,128)S(1)}, u32[]{:S(2)}, u32[]{:S(2)}) %collective-permute-start.8) | collective-permute-done | bytes 262176 | tf_op jit(solution)/shard_map/ppermute | solution.py:170
  40.8 3.0 %collective-permute-start.7 = (f32[16,16,256]{2,1,0:T(8,128)S(1)}, f32[16,16,256]{2,1,0:T(8,128)S(1)}, u32[]{:S(2)}, u32[]{:S(2)}) collective-permute-start(f32[16,16,256]{2,1,0:T(8,128)S(1)} %add_add_fusion.4), channel_id=1, source_target_pairs={{0,16},{4,20},{8,24},{12,28},{16,0},{20,4},{24,8},{28,12},{1,17},{... | collective-permute-start | bytes 786440 | tf_op jit(solution)/shard_map/ppermute | solution.py:170
  44.0 2.6 %primal_step.6 = (f32[16,16384]{1,0:T(8,128)S(1)}, f32[8,16,256]{2,1,0:T(8,128)S(1)}, f32[8,16,256]{2,1,0:T(8,128)S(1)}) custom-call(s32[3,48]{1,0:T(4,128)S(1)} %pad_add_fusion.refs_0_.meta_ref, bf16[48,256,256]{2,1,0:T(8,128)(2,1)S(1)} %bitcast.9, f32[32,16384]{1,0:T(8,128)S(1)} %copy-done.2, f32[1,16384]{1,0:T(1,128)S(1)} %bitcast.19, ...), custom_call_target="tpu_custom_call" | custom-call | flops 99999997952 | bytes 1000000000 | tf_op jit(solution)/shard_map/primal_step/pallas_call | solution.py:214
  49.6 2.6 %collective-permute-done.12 = f32[8,16,256]{2,1,0:T(8,128)S(1)} collective-permute-done((f32[8,16,256]{2,1,0:T(8,128)S(1)}, f32[8,16,256]{2,1,0:T(8,128)S(1)}, u32[]{:S(2)}, u32[]{:S(2)}) %collective-permute-start.12) | collective-permute-done | bytes 131104 | tf_op jit(solution)/shard_map/ppermute | solution.py:170
  62.5 2.2 %collective-permute-done.13.refs_7_ = f32[16,16,256]{2,1,0:T(8,128)S(1)} collective-permute-done((f32[16,16,256]{2,1,0:T(8,128)S(1)}, f32[16,16,256]{2,1,0:T(8,128)S(1)}, u32[]{:S(2)}, u32[]{:S(2)}) %collective-permute-start.13) | collective-permute-done | bytes 262176 | tf_op jit(solution)/shard_map/ppermute | solution.py:170
  66.2 2.6 %primal_step.7 = (f32[16,16384]{1,0:T(8,128)S(1)}, f32[8,16,256]{2,1,0:T(8,128)S(1)}, f32[8,16,256]{2,1,0:T(8,128)S(1)}) custom-call(s32[3,48]{1,0:T(4,128)S(1)} %pad_add_fusion.refs_0_.meta_ref, bf16[48,256,256]{2,1,0:T(8,128)(2,1)S(1)} %bitcast.11, f32[32,16384]{1,0:T(8,128)S(1)} %copy-done.2, f32[1,16384]{1,0:T(1,128)S(1)} %bitcast.20, ...), custom_call_target="tpu_custom_call" | custom-call | flops 99999997952 | bytes 1000000000 | tf_op jit(solution)/shard_map/primal_step/pallas_call | solution.py:214
  77.9 3.1 %collective-permute-start.28 = (f32[16,16,256]{2,1,0:T(8,128)S(1)}, f32[16,16,256]{2,1,0:T(8,128)S(1)}, u32[]{:S(2)}, u32[]{:S(2)}) collective-permute-start(f32[16,16,256]{2,1,0:T(8,128)S(1)} %add_add_fusion.3), channel_id=1, source_target_pairs={{0,16},{4,20},{8,24},{12,28},{16,0},{20,4},{24,8},{28,12},{1,17},{... | collective-permute-start | bytes 786440 | tf_op jit(solution)/shard_map/ppermute | solution.py:170
  83.1 8.1 %collective-permute-done.28 = f32[16,16,256]{2,1,0:T(8,128)S(1)} collective-permute-done((f32[16,16,256]{2,1,0:T(8,128)S(1)}, f32[16,16,256]{2,1,0:T(8,128)S(1)}, u32[]{:S(2)}, u32[]{:S(2)}) %collective-permute-start.28) | collective-permute-done | bytes 262176 | tf_op jit(solution)/shard_map/ppermute | solution.py:170
  93.7 6.9 %collective-permute-done.30.refs_7_ = f32[16,16,256]{2,1,0:T(8,128)S(1)} collective-permute-done((f32[16,16,256]{2,1,0:T(8,128)S(1)}, f32[16,16,256]{2,1,0:T(8,128)S(1)}, u32[]{:S(2)}, u32[]{:S(2)}) %collective-permute-start.30) | collective-permute-done | bytes 262176 | tf_op jit(solution)/shard_map/ppermute | solution.py:170
  100.6 3.5 %collective-permute-done.27 = f32[16,16,256]{2,1,0:T(8,128)S(1)} collective-permute-done((f32[16,16,256]{2,1,0:T(8,128)S(1)}, f32[16,16,256]{2,1,0:T(8,128)S(1)}, u32[]{:S(2)}, u32[]{:S(2)}) %collective-permute-start.27) | collective-permute-done | bytes 262176 | tf_op jit(solution)/shard_map/ppermute | solution.py:170
  104.1 3.4 %collective-permute-start.29 = (f32[16,16,256]{2,1,0:T(8,128)S(1)}, f32[16,16,256]{2,1,0:T(8,128)S(1)}, u32[]{:S(2)}, u32[]{:S(2)}) collective-permute-start(f32[16,16,256]{2,1,0:T(8,128)S(1)} %add_add_fusion.2), channel_id=1, source_target_pairs={{0,16},{4,20},{8,24},{12,28},{16,0},{20,4},{24,8},{28,12},{1,17},{... | collective-permute-start | bytes 786440 | tf_op jit(solution)/shard_map/ppermute | solution.py:170
  107.6 2.6 %primal_step.8 = (f32[16,16384]{1,0:T(8,128)S(1)}, f32[8,16,256]{2,1,0:T(8,128)S(1)}, f32[8,16,256]{2,1,0:T(8,128)S(1)}) custom-call(s32[3,48]{1,0:T(4,128)S(1)} %pad_add_fusion.refs_0_.meta_ref, bf16[48,256,256]{2,1,0:T(8,128)(2,1)S(1)} %bitcast.13, f32[16,16384]{1,0:T(8,128)S(1)} %get-tuple-element.337.refs_2_, f32[1,16384]{1,0:T(1,128)S(1)} %bitcast.21, ...), custom_call_target="tpu_custom_call" | custom-call | flops 99999997952 | bytes 1000000000 | tf_op jit(solution)/shard_map/primal_step/pallas_call | solution.py:214
  112.3 6.9 %collective-permute-done.29 = f32[16,16,256]{2,1,0:T(8,128)S(1)} collective-permute-done((f32[16,16,256]{2,1,0:T(8,128)S(1)}, f32[16,16,256]{2,1,0:T(8,128)S(1)}, u32[]{:S(2)}, u32[]{:S(2)}) %collective-permute-start.29) | collective-permute-done | bytes 262176 | tf_op jit(solution)/shard_map/ppermute | solution.py:170
  122.1 3.0 %collective-permute-done.36.refs_6_ = f32[8,16,256]{2,1,0:T(8,128)S(1)} collective-permute-done((f32[8,16,256]{2,1,0:T(8,128)S(1)}, f32[8,16,256]{2,1,0:T(8,128)S(1)}, u32[]{:S(2)}, u32[]{:S(2)}) %collective-permute-start.36) | collective-permute-done | bytes 131104 | tf_op jit(solution)/shard_map/ppermute | solution.py:170
  128.3 2.8 %primal_step.9 = (f32[16,16384]{1,0:T(8,128)S(1)}, f32[8,16,256]{2,1,0:T(8,128)S(1)}, f32[8,16,256]{2,1,0:T(8,128)S(1)}) custom-call(s32[3,48]{1,0:T(4,128)S(1)} %pad_add_fusion.refs_0_.meta_ref, bf16[48,256,256]{2,1,0:T(8,128)(2,1)S(1)} %bitcast.15, f32[16,16384]{1,0:T(8,128)S(1)} %get-tuple-element.292.refs_2_, f32[1,16384]{1,0:T(1,128)S(1)} %bitcast.22, ...), custom_call_target="tpu_custom_call" | custom-call | flops 99999997952 | bytes 1000000000 | tf_op jit(solution)/shard_map/primal_step/pallas_call | solution.py:214
  133.2 3.9 %collective-permute-done.40 = f32[8,16,256]{2,1,0:T(8,128)S(1)} collective-permute-done((f32[8,16,256]{2,1,0:T(8,128)S(1)}, f32[8,16,256]{2,1,0:T(8,128)S(1)}, u32[]{:S(2)}, u32[]{:S(2)}) %collective-permute-start.40) | collective-permute-done | bytes 131104 | tf_op jit(solution)/shard_map/ppermute | solution.py:170
  141.1 2.2 %collective-permute-done.44.refs_8_ = f32[8,16,256]{2,1,0:T(8,128)S(1)} collective-permute-done((f32[8,16,256]{2,1,0:T(8,128)S(1)}, f32[8,16,256]{2,1,0:T(8,128)S(1)}, u32[]{:S(2)}, u32[]{:S(2)}) %collective-permute-start.44) | collective-permute-done | bytes 131104 | tf_op jit(solution)/shard_map/ppermute | solution.py:170
  145.7 2.6 %collective-permute-done.53 = f32[16,16,256]{2,1,0:T(8,128)S(1)} collective-permute-done((f32[16,16,256]{2,1,0:T(8,128)S(1)}, f32[16,16,256]{2,1,0:T(8,128)S(1)}, u32[]{:S(2)}, u32[]{:S(2)}) %collective-permute-start.53) | collective-permute-done | bytes 262176 | tf_op jit(solution)/shard_map/ppermute | solution.py:170
  148.4 3.4 %collective-permute-start.54 = (f32[16,16,256]{2,1,0:T(8,128)S(1)}, f32[16,16,256]{2,1,0:T(8,128)S(1)}, u32[]{:S(2)}, u32[]{:S(2)}) collective-permute-start(f32[16,16,256]{2,1,0:T(8,128)S(1)} %add_add_fusion), channel_id=1, source_target_pairs={{0,16},{4,20},{8,24},{12,28},{16,0},{20,4},{24,8},{28,12},{1,17},{... | collective-permute-start | bytes 786440 | tf_op jit(solution)/shard_map/ppermute | solution.py:170
  153.5 10.3 %collective-permute-done.54 = f32[16,16,256]{2,1,0:T(8,128)S(1)} collective-permute-done((f32[16,16,256]{2,1,0:T(8,128)S(1)}, f32[16,16,256]{2,1,0:T(8,128)S(1)}, u32[]{:S(2)}, u32[]{:S(2)}) %collective-permute-start.54) | collective-permute-done | bytes 262176 | tf_op jit(solution)/shard_map/ppermute | solution.py:170
  165.3 2.8 %collective-permute-start.48 = (f32[16,16,256]{2,1,0:T(8,128)S(1)}, f32[16,16,256]{2,1,0:T(8,128)S(1)}, u32[]{:S(2)}, u32[]{:S(2)}) collective-permute-start(f32[16,16,256]{2,1,0:T(8,128)S(1)} %add_add_fusion.1), channel_id=1, source_target_pairs={{0,16},{4,20},{8,24},{12,28},{16,0},{20,4},{24,8},{28,12},{1,17},{... | collective-permute-start | bytes 786440 | tf_op jit(solution)/shard_map/ppermute | solution.py:170
  168.1 8.3 %collective-permute-done.55.refs_7_ = f32[16,16,256]{2,1,0:T(8,128)S(1)} collective-permute-done((f32[16,16,256]{2,1,0:T(8,128)S(1)}, f32[16,16,256]{2,1,0:T(8,128)S(1)}, u32[]{:S(2)}, u32[]{:S(2)}) %collective-permute-start.55) | collective-permute-done | bytes 262176 | tf_op jit(solution)/shard_map/ppermute | solution.py:170
  176.5 3.5 %collective-permute-done.48 = f32[16,16,256]{2,1,0:T(8,128)S(1)} collective-permute-done((f32[16,16,256]{2,1,0:T(8,128)S(1)}, f32[16,16,256]{2,1,0:T(8,128)S(1)}, u32[]{:S(2)}, u32[]{:S(2)}) %collective-permute-start.48) | collective-permute-done | bytes 262176 | tf_op jit(solution)/shard_map/ppermute | solution.py:170
  180.3 6.2 %collective-permute-done.49.refs_7_ = f32[16,16,256]{2,1,0:T(8,128)S(1)} collective-permute-done((f32[16,16,256]{2,1,0:T(8,128)S(1)}, f32[16,16,256]{2,1,0:T(8,128)S(1)}, u32[]{:S(2)}, u32[]{:S(2)}) %collective-permute-start.49) | collective-permute-done | bytes 262176 | tf_op jit(solution)/shard_map/ppermute | solution.py:170
  186.4 3.4 %primal_step.10 = (f32[32,16384]{1,0:T(8,128)}, f32[8,16,256]{2,1,0:T(8,128)S(1)}, f32[8,16,256]{2,1,0:T(8,128)S(1)}) custom-call(s32[3,48]{1,0:T(4,128)S(1)} %pad_add_fusion.refs_0_.meta_ref, bf16[48,256,256]{2,1,0:T(8,128)(2,1)S(1)} %bitcast.17, f32[16,16384]{1,0:T(8,128)S(1)} %get-tuple-element.413.refs_2_, f32[1,16384]{1,0:T(1,128)S(1)} %bitcast.23, ...), custom_call_target="tpu_custom_call" | custom-call | flops 99999997952 | bytes 1000000000 | tf_op jit(solution)/shard_map/primal_step/pallas_call | solution.py:214
  192.7 3.4 %primal_step.11 = (f32[32,16384]{1,0:T(8,128)}, f32[8,16,256]{2,1,0:T(8,128)S(1)}, f32[8,16,256]{2,1,0:T(8,128)S(1)}) custom-call(s32[3,48]{1,0:T(4,128)S(1)} %pad_add_fusion.refs_0_.meta_ref, bf16[48,256,256]{2,1,0:T(8,128)(2,1)S(1)} %bitcast.18, f32[16,16384]{1,0:T(8,128)S(1)} %get-tuple-element.378.refs_2_, ...), custom_call_target="tpu_custom_call", output_to_operand_aliasing={{0}: (10, {})} | custom-call | flops 99999997952 | bytes 1000000000 | tf_op jit(solution)/shard_map/primal_step/pallas_call | solution.py:214
  200.4 2.1 %collective-permute-done.58 = f32[8,16,256]{2,1,0:T(8,128)S(1)} collective-permute-done((f32[8,16,256]{2,1,0:T(8,128)S(1)}, f32[8,16,256]{2,1,0:T(8,128)S(1)}, u32[]{:S(2)}, u32[]{:S(2)}) %collective-permute-start.58) | collective-permute-done | bytes 131104 | tf_op jit(solution)/shard_map/ppermute | solution.py:170
  (164 shorter events, 74.9 us)
Async XLA Ops:
  9.2 9.6 %collective-permute-start.4 = (f32[16,16,256]{2,1,0:T(8,128)S(1)}, f32[16,16,256]{2,1,0:T(8,128)S(1)}, u32[]{:S(2)}, u32[]{:S(2)}) collective-permute-start(f32[16,16,256]{2,1,0:T(8,128)S(1)} %add.108), channel_id=1, source_target_pairs={{0,8},{4,12},{8,0},{12,4},{16,24},{20,28},{24,16},{28,20},{1,9},{5... | collective-permute-start | bytes 786440 | tf_op jit(solution)/shard_map/ppermute | solution.py:170
  13.9 7.8 %collective-permute-start.1 = (f32[16,16,256]{2,1,0:T(8,128)S(1)}, f32[16,16,256]{2,1,0:T(8,128)S(1)}, u32[]{:S(2)}, u32[]{:S(2)}) collective-permute-start(f32[16,16,256]{2,1,0:T(8,128)S(1)} %get-tuple-element.230), channel_id=1, source_target_pairs={{0,4},{4,0},{8,12},{12,8},{16,20},{20,16},{24,28},{28,24},{1,5},{5... | collective-permute-start | bytes 786440 | tf_op jit(solution)/shard_map/ppermute | solution.py:170
  18.9 14.5 %collective-permute-start.6 = (f32[16,16,256]{2,1,0:T(8,128)S(1)}, f32[16,16,256]{2,1,0:T(8,128)S(1)}, u32[]{:S(2)}, u32[]{:S(2)}) collective-permute-start(f32[16,16,256]{2,1,0:T(8,128)S(1)} %add_add_fusion.5), channel_id=1, source_target_pairs={{0,16},{4,20},{8,24},{12,28},{16,0},{20,4},{24,8},{28,12},{1,17},{... | collective-permute-start | bytes 786440 | tf_op jit(solution)/shard_map/ppermute | solution.py:170
  21.7 12.3 %collective-permute-start = (f32[16,16,256]{2,1,0:T(8,128)S(1)}, f32[16,16,256]{2,1,0:T(8,128)S(1)}, u32[]{:S(2)}, u32[]{:S(2)}) collective-permute-start(f32[16,16,256]{2,1,0:T(8,128)S(1)} %get-tuple-element.228), channel_id=1, source_target_pairs={{0,4},{4,0},{8,12},{12,8},{16,20},{20,16},{24,28},{28,24},{1,5},{5... | collective-permute-start | bytes 786440 | tf_op jit(solution)/shard_map/ppermute | solution.py:170
  21.7 13.4 %collective-permute-start.5 = (f32[16,16,256]{2,1,0:T(8,128)S(1)}, f32[16,16,256]{2,1,0:T(8,128)S(1)}, u32[]{:S(2)}, u32[]{:S(2)}) collective-permute-start(f32[16,16,256]{2,1,0:T(8,128)S(1)} %add.111), channel_id=1, source_target_pairs={{0,8},{4,12},{8,0},{12,4},{16,24},{20,28},{24,16},{28,20},{1,9},{5... | collective-permute-start | bytes 786440 | tf_op jit(solution)/shard_map/ppermute | solution.py:170
  33.4 7.4 %collective-permute-start.8 = (f32[16,16,256]{2,1,0:T(8,128)S(1)}, f32[16,16,256]{2,1,0:T(8,128)S(1)}, u32[]{:S(2)}, u32[]{:S(2)}) collective-permute-start(f32[16,16,256]{2,1,0:T(8,128)S(1)} %add.112.refs_6_), channel_id=1, source_target_pairs={{0,8},{4,12},{8,0},{12,4},{16,24},{20,28},{24,16},{28,20},{1,9},{5... | collective-permute-start | bytes 786440 | tf_op jit(solution)/shard_map/ppermute | solution.py:170
  34.0 9.9 %collective-permute-start.9 = (f32[16,16,256]{2,1,0:T(8,128)S(1)}, f32[16,16,256]{2,1,0:T(8,128)S(1)}, u32[]{:S(2)}, u32[]{:S(2)}) collective-permute-start(f32[16,16,256]{2,1,0:T(8,128)S(1)} %add.112.refs_6_), channel_id=1, source_target_pairs={{0,4},{4,0},{8,12},{12,8},{16,20},{20,16},{24,28},{28,24},{1,5},{5... | collective-permute-start | bytes 786440 | tf_op jit(solution)/shard_map/ppermute | solution.py:170
  40.8 15.6 %collective-permute-start.7 = (f32[16,16,256]{2,1,0:T(8,128)S(1)}, f32[16,16,256]{2,1,0:T(8,128)S(1)}, u32[]{:S(2)}, u32[]{:S(2)}) collective-permute-start(f32[16,16,256]{2,1,0:T(8,128)S(1)} %add_add_fusion.4), channel_id=1, source_target_pairs={{0,16},{4,20},{8,24},{12,28},{16,0},{20,4},{24,8},{28,12},{1,17},{... | collective-permute-start | bytes 786440 | tf_op jit(solution)/shard_map/ppermute | solution.py:170
  56.5 8.2 %collective-permute-start.13 = (f32[16,16,256]{2,1,0:T(8,128)S(1)}, f32[16,16,256]{2,1,0:T(8,128)S(1)}, u32[]{:S(2)}, u32[]{:S(2)}) collective-permute-start(f32[16,16,256]{2,1,0:T(8,128)S(1)} %add.116.refs_6_), channel_id=1, source_target_pairs={{0,8},{4,12},{8,0},{12,4},{16,24},{20,28},{24,16},{28,20},{1,9},{5... | collective-permute-start | bytes 786440 | tf_op jit(solution)/shard_map/ppermute | solution.py:170
  64.7 7.2 %collective-permute-start.23 = (f32[16,16,256]{2,1,0:T(8,128)S(1)}, f32[16,16,256]{2,1,0:T(8,128)S(1)}, u32[]{:S(2)}, u32[]{:S(2)}) collective-permute-start(f32[16,16,256]{2,1,0:T(8,128)S(1)} %get-tuple-element.306), channel_id=1, source_target_pairs={{0,4},{4,0},{8,12},{12,8},{16,20},{20,16},{24,28},{28,24},{1,5},{5... | collective-permute-start | bytes 786440 | tf_op jit(solution)/shard_map/ppermute | solution.py:170
  65.2 8.3 %collective-permute-start.24 = (f32[16,16,256]{2,1,0:T(8,128)S(1)}, f32[16,16,256]{2,1,0:T(8,128)S(1)}, u32[]{:S(2)}, u32[]{:S(2)}) collective-permute-start(f32[16,16,256]{2,1,0:T(8,128)S(1)} %add.120), channel_id=1, source_target_pairs={{0,8},{4,12},{8,0},{12,4},{16,24},{20,28},{24,16},{28,20},{1,9},{5... | collective-permute-start | bytes 786440 | tf_op jit(solution)/shard_map/ppermute | solution.py:170
  77.9 13.3 %collective-permute-start.28 = (f32[16,16,256]{2,1,0:T(8,128)S(1)}, f32[16,16,256]{2,1,0:T(8,128)S(1)}, u32[]{:S(2)}, u32[]{:S(2)}) collective-permute-start(f32[16,16,256]{2,1,0:T(8,128)S(1)} %add_add_fusion.3), channel_id=1, source_target_pairs={{0,16},{4,20},{8,24},{12,28},{16,0},{20,4},{24,8},{28,12},{1,17},{... | collective-permute-start | bytes 786440 | tf_op jit(solution)/shard_map/ppermute | solution.py:170
  83.0 9.0 %collective-permute-start.26 = (f32[16,16,256]{2,1,0:T(8,128)S(1)}, f32[16,16,256]{2,1,0:T(8,128)S(1)}, u32[]{:S(2)}, u32[]{:S(2)}) collective-permute-start(f32[16,16,256]{2,1,0:T(8,128)S(1)} %get-tuple-element.323), channel_id=1, source_target_pairs={{0,4},{4,0},{8,12},{12,8},{16,20},{20,16},{24,28},{28,24},{1,5},{5... | collective-permute-start | bytes 786440 | tf_op jit(solution)/shard_map/ppermute | solution.py:170
  91.3 9.3 %collective-permute-start.30 = (f32[16,16,256]{2,1,0:T(8,128)S(1)}, f32[16,16,256]{2,1,0:T(8,128)S(1)}, u32[]{:S(2)}, u32[]{:S(2)}) collective-permute-start(f32[16,16,256]{2,1,0:T(8,128)S(1)} %add.124.refs_6_), channel_id=1, source_target_pairs={{0,8},{4,12},{8,0},{12,4},{16,24},{20,28},{24,16},{28,20},{1,9},{5... | collective-permute-start | bytes 786440 | tf_op jit(solution)/shard_map/ppermute | solution.py:170
  92.0 8.6 %collective-permute-start.25 = (f32[16,16,256]{2,1,0:T(8,128)S(1)}, f32[16,16,256]{2,1,0:T(8,128)S(1)}, u32[]{:S(2)}, u32[]{:S(2)}) collective-permute-start(f32[16,16,256]{2,1,0:T(8,128)S(1)} %get-tuple-element.321), channel_id=1, source_target_pairs={{0,4},{4,0},{8,12},{12,8},{16,20},{20,16},{24,28},{28,24},{1,5},{5... | collective-permute-start | bytes 786440 | tf_op jit(solution)/shard_map/ppermute | solution.py:170
  92.0 12.1 %collective-permute-start.27 = (f32[16,16,256]{2,1,0:T(8,128)S(1)}, f32[16,16,256]{2,1,0:T(8,128)S(1)}, u32[]{:S(2)}, u32[]{:S(2)}) collective-permute-start(f32[16,16,256]{2,1,0:T(8,128)S(1)} %add.123), channel_id=1, source_target_pairs={{0,8},{4,12},{8,0},{12,4},{16,24},{20,28},{24,16},{28,20},{1,9},{5... | collective-permute-start | bytes 786440 | tf_op jit(solution)/shard_map/ppermute | solution.py:170
  93.5 14.1 %collective-permute-start.31 = (f32[16,16,256]{2,1,0:T(8,128)S(1)}, f32[16,16,256]{2,1,0:T(8,128)S(1)}, u32[]{:S(2)}, u32[]{:S(2)}) collective-permute-start(f32[16,16,256]{2,1,0:T(8,128)S(1)} %add.124.refs_6_), channel_id=1, source_target_pairs={{0,4},{4,0},{8,12},{12,8},{16,20},{20,16},{24,28},{28,24},{1,5},{5... | collective-permute-start | bytes 786440 | tf_op jit(solution)/shard_map/ppermute | solution.py:170
  100.6 7.0 %collective-permute-start.32 = (f32[16,16,256]{2,1,0:T(8,128)S(1)}, f32[16,16,256]{2,1,0:T(8,128)S(1)}, u32[]{:S(2)}, u32[]{:S(2)}) collective-permute-start(f32[16,16,256]{2,1,0:T(8,128)S(1)} %collective-permute-done.30.refs_7_), channel_id=1, source_target_pairs={{0,4},{4,0},{8,12},{12,8},{16,20},{20,16},{24,28},{28,24},{1,5},{5... | collective-permute-start | bytes 786440 | tf_op jit(solution)/shard_map/ppermute | solution.py:170
  104.1 15.0 %collective-permute-start.29 = (f32[16,16,256]{2,1,0:T(8,128)S(1)}, f32[16,16,256]{2,1,0:T(8,128)S(1)}, u32[]{:S(2)}, u32[]{:S(2)}) collective-permute-start(f32[16,16,256]{2,1,0:T(8,128)S(1)} %add_add_fusion.2), channel_id=1, source_target_pairs={{0,16},{4,20},{8,24},{12,28},{16,0},{20,4},{24,8},{28,12},{1,17},{... | collective-permute-start | bytes 786440 | tf_op jit(solution)/shard_map/ppermute | solution.py:170
  110.2 9.8 %collective-permute-start.33 = (f32[8,16,256]{2,1,0:T(8,128)S(1)}, f32[8,16,256]{2,1,0:T(8,128)S(1)}, u32[]{:S(2)}, u32[]{:S(2)}) collective-permute-start(f32[8,16,256]{2,1,0:T(8,128)S(1)} %get-tuple-element.353), channel_id=1, source_target_pairs={{0,1},{1,0},{2,3},{3,2},{4,5},{5,4},{6,7},{7,6},{8,9},{9,8},{10,11... | collective-permute-start | bytes 393224 | tf_op jit(solution)/shard_map/ppermute | solution.py:170
  111.8 8.2 %collective-permute-start.34 = (f32[8,16,256]{2,1,0:T(8,128)S(1)}, f32[8,16,256]{2,1,0:T(8,128)S(1)}, u32[]{:S(2)}, u32[]{:S(2)}) collective-permute-start(f32[8,16,256]{2,1,0:T(8,128)S(1)} %get-tuple-element.358), channel_id=1, source_target_pairs={{0,2},{1,3},{2,0},{3,1},{4,6},{5,7},{6,4},{7,5},{8,10},{9,11},{10,... | collective-permute-start | bytes 393224 | tf_op jit(solution)/shard_map/ppermute | solution.py:170
  119.2 7.4 %collective-permute-start.35 = (f32[16,16,256]{2,1,0:T(8,128)S(1)}, f32[16,16,256]{2,1,0:T(8,128)S(1)}, u32[]{:S(2)}, u32[]{:S(2)}) collective-permute-start(f32[16,16,256]{2,1,0:T(8,128)S(1)} %add.128.refs_6_), channel_id=1, source_target_pairs={{0,8},{4,12},{8,0},{12,4},{16,24},{20,28},{24,16},{28,20},{1,9},{5... | collective-permute-start | bytes 786440 | tf_op jit(solution)/shard_map/ppermute | solution.py:170
  139.6 8.8 %collective-permute-start.53 = (f32[16,16,256]{2,1,0:T(8,128)S(1)}, f32[16,16,256]{2,1,0:T(8,128)S(1)}, u32[]{:S(2)}, u32[]{:S(2)}) collective-permute-start(f32[16,16,256]{2,1,0:T(8,128)S(1)} %add.136), channel_id=1, source_target_pairs={{0,8},{4,12},{8,0},{12,4},{16,24},{20,28},{24,16},{28,20},{1,9},{5... | collective-permute-start | bytes 786440 | tf_op jit(solution)/shard_map/ppermute | solution.py:170
  148.4 15.4 %collective-permute-start.54 = (f32[16,16,256]{2,1,0:T(8,128)S(1)}, f32[16,16,256]{2,1,0:T(8,128)S(1)}, u32[]{:S(2)}, u32[]{:S(2)}) collective-permute-start(f32[16,16,256]{2,1,0:T(8,128)S(1)} %add_add_fusion), channel_id=1, source_target_pairs={{0,16},{4,20},{8,24},{12,28},{16,0},{20,4},{24,8},{28,12},{1,17},{... | collective-permute-start | bytes 786440 | tf_op jit(solution)/shard_map/ppermute | solution.py:170
  151.9 12.7 %collective-permute-start.45 = (f32[16,16,256]{2,1,0:T(8,128)S(1)}, f32[16,16,256]{2,1,0:T(8,128)S(1)}, u32[]{:S(2)}, u32[]{:S(2)}) collective-permute-start(f32[16,16,256]{2,1,0:T(8,128)S(1)} %get-tuple-element.397), channel_id=1, source_target_pairs={{0,4},{4,0},{8,12},{12,8},{16,20},{20,16},{24,28},{28,24},{1,5},{5... | collective-permute-start | bytes 786440 | tf_op jit(solution)/shard_map/ppermute | solution.py:170
  151.9 13.4 %collective-permute-start.47 = (f32[16,16,256]{2,1,0:T(8,128)S(1)}, f32[16,16,256]{2,1,0:T(8,128)S(1)}, u32[]{:S(2)}, u32[]{:S(2)}) collective-permute-start(f32[16,16,256]{2,1,0:T(8,128)S(1)} %add.132), channel_id=1, source_target_pairs={{0,8},{4,12},{8,0},{12,4},{16,24},{20,28},{24,16},{28,20},{1,9},{5... | collective-permute-start | bytes 786440 | tf_op jit(solution)/shard_map/ppermute | solution.py:170
  163.8 12.6 %collective-permute-start.55 = (f32[16,16,256]{2,1,0:T(8,128)S(1)}, f32[16,16,256]{2,1,0:T(8,128)S(1)}, u32[]{:S(2)}, u32[]{:S(2)}) collective-permute-start(f32[16,16,256]{2,1,0:T(8,128)S(1)} %add.139.refs_6_), channel_id=1, source_target_pairs={{0,8},{4,12},{8,0},{12,4},{16,24},{20,28},{24,16},{28,20},{1,9},{5... | collective-permute-start | bytes 786440 | tf_op jit(solution)/shard_map/ppermute | solution.py:170
  165.3 14.6 %collective-permute-start.48 = (f32[16,16,256]{2,1,0:T(8,128)S(1)}, f32[16,16,256]{2,1,0:T(8,128)S(1)}, u32[]{:S(2)}, u32[]{:S(2)}) collective-permute-start(f32[16,16,256]{2,1,0:T(8,128)S(1)} %add_add_fusion.1), channel_id=1, source_target_pairs={{0,16},{4,20},{8,24},{12,28},{16,0},{20,4},{24,8},{28,12},{1,17},{... | collective-permute-start | bytes 786440 | tf_op jit(solution)/shard_map/ppermute | solution.py:170
  168.1 12.1 %collective-permute-start.56 = (f32[16,16,256]{2,1,0:T(8,128)S(1)}, f32[16,16,256]{2,1,0:T(8,128)S(1)}, u32[]{:S(2)}, u32[]{:S(2)}) collective-permute-start(f32[16,16,256]{2,1,0:T(8,128)S(1)} %add.139.refs_6_), channel_id=1, source_target_pairs={{0,4},{4,0},{8,12},{12,8},{16,20},{20,16},{24,28},{28,24},{1,5},{5... | collective-permute-start | bytes 786440 | tf_op jit(solution)/shard_map/ppermute | solution.py:170
  180.2 12.5 %collective-permute-start.50 = (f32[16,16,256]{2,1,0:T(8,128)S(1)}, f32[16,16,256]{2,1,0:T(8,128)S(1)}, u32[]{:S(2)}, u32[]{:S(2)}) collective-permute-start(f32[16,16,256]{2,1,0:T(8,128)S(1)} %add.135.refs_6_), channel_id=1, source_target_pairs={{0,4},{4,0},{8,12},{12,8},{16,20},{20,16},{24,28},{28,24},{1,5},{5... | collective-permute-start | bytes 786440 | tf_op jit(solution)/shard_map/ppermute | solution.py:170
  189.8 7.6 %collective-permute-start.62 = (f32[8,16,256]{2,1,0:T(8,128)S(1)}, f32[8,16,256]{2,1,0:T(8,128)S(1)}, u32[]{:S(2)}, u32[]{:S(2)}) collective-permute-start(f32[8,16,256]{2,1,0:T(8,128)S(1)} %get-tuple-element.444), channel_id=1, source_target_pairs={{0,1},{1,0},{2,3},{3,2},{4,5},{5,4},{6,7},{7,6},{8,9},{9,8},{10,11... | collective-permute-start | bytes 393224 | tf_op jit(solution)/shard_map/ppermute | solution.py:170
  197.5 8.1 %collective-permute-start.65 = (f32[8,16,256]{2,1,0:T(8,128)S(1)}, f32[8,16,256]{2,1,0:T(8,128)S(1)}, u32[]{:S(2)}, u32[]{:S(2)}) collective-permute-start(f32[8,16,256]{2,1,0:T(8,128)S(1)} %add.143.r_ref), channel_id=1, source_target_pairs={{0,1},{1,0},{2,3},{3,2},{4,5},{5,4},{6,7},{7,6},{8,9},{9,8},{10,11... | collective-permute-start | bytes 393224 | tf_op jit(solution)/shard_map/ppermute | solution.py:170
  (42 other events, 328.6 us)
